TPU v7x, 256 devices: a whole 4x4x8 slice. The times are simulated.
256 devices in a mesh: dp: 32 (over z, x), seq: 8 (over y, core).
Axes of the slice: x: 4, y: 4, z: 8, core: 2. Of those that a mesh axis runs over, the one named last changes fastest.
Arguments:
- residual_tiles: bfloat16 [32, 2048, 1024], P('dp', 'seq'), may hold values from -16 to 16
- picture_label_tile: int32 [32, 2048], P('dp', 'seq'), may hold values from 0 to 11, never falling along the last dimension, each value on 1 to 1024 neighbouring positions
- prenorm_multiplier: float32 [1024], replicated, may hold values from 0.5 to 1.5
- triple_projector: bfloat16 [1024, 3072], P('dp'), may hold values from -0.25 to 0.25
- logit_scaling: float32 [16], replicated, may hold values from 0.3 to 30
- final_projector: bfloat16 [1024, 1024], P('dp'), may hold values from -0.1875 to 0.1875
- binarizer_projector: bfloat16 [1024, 18], replicated, may hold values from -0.1875 to 0.1875
- binarizer_offset: float32 [18], replicated, may hold values from -1 to 1
Outputs:
- mixed: bfloat16 [32, 2048, 1024], P('dp', 'seq')
- bit_codes: float32 [32, 18, 2048], P('dp', None, 'seq')
- code_entropy: float32 [18], replicated
Inputs may be any that keep to these rules, and one draw needn't show every extreme that they name: `picture_label_tile`: in each pack image numbers never fall, every image number of 0 to 11 occurs, and an image has at most 1024 patches.
All inputs are finite; a program needn't handle non-finite values.
Results may differ from a plain program's by a relative error of at most 0.0053.
The roundings to bfloat16 on the way count: a program that leaves them out, or rounds other values in their place, can miss the bound.
Values may be sent and summed in bfloat16 or wider, within the bound.
No kernel may reach another device: no remote copies, remote signals or barrier semaphores. Data moves between devices by JAX's collectives and lax.ppermute only.
A program may use at most 64 MiB of HBM per device.

v0:
```python
import math

import jax
import jax.numpy as jnp
from jax import lax
from jax.sharding import Mesh
from jax.sharding import PartitionSpec as P

SEQ = ("seq_0", "seq_1")
DP = ("dp_0", "dp_1")
DP_SEQ = ("dp_0", "dp_1", "seq_0", "seq_1")


epsilon = 1e-06


def joined_along(pieces, dim):
    pieces = jnp.moveaxis(pieces, 0, dim)
    lengths = pieces.shape
    return pieces.reshape(*lengths[:dim], lengths[dim] * lengths[dim + 1], *lengths[dim + 2 :])


def copy_for_each(x, axis):
    length = lax.axis_size(axis)
    return lax.all_to_all(jnp.broadcast_to(x[None], (length, *x.shape)), axis, 0, 0, tiled=True)


def gather_directly(x, axis, dim):
    return joined_along(copy_for_each(x, axis), dim)


def whole_of(x, axes, dim):
    if not axes:
        return x
    nearer = lax.all_gather(x, axes[-1], axis=dim, tiled=True)
    return whole_of(nearer, axes[:-1], dim)


def by_axis(x, axes):
    for axis in axes:
        x = lax.psum(x, axis)
    return x


def rms_scale(values):
    return lax.rsqrt(jnp.mean(values * values, axis=-1, keepdims=True) + epsilon)


def split_subspaces(combined_subspaces, scales, channel_extent):
    token_count = combined_subspaces.shape[0]
    pieces = combined_subspaces.reshape(token_count, 3, scales.shape[0], channel_extent).astype(
        jnp.float32
    )
    asking_tensor = (
        pieces[:, 0] * rms_scale(pieces[:, 0]) * (scales[:, None] / math.sqrt(channel_extent))
    )
    rescaled_lookups = pieces[:, 1] * rms_scale(pieces[:, 1])
    return (
        asking_tensor.astype(jnp.bfloat16),
        rescaled_lookups.astype(jnp.bfloat16),
        pieces[:, 2].astype(jnp.bfloat16),
    )


def on_device(
    residual_tiles,
    picture_label_tile,
    prenorm_multiplier,
    triple_projector,
    logit_scaling,
    final_projector,
    binarizer_projector,
    binarizer_offset,
):
    pack_rows = residual_tiles[0]
    token_rows = pack_rows.shape[0]
    width = pack_rows.shape[1]
    subspace_total = logit_scaling.shape[0]
    channel_extent = width // subspace_total
    wide_pack = pack_rows.astype(jnp.float32)
    normed = (wide_pack * rms_scale(wide_pack) * prenorm_multiplier).astype(jnp.bfloat16)
    query_ids = picture_label_tile[0].astype(jnp.bfloat16)
    gathered, gathered_ids = (
        lax.all_gather(normed, SEQ, axis=0, tiled=True),
        lax.all_gather(query_ids, SEQ, axis=0, tiled=True),
    )
    seq_length = gathered.shape[0]
    group = lax.axis_size(SEQ)
    member = lax.axis_index(SEQ)
    local_heads = subspace_total // group
    shard_rows = triple_projector.shape[0]
    shaped = triple_projector.reshape(shard_rows, 3, subspace_total, channel_extent)
    owned = lax.dynamic_slice_in_dim(shaped, member * local_heads, local_heads, 2).reshape(
        shard_rows, 3 * local_heads * channel_extent
    )
    columns = gathered
    combined_subspaces = jnp.dot(
        columns, gather_directly(owned, DP, 0), preferred_element_type=jnp.float32
    ).astype(jnp.bfloat16)
    scales = lax.dynamic_slice_in_dim(logit_scaling, member * local_heads, local_heads, 0)
    asking_tensor, rescaled_lookups, surviving_contents = split_subspaces(
        combined_subspaces, scales, channel_extent
    )
    per_block = 1
    for candidate in range(1, group + 1):
        if group % candidate == 0 and candidate <= max(1, 512 // token_rows):
            per_block = candidate
    block_rows = token_rows * per_block
    query_blocks = asking_tensor.reshape(
        seq_length // block_rows, block_rows, local_heads, channel_extent
    )
    id_blocks = gathered_ids.reshape(seq_length // block_rows, block_rows)

    def attend_block(contraction_operands):
        query_block, id_block = contraction_operands
        same_image = id_block[:, None] == gathered_ids[None, :]
        scores = jnp.einsum(
            "qhd,khd->hqk", query_block, rescaled_lookups, preferred_element_type=jnp.float32
        )
        masked = jnp.where(same_image[None], scores, -1e30)
        highest = jnp.max(masked, axis=-1, keepdims=True)
        probs = jnp.where(same_image[None], jnp.exp(scores - highest), 0.0)
        summed = jnp.einsum(
            "hqk,khd->qhd",
            probs.astype(jnp.bfloat16),
            surviving_contents,
            preferred_element_type=jnp.float32,
        )
        return summed / jnp.swapaxes(jnp.sum(probs, axis=-1), 0, 1)[:, :, None]

    attended = lax.map(attend_block, (query_blocks, id_blocks))
    attended = attended.reshape(seq_length, local_heads * channel_extent).astype(jnp.bfloat16)
    attention = lax.all_to_all(attended, SEQ, split_axis=0, concat_axis=1, tiled=True)
    columns = attention
    projected = jnp.dot(
        columns, whole_of(final_projector, DP, 0), preferred_element_type=jnp.float32
    )
    mixed = (wide_pack + projected).astype(jnp.bfloat16)
    logits = (
        jnp.dot(mixed, binarizer_projector, preferred_element_type=jnp.float32) + binarizer_offset
    )
    bit_probs = jax.nn.sigmoid(4.0 * logits)
    patch_total = token_rows * lax.axis_size(SEQ) * lax.axis_size(DP)
    marginal = by_axis(jnp.sum(bit_probs, axis=0), DP_SEQ) / patch_total
    code_entropy = -(marginal * jnp.log(marginal) + (1.0 - marginal) * jnp.log(1.0 - marginal))
    bit_codes = jnp.swapaxes(bit_probs - marginal, 0, 1)[None]
    return (mixed[None], bit_codes, code_entropy)


def solution(mesh):
    finer = Mesh(mesh.devices.reshape(8, 4, 4, 2), ("dp_0", "dp_1", "seq_0", "seq_1"))
    placed = (P(DP, SEQ, None), P(DP, SEQ), P(), P(DP, None), P(), P(DP, None), P(), P())
    return jax.shard_map(
        on_device,
        mesh=finer,
        in_specs=placed,
        out_specs=(P(DP, SEQ, None), P(DP, None, SEQ), P()),
        check_vma=False,
    )
```

profile of v0, /device:TPU:1, one launch (start us, length us, event | category | flops | bytes accessed | tf_op | source)
XLA Modules:
  0.0 184.1 jit_solution(2955432564112788276)
XLA Ops:
  7.2 0.0 copy-start
  7.2 0.0 copy-start.5
  7.2 0.0 copy-start.6
  7.2 0.0 copy-start.8
  7.2 0.0 all-gather.4.cloned.1.call-start
  7.3 1.2 fusion.39
  8.5 2.0 %fusion.41 = bf16[256,1024]{1,0:T(8,128)(2,1)} fusion(bf16[1,256,1024]{2,1,0:T(8,128)(2,1)} %param.10, f32[1024]{0:T(1024)} %param.12, f32[256]{0:T(256)S(1)} %add_rsqrt_fusion.2), kind=kLoop, calls=%fused_computation.35 | loop fusion | flops 1048576 | bytes 1053696 | tf_op jit(solution)/shard_map/convert_element_type | solution.py:81
  10.5 0.0 all-gather.4.cloned.1.call-update
  10.6 1.2 reshape.103
  11.8 0.1 constant_dynamic-slice_fusion
  11.9 0.1 broadcast_in_dim.53
  12.0 1.0 broadcast_in_dim.54
  12.9 11.9 %all-to-all-start = ((bf16[32,32,384]{2,1,0:T(8,128)(2,1)}), bf16[32,32,384]{2,1,0:T(8,128)(2,1)S(1)}, u32[]{:S(2)}, u32[]{:S(2)}) async-start(bf16[32,32,384]{2,1,0:T(8,128)(2,1)} %broadcast_in_dim.54), calls=%async_computation | async-start | bytes 1572864 | tf_op jit(solution)/shard_map/all_to_all | solution.py:25
  24.8 0.0 all-gather.6.cloned.1.call-start
  24.9 0.0 copy-done.5
  24.9 12.8 %all_gather.14 = bf16[128,1024]{1,0:T(8,128)(2,1)} all-gather(bf16[32,1024]{1,0:T(8,128)(2,1)S(1)} %copy-done.5), channel_id=1, replica_groups=mesh['dp_0'=8,'dp_1'=4,'seq_0'=4,'seq_1'=2] {'dp_1'}, dimensions={0}, use_global_device_ids=true | all-gather | bytes 327680 | tf_op jit(solution)/shard_map/all_gather | solution.py:35
  37.7 0.0 all-gather.6.cloned.1.call-update
  37.8 14.2 %all-gather = bf16[1,2048]{1,0:T(2,128)(2,1)S(1)} all-gather(bf16[1,256]{1,0:T(2,128)(2,1)S(1)} %convert_element_type.50), channel_id=2, replica_groups=mesh['dp_0'=8,'dp_1'=4,'seq_0'=4,'seq_1'=2] {'seq_0','seq_1'}, dimensions={1}, use_global_device_ids=true | all-gather | bytes 4608 | tf_op jit(solution)/shard_map/all_gather | solution.py:85
  52.0 0.1 dynamic-slice_multiply_fusion
  52.1 0.0 all-to-all-done
  52.1 4.0 %convolution_convert_fusion = bf16[2048,384]{0,1:T(8,128)(2,1)S(1)} fusion(bf16[2048,1024]{1,0:T(8,128)(2,1)} %all-gather.4.cloned.1.call-done, bf16[1024,384]{1,0:T(8,128)(2,1)S(1)} %bitcast.71), kind=kOutput, calls=%fused_computation.22 | convolution fusion | flops 1611399168 | bytes 6553600 | tf_op jit(solution)/shard_map/dot_general | solution.py:97
  56.2 0.4 convert_element_type.55
  56.5 0.1 slice.15
  56.6 0.1 multiply_reduce_fusion.1
  56.8 1.4 copy-done.2
  58.2 0.1 multiply_reduce_fusion
  58.4 0.7 squeeze.9
  59.1 1.3 multiply_convert_fusion
  60.5 0.3 fusion.43
  60.8 58.7 %while.10 = (s32[]{:T(128)}, bf16[4,512,2,64]{1,3,2,0:T(8,128)(2,1)}, bf16[4,512]{1,0:T(4,128)(2,1)S(1)}, bf16[2048]{0:T(1024)(128)(2,1)S(1)}, bf16[4,512,2,64]{...) while((s32[]{:T(128)}, ...), condition=%wide.region_6.7_spmd, body=%wide.region_3.6_spmd.sunk | while | flops 554767360 | bytes 72760952 | solution.py:131
  60.8 1.3 fusion.69
  62.1 0.6 broadcast_compare_fusion.2
  62.8 3.1 %fusion.70 = f32[2,512]{1,0:T(2,128)S(1)} fusion(f32[2,512,2048]{2,1,0:T(8,128)S(1)} %fusion.69, pred[512,2048]{1,0:T(8,128)(4,1)S(1)} %broadcast_compare_fusion.2), kind=kOutput, calls=%fused_computation.55.clone.1 | output fusion | flops 8390655 | bytes 9441280 | tf_op jit(solution)/shard_map/while/body/eval_jaxpr/sub | solution.py:122
  65.9 9.6 %fusion.71 = bf16[4,512,2,64]{1,3,2,0:T(8,128)(2,1)} fusion(bf16[4,512,2,64]{1,3,2,0:T(8,128)(2,1)} %get-tuple-element.120, s32[]{:T(128)} %get-tuple-element.119, bf16[2048,2,64]{0,2,1:T(8,128)(2,1)S(1)} %get-tuple-element.133, f32[512,2]{0,1:T(2,128)S(1)} %bitcast.73, f32[2,512,2048]{2,1,0:T(8,128)} %copy-done.1, ...), kind=kOutput, calls=%fused_computation.11.clone.1 | convolution fusion | flops 276892672 | bytes 19665408 | tf_op jit(solution)/shard_map/while/body/eval_jaxpr/hqk,khd->qhd/dot_general | solution.py:123
  75.5 1.3 fusion.69
  76.9 0.6 broadcast_compare_fusion.2
  77.5 3.1 %fusion.70 = f32[2,512]{1,0:T(2,128)S(1)} fusion(f32[2,512,2048]{2,1,0:T(8,128)S(1)} %fusion.69, pred[512,2048]{1,0:T(8,128)(4,1)S(1)} %broadcast_compare_fusion.2), kind=kOutput, calls=%fused_computation.55.clone.1 | output fusion | flops 8390655 | bytes 9441280 | tf_op jit(solution)/shard_map/while/body/eval_jaxpr/sub | solution.py:122
  80.6 9.7 %fusion.71 = bf16[4,512,2,64]{1,3,2,0:T(8,128)(2,1)} fusion(bf16[4,512,2,64]{1,3,2,0:T(8,128)(2,1)} %get-tuple-element.120, s32[]{:T(128)} %get-tuple-element.119, bf16[2048,2,64]{0,2,1:T(8,128)(2,1)S(1)} %get-tuple-element.133, f32[512,2]{0,1:T(2,128)S(1)} %bitcast.73, f32[2,512,2048]{2,1,0:T(8,128)} %copy-done.1, ...), kind=kOutput, calls=%fused_computation.11.clone.1 | convolution fusion | flops 276892672 | bytes 19665408 | tf_op jit(solution)/shard_map/while/body/eval_jaxpr/hqk,khd->qhd/dot_general | solution.py:123
  90.3 1.3 fusion.69
  91.6 0.6 broadcast_compare_fusion.2
  92.2 3.1 %fusion.70 = f32[2,512]{1,0:T(2,128)S(1)} fusion(f32[2,512,2048]{2,1,0:T(8,128)S(1)} %fusion.69, pred[512,2048]{1,0:T(8,128)(4,1)S(1)} %broadcast_compare_fusion.2), kind=kOutput, calls=%fused_computation.55.clone.1 | output fusion | flops 8390655 | bytes 9441280 | tf_op jit(solution)/shard_map/while/body/eval_jaxpr/sub | solution.py:122
  95.4 9.5 %fusion.71 = bf16[4,512,2,64]{1,3,2,0:T(8,128)(2,1)} fusion(bf16[4,512,2,64]{1,3,2,0:T(8,128)(2,1)} %get-tuple-element.120, s32[]{:T(128)} %get-tuple-element.119, bf16[2048,2,64]{0,2,1:T(8,128)(2,1)S(1)} %get-tuple-element.133, f32[512,2]{0,1:T(2,128)S(1)} %bitcast.73, f32[2,512,2048]{2,1,0:T(8,128)} %copy-done.1, ...), kind=kOutput, calls=%fused_computation.11.clone.1 | convolution fusion | flops 276892672 | bytes 19665408 | tf_op jit(solution)/shard_map/while/body/eval_jaxpr/hqk,khd->qhd/dot_general | solution.py:123
  104.9 1.3 fusion.69
  106.2 0.6 broadcast_compare_fusion.2
  106.9 3.1 %fusion.70 = f32[2,512]{1,0:T(2,128)S(1)} fusion(f32[2,512,2048]{2,1,0:T(8,128)S(1)} %fusion.69, pred[512,2048]{1,0:T(8,128)(4,1)S(1)} %broadcast_compare_fusion.2), kind=kOutput, calls=%fused_computation.55.clone.1 | output fusion | flops 8390655 | bytes 9441280 | tf_op jit(solution)/shard_map/while/body/eval_jaxpr/sub | solution.py:122
  110.0 9.5 %fusion.71 = bf16[4,512,2,64]{1,3,2,0:T(8,128)(2,1)} fusion(bf16[4,512,2,64]{1,3,2,0:T(8,128)(2,1)} %get-tuple-element.120, s32[]{:T(128)} %get-tuple-element.119, bf16[2048,2,64]{0,2,1:T(8,128)(2,1)S(1)} %get-tuple-element.133, f32[512,2]{0,1:T(2,128)S(1)} %bitcast.73, f32[2,512,2048]{2,1,0:T(8,128)} %copy-done.1, ...), kind=kOutput, calls=%fused_computation.11.clone.1 | convolution fusion | flops 276892672 | bytes 19665408 | tf_op jit(solution)/shard_map/while/body/eval_jaxpr/hqk,khd->qhd/dot_general | solution.py:123
  119.5 1.5 copy.21
  121.0 0.1 convert_element_type.60
  121.1 0.9 copy.22
  122.0 3.5 %all-to-all-start.1 = ((bf16[8,256,128]{1,2,0:T(8,128)(2,1)}), bf16[8,256,128]{1,2,0:T(8,128)(2,1)S(1)}, u32[]{:S(2)}, u32[]{:S(2)}) async-start(bf16[8,256,128]{1,2,0:T(8,128)(2,1)} %copy.22), calls=%async_computation.1 | async-start | bytes 1048576 | tf_op jit(solution)/shard_map/all_to_all | solution.py:133
  125.6 9.5 %all-to-all-done.1 = bf16[8,256,128]{1,2,0:T(8,128)(2,1)S(1)} async-done(((bf16[8,256,128]{1,2,0:T(8,128)(2,1)}), bf16[8,256,128]{1,2,0:T(8,128)(2,1)S(1)}, u32[]{:S(2)}, u32[]{:S(2)}) %all-to-all-start.1) | async-done | bytes 524320 | tf_op jit(solution)/shard_map/all_to_all | solution.py:133
  135.1 2.3 %fusion.33 = bf16[256,1024]{1,0:T(8,128)(2,1)S(1)} fusion(bf16[256,1024]{0,1:T(8,128)(2,1)S(1)} %bitcast.70, bf16[1024,1024]{1,0:T(8,128)(2,1)} %all-gather.6.cloned.1.call-done, bf16[1,256,1024]{2,1,0:T(8,128)(2,1)S(1)} %copy-done.3), kind=kOutput, calls=%fused_computation.26 | convolution fusion | flops 537657344 | bytes 3670016 | tf_op jit(solution)/shard_map/dot_general | solution.py:135
  137.4 0.0 copy-done
  137.4 0.0 copy-done.7
  137.4 0.0 copy-start.4
  137.4 0.4 fusion.47
  137.8 11.9 %psum.28 = f32[18]{0:T(128)S(1)} all-reduce(f32[18]{0:T(128)S(1)} %get-tuple-element.66), channel_id=1, replica_groups=mesh['dp_0'=8,'dp_1'=4,'seq_0'=4,'seq_1'=2] {'dp_0'}, use_global_device_ids=true, to_apply=%region_8.9 | all-reduce | flops 18 | bytes 144 | tf_op jit(solution)/shard_map/psum | solution.py:41
  149.7 8.7 %psum.29 = f32[18]{0:T(128)S(1)} all-reduce(f32[18]{0:T(128)S(1)} %psum.28), channel_id=1, replica_groups=mesh['dp_0'=8,'dp_1'=4,'seq_0'=4,'seq_1'=2] {'dp_1'}, use_global_device_ids=true, to_apply=%region_9.10 | all-reduce | flops 18 | bytes 144 | tf_op jit(solution)/shard_map/psum | solution.py:41
  158.4 6.9 %psum.30 = f32[18]{0:T(128)S(1)} all-reduce(f32[18]{0:T(128)S(1)} %psum.29), channel_id=1, replica_groups=mesh['dp_0'=8,'dp_1'=4,'seq_0'=4,'seq_1'=2] {'seq_0'}, use_global_device_ids=true, to_apply=%region_10.11 | all-reduce | flops 18 | bytes 144 | tf_op jit(solution)/shard_map/psum | solution.py:41
  165.2 10.8 %psum.31 = f32[18]{0:T(128)S(1)} all-reduce(f32[18]{0:T(128)S(1)} %psum.30), channel_id=1, replica_groups=mesh['dp_0'=8,'dp_1'=4,'seq_0'=4,'seq_1'=2] {'seq_1'}, use_global_device_ids=true, to_apply=%region_11.12 | all-reduce | flops 18 | bytes 144 | tf_op jit(solution)/shard_map/psum | solution.py:41
  176.0 0.5 fusion.45
  176.5 0.1 subtract_bitcast_fusion
  176.6 0.6 copy.23
  177.2 0.0 copy-done.4
  (28 shorter events, 0.3 us)
Async XLA Ops:
  7.2 130.2 %copy-start = (bf16[1024,18]{0,1:T(8,128)(2,1)S(1)}, bf16[1024,18]{0,1:T(8,128)(2,1)}, u32[]{:S(2)}) copy-start(bf16[1024,18]{0,1:T(8,128)(2,1)} %param.16) | copy-start | bytes 110596
  7.2 17.7 %copy-start.5 = (bf16[32,1024]{1,0:T(8,128)(2,1)S(1)}, bf16[32,1024]{1,0:T(8,128)(2,1)}, u32[]{:S(2)}) copy-start(bf16[32,1024]{1,0:T(8,128)(2,1)} %param.15) | copy-start | bytes 196612
  7.2 30.6 %copy-start.6 = (s32[1,256]{1,0:T(1,128)S(1)}, s32[1,256]{1,0:T(1,128)}, u32[]{:S(2)}) copy-start(s32[1,256]{1,0:T(1,128)} %param.11) | copy-start | bytes 3076
  7.2 44.8 %copy-start.8 = (f32[16]{0:T(128)S(1)}, f32[16]{0:T(128)}, u32[]{:S(2)}) copy-start(f32[16]{0:T(128)} %param.14) | copy-start | bytes 196
  7.2 44.9 %all-gather.4.cloned.1.call-start = ((), (), s32[]{:S(2)}) async-start(), calls=%async_computation.2 | async-start | bytes 4718592 | tf_op jit(solution)/shard_map/all_gather | solution.py:84
  12.9 39.2 %all-to-all-start = ((bf16[32,32,384]{2,1,0:T(8,128)(2,1)}), bf16[32,32,384]{2,1,0:T(8,128)(2,1)S(1)}, u32[]{:S(2)}, u32[]{:S(2)}) async-start(bf16[32,32,384]{2,1,0:T(8,128)(2,1)} %broadcast_in_dim.54), calls=%async_computation | async-start | bytes 1572864 | tf_op jit(solution)/shard_map/all_to_all | solution.py:25
  24.8 100.8 %all-gather.6.cloned.1.call-start = ((), (), s32[]{:S(2)}) async-start(), calls=%async_computation.3 | async-start | bytes 2359296 | tf_op jit(solution)/shard_map/all_gather | solution.py:35
  56.5 1.7 copy-start.2
  62.1 3.8 %copy-start.1 = (f32[2,512,2048]{2,1,0:T(8,128)}, f32[2,512,2048]{2,1,0:T(8,128)S(1)}, u32[]{:S(2)}) copy-start(f32[2,512,2048]{2,1,0:T(8,128)S(1)} %fusion.69) | copy-start | bytes 25165828 | tf_op jit(solution)/shard_map/while
  76.8 3.8 %copy-start.1 = (f32[2,512,2048]{2,1,0:T(8,128)}, f32[2,512,2048]{2,1,0:T(8,128)S(1)}, u32[]{:S(2)}) copy-start(f32[2,512,2048]{2,1,0:T(8,128)S(1)} %fusion.69) | copy-start | bytes 25165828 | tf_op jit(solution)/shard_map/while
  91.6 3.8 %copy-start.1 = (f32[2,512,2048]{2,1,0:T(8,128)}, f32[2,512,2048]{2,1,0:T(8,128)S(1)}, u32[]{:S(2)}) copy-start(f32[2,512,2048]{2,1,0:T(8,128)S(1)} %fusion.69) | copy-start | bytes 25165828 | tf_op jit(solution)/shard_map/while
  106.2 3.8 %copy-start.1 = (f32[2,512,2048]{2,1,0:T(8,128)}, f32[2,512,2048]{2,1,0:T(8,128)S(1)}, u32[]{:S(2)}) copy-start(f32[2,512,2048]{2,1,0:T(8,128)S(1)} %fusion.69) | copy-start | bytes 25165828 | tf_op jit(solution)/shard_map/while
  119.5 15.6 %copy-start.3 = (bf16[1,256,1024]{2,1,0:T(8,128)(2,1)S(1)}, bf16[1,256,1024]{2,1,0:T(8,128)(2,1)}, u32[]{:S(2)}) copy-start(bf16[1,256,1024]{2,1,0:T(8,128)(2,1)} %param.10) | copy-start | bytes 1572868
  119.5 17.9 %copy-start.7 = (f32[18]{0:T(128)S(1)}, f32[18]{0:T(128)}, u32[]{:S(2)}) copy-start(f32[18]{0:T(128)} %param.17) | copy-start | bytes 220
  122.0 13.0 %all-to-all-start.1 = ((bf16[8,256,128]{1,2,0:T(8,128)(2,1)}), bf16[8,256,128]{1,2,0:T(8,128)(2,1)S(1)}, u32[]{:S(2)}, u32[]{:S(2)}) async-start(bf16[8,256,128]{1,2,0:T(8,128)(2,1)} %copy.22), calls=%async_computation.1 | async-start | bytes 1048576 | tf_op jit(solution)/shard_map/all_to_all | solution.py:133
  137.4 39.8 %copy-start.4 = (bf16[256,1024]{1,0:T(8,128)(2,1)}, bf16[256,1024]{1,0:T(8,128)(2,1)S(1)}, u32[]{:S(2)}) copy-start(bf16[256,1024]{1,0:T(8,128)(2,1)S(1)} %fusion.33) | copy-start | bytes 1572868
Sparse Core Ops, SparseCore 0:
  10.7 38.9 all-gather.3
  51.4 36.9 all-gather.5
where the time goes:
time: 185 us; the launch traced here: 184 us
  blocking collectives  65.3 us (35%)
  matrix products  50.2 us (27%)
  other arithmetic  21.2 us (11%)
  starting transfers between devices  15.5 us (8%)
  between operations  14.3 us (8%)
  waiting for transfers between devices  9.54 us (5%)
  local copies, waits for them, and re-layouts  7.97 us (4%)
    dot_general x4, matrix products, attend_block(): jnp.einsum('hqk,khd->qhd', probs.astype(jnp.bfloat16), surviving_contents...  38.3 us
    psum x4, blocking collectives, by_axis(): x = lax.psum(x, axis)  38.2 us
    all_gather x1, blocking collectives, on_device(): lax.all_gather(query_ids, SEQ, axis=0, tiled=True)  14.2 us
    all_gather x1, blocking collectives, whole_of(): nearer = lax.all_gather(x, axes[-1], axis=dim, tiled=True)  12.8 us
    sub x4, other arithmetic, attend_block(): probs = jnp.where(same_image[None], jnp.exp(scores - highest), 0.0)  12.5 us
    all_to_all x1, starting transfers between devices, copy_for_each(): lax.all_to_all(jnp.broadcast_to(x[None], (length, *x.shape)), axis, 0, 0,...  11.9 us
    all_to_all x1, waiting for transfers between devices, on_device(): lax.all_to_all(attended, SEQ, split_axis=0, concat_axis=1, tiled=True)  9.5 us
    dot_general x4, matrix products, attend_block(): jnp.einsum('qhd,khd->hqk', query_block, rescaled_lookups, preferred_eleme...  5.19 us
  transfers between devices with their start and end apart: 4, of which 1 were waited for; matrix products, arithmetic and copies ran while one was open for 38% of the time, Pallas kernels for 0%

commit v1 on v0

v1 whole, which is shorter than its diff:
```python
import functools
import math

import jax
import jax.numpy as jnp
from jax import lax
from jax.experimental import pallas as pl
from jax.experimental.pallas import tpu as pltpu
from jax.sharding import Mesh
from jax.sharding import PartitionSpec as P

SEQ = ("seq_0", "seq_1")
DP = ("dp_0", "dp_1")
ALL = ("dp_0", "dp_1", "seq_0", "seq_1")

EPS = 1e-06
EXCLUDED = -32768.0
KEYS = 512
ROWS = 256
SAFE = 8.0
LIMIT = 60 * 1024 * 1024
F32 = jnp.float32
BF16 = jnp.bfloat16


def params():
    return pltpu.CompilerParams(vmem_limit_bytes=LIMIT)


def vmem():
    return pl.BlockSpec(memory_space=pltpu.VMEM)


def smem():
    return pl.BlockSpec(memory_space=pltpu.SMEM)


def copy_for_each(x, axis):
    length = lax.axis_size(axis)
    return lax.all_to_all(jnp.broadcast_to(x[None], (length, *x.shape)), axis, 0, 0, tiled=True)


def any_space():
    return pl.BlockSpec(memory_space=pl.ANY)


def layer_kernel(at, scale, gain, *refs):
    pieces, shards, out = refs[:8], refs[8], refs[9]
    held, weights, normed, labels, queries, keys, values, total, even, odd, table, sems = refs[10:]
    core, chip = at[0], at[1]
    rows = ROWS
    arrivals = [
        pltpu.make_async_copy(pieces[i], held.at[i // 2, i % 2], sems.at[i]) for i in range(8)
    ]
    for i in range(4):
        copy = pltpu.make_async_copy(shards.at[i], weights.at[:, i], sems.at[8 + i])
        copy.start()
        arrivals.append(copy)
    for copy in arrivals[:8]:
        copy.start()
    for copy in arrivals[8:]:
        copy.wait()
    width, head = held.shape[3], 64
    matrix = weights[...].reshape(width, 384)
    lane = lax.broadcasted_iota(jnp.int32, (rows, 128), 1)
    spot = lax.broadcasted_iota(jnp.int32, (head, rows), 0)
    for pair in range(4):
        step = (0, 1, 3, 2)[pair]
        for side in range(2):
            arrivals[2 * pair + side].wait()
            wide = held[pair, side, 0:rows].astype(F32)
            inv = lax.rsqrt(jnp.mean(wide * wide, axis=-1, keepdims=True) + EPS)
            normed[side * rows : (side + 1) * rows] = (wide * inv * gain[...]).astype(BF16)
        both = jnp.dot(normed[...], matrix, preferred_element_type=F32).astype(BF16).astype(F32)
        for side in range(2):
            part = core if side == 0 else 1 - core
            block = 2 * lax.rem(chip + step, 4) + part
            start = pl.multiple_of(block * rows, rows)
            joined = both[side * rows : (side + 1) * rows]
            ids = held[pair, side, rows : rows + 8, 0:rows].astype(F32)[0:1].astype(jnp.int32)
            labels[pl.ds(block, 1), :] = ids
            same = spot == ids
            bars = jnp.where(same, 0.0, EXCLUDED).astype(F32)
            query = joined[:, 0:128].T
            key = joined[:, 128:256].T
            marks = jnp.where(same, 1.0, 0.0).astype(BF16)
            for h in range(2):
                one = query[h * head : (h + 1) * head]
                inv = lax.rsqrt(jnp.mean(one * one, axis=0, keepdims=True) + EPS)
                queries[h, pl.ds(start, rows), :] = (
                    jnp.concatenate([one * inv * scale[h], bars], axis=0).T.astype(BF16)
                )
                one = key[h * head : (h + 1) * head]
                inv = lax.rsqrt(jnp.mean(one * one, axis=0, keepdims=True) + EPS)
                keys[h, 0:head, pl.ds(start, rows)] = (one * inv).astype(BF16)
                keys[h, head : 2 * head, pl.ds(start, rows)] = marks
            value = joined[:, 256:384]
            values[0, pl.ds(start, rows), :] = jnp.where(lane < head, value, 1.0).astype(BF16)
            values[1, pl.ds(start, rows), :] = jnp.where(
                lane < head, pltpu.roll(value, head, 1), 1.0
            ).astype(BF16)

    every = labels[...]
    first, last = every[:, 0:1], every[:, rows - 1 : rows]
    below = jnp.zeros((8, rows), jnp.int32)
    upto = jnp.zeros((8, rows), jnp.int32)
    for b in range(8):
        below += (every[b : b + 1] < first).astype(jnp.int32)
        upto += (every[b : b + 1] <= last).astype(jnp.int32)
    low = jnp.sum(below, axis=1, keepdims=True)
    high = jnp.sum(upto, axis=1, keepdims=True)
    low = low & -128
    counts = lax.shift_right_logical(high - low + (KEYS - 1), 9)
    low = jnp.minimum(low, 2048 - counts * KEYS)
    lows = [low[b, 0] for b in range(8)]
    counts = [counts[b, 0] for b in range(8)]
    total[...] = jnp.zeros(total.shape, F32)

    pairs = jnp.int32(0)
    for b in range(8):

        def note(s, pairs, b=b):
            table[0, pairs] = jnp.int32(b * rows)
            table[1, pairs] = lows[b] + s * KEYS
            return pairs + 1

        pairs = lax.fori_loop(0, counts[b], note, pairs)
    for spare in range(2):
        table[0, pairs + spare] = jnp.int32(8 * rows)
        table[1, pairs + spare] = jnp.int32(0)

    def score(j, into):
        row = pl.multiple_of(table[0, j], rows)
        key = pl.multiple_of(table[1, j], 128)
        for h in range(2):
            into[h] = jnp.dot(
                queries[h, pl.ds(row, rows), :],
                keys[h, :, pl.ds(key, KEYS)],
                preferred_element_type=F32,
            )

    def absorb(j, source):
        row = pl.multiple_of(table[0, j], rows)
        key = pl.multiple_of(table[1, j], 128)
        for h in range(2):
            total[h, pl.ds(row, rows), :] += jnp.dot(
                jnp.exp(source[h]).astype(BF16),
                values[h, pl.ds(key, KEYS), :],
                preferred_element_type=F32,
            )

    small = jnp.maximum(scale[0], scale[1]) * 8.0 <= SAFE

    @pl.when(small)
    def _():
        score(0, even)

        def twice(j, carry):
            score(2 * j + 1, odd)
            absorb(2 * j, even)
            score(2 * j + 2, even)
            absorb(2 * j + 1, odd)
            return carry

        lax.fori_loop(0, (pairs + 1) // 2, twice, 0)

    @pl.when(jnp.logical_not(small))
    def _():
        for b in range(8):
            own = pl.ds(b * rows, rows)
            for h in range(2):

                def scores(j, b=b, h=h, own=own):
                    key = pl.multiple_of(lows[b] + j * KEYS, 128)
                    return key, jnp.dot(
                        queries[h, own, :], keys[h, :, pl.ds(key, KEYS)], preferred_element_type=F32
                    )

                def top(j, most, scores=scores):
                    return jnp.maximum(most, jnp.max(scores(j)[1], axis=-1, keepdims=True))

                largest = lax.fori_loop(
                    0, counts[b], top, jnp.full((rows, 1), 2.0 * EXCLUDED, F32)
                )

                def gather(j, carry, h=h, own=own, scores=scores, largest=largest):
                    key, found = scores(j)
                    total[h, own, :] += jnp.dot(
                        jnp.exp(found - largest).astype(BF16),
                        values[h, pl.ds(key, KEYS), :],
                        preferred_element_type=F32,
                    )
                    return carry

                lax.fori_loop(0, counts[b], gather, 0)

    for b in range(8):
        own = slice(b * rows, (b + 1) * rows)
        left, right = total[0, own, :], total[1, own, :]
        over = jnp.where(lane < head, left, pltpu.roll(right, head, 1))
        under = jnp.where(lane < head, pltpu.roll(left, head, 1), right)
        out[b] = (over / under).astype(BF16)


def layer(at, scale, gain, pieces, shard):
    total = 8 * ROWS
    return pl.pallas_call(
        layer_kernel,
        in_specs=[smem(), smem(), vmem()] + [any_space()] * 9,
        out_specs=vmem(),
        out_shape=jax.ShapeDtypeStruct((8, ROWS, 128), BF16),
        scratch_shapes=[
            pltpu.VMEM((4, 2, *pieces[0].shape), BF16),
            pltpu.VMEM((8, 4, 32, 384), BF16),
            pltpu.VMEM((2 * ROWS, pieces[0].shape[1]), BF16),
            pltpu.VMEM((8, ROWS), jnp.int32),
            pltpu.VMEM((2, total + ROWS, 128), BF16),
            pltpu.VMEM((2, 128, total), BF16),
            pltpu.VMEM((2, total, 128), BF16),
            pltpu.VMEM((2, total + ROWS, 128), F32),
            pltpu.VMEM((2, ROWS, KEYS), F32),
            pltpu.VMEM((2, ROWS, KEYS), F32),
            pltpu.SMEM((2, 48), jnp.int32),
            pltpu.SemaphoreType.DMA((12,)),
        ],
        compiler_params=params(),
        name="layer",
    )(at, scale, gain, *pieces, shard)


def finish_kernel(at, pieces, *refs):
    shards, (rows, bits, offset, mixed, probs, sums, weights, joined, sems) = refs[:8], refs[8:]
    copies = []
    for i in range(8):
        part = at[0] if i < 4 else 1 - at[0]
        place = lax.rem(at[2] + (0, 2, 1, 3)[i % 4], 4)
        copies.append(pltpu.make_async_copy(shards[i], weights.at[part, :, place], sems.at[i]))
        copies[i].start()
    for source in range(8):
        joined[:, source * 128 : (source + 1) * 128] = pieces[source]
    for copy in copies:
        copy.wait()
    for part in range(2):
        columns = slice(part * 512, part * 512 + 512)
        moved = jnp.dot(
            joined[...], weights[part].reshape(1024, 512), preferred_element_type=F32
        )
        mixed[:, columns] = (rows[:, columns].astype(F32) + moved).astype(BF16)
    logits = lax.dot_general(
        bits[...], mixed[...], (((1,), (1,)), ((), ())), preferred_element_type=F32
    )
    chance = jax.nn.sigmoid(4.0 * (logits + offset[...]))
    probs[...] = chance
    row = lax.dot_general(
        jnp.ones((8, chance.shape[1]), F32),
        chance,
        (((1,), (1,)), ((), ())),
        preferred_element_type=F32,
        precision=lax.Precision.HIGHEST,
    )
    sums[...] = row[0:1]


def finish(at, pieces, shards, rows, bits, offset):
    count = rows.shape[0]
    return pl.pallas_call(
        finish_kernel,
        in_specs=[smem(), vmem()] + [any_space()] * 8 + [vmem()] * 3,
        out_specs=[vmem()] * 3,
        out_shape=[
            jax.ShapeDtypeStruct(rows.shape, BF16),
            jax.ShapeDtypeStruct((bits.shape[0], count), F32),
            jax.ShapeDtypeStruct((1, bits.shape[0]), F32),
        ],
        scratch_shapes=[
            pltpu.VMEM((2, 8, 4, 32, 512), BF16),
            pltpu.VMEM((count, 1024), BF16),
            pltpu.SemaphoreType.DMA((8,)),
        ],
        compiler_params=params(),
        name="finish",
    )(at, pieces, *shards, rows, bits, offset)


def on_device(
    residual_tiles,
    picture_label_tile,
    prenorm_multiplier,
    triple_projector,
    logit_scaling,
    final_projector,
    binarizer_projector,
    binarizer_offset,
):
    rows = residual_tiles[0]
    count, width = rows.shape
    core = lax.axis_index("seq_1")
    member = lax.axis_index(SEQ)
    at = jnp.stack([core, lax.axis_index("seq_0"), lax.axis_index("dp_1")]).astype(jnp.int32)

    def from_step(x, k, axis="seq_0"):
        length = lax.axis_size(axis)
        return lax.ppermute(x, axis, [(i, (i - k) % length) for i in range(length)])

    def from_other_core(x):
        return lax.ppermute(x, "seq_1", [(0, 1), (1, 0)])

    marked = jnp.pad(picture_label_tile.astype(BF16), ((0, 15), (0, width - count)))
    load = jnp.concatenate([rows, marked], axis=0)
    near = [load] + [from_step(load, k) for k in (1, 3, 2)]
    pieces = [x for own in near for x in (own, from_other_core(own))]

    owned = jnp.concatenate(
        [
            lax.dynamic_slice_in_dim(triple_projector, member * 128 + 1024 * i, 128, 1)
            for i in range(3)
        ]
        + [lax.dynamic_slice_in_dim(final_projector, core * 512, 512, 1)],
        axis=1,
    )
    owned = copy_for_each(owned, "dp_0")
    shard, mixing = owned[:, :, :384], owned[:, :, 384:]
    shard = copy_for_each(shard, "dp_1")
    mixing, _ = lax.optimization_barrier((mixing, shard))
    mixings = [mixing] + [from_step(mixing, k, "dp_1") for k in (2, 1, 3)]

    scale = lax.dynamic_slice_in_dim(logit_scaling, member * 2, 2, 0) / math.sqrt(64)
    attended = layer(at, scale, prenorm_multiplier[None], pieces, shard)
    mixings, attended = lax.optimization_barrier((mixings, attended))
    mixings = mixings + [from_other_core(m) for m in mixings]
    attended = lax.all_to_all(attended, SEQ, 0, 0, tiled=True)
    mixed, probs, sums = finish(
        at,
        attended,
        mixings,
        rows,
        binarizer_projector.T,
        binarizer_offset[:, None],
    )
    sums = sums + from_other_core(sums)
    sums = copy_for_each(sums, ("dp_0", "dp_1", "seq_0"))
    marginal = jnp.sum(sums, axis=(0, 1)) / (count * lax.axis_size(ALL))
    code_entropy = -(marginal * jnp.log(marginal) + (1.0 - marginal) * jnp.log(1.0 - marginal))
    bit_codes = (probs - marginal[:, None])[None]
    return (mixed[None], bit_codes, code_entropy)


def solution(mesh):
    finer = Mesh(mesh.devices.reshape(8, 4, 4, 2), ("dp_0", "dp_1", "seq_0", "seq_1"))
    placed = (P(DP, SEQ, None), P(DP, SEQ), P(), P(DP, None), P(), P(DP, None), P(), P())
    return jax.shard_map(
        on_device,
        mesh=finer,
        in_specs=placed,
        out_specs=(P(DP, SEQ, None), P(DP, None, SEQ), P()),
        check_vma=False,
    )
```

time: 185 us -> 128 us (0.69)
  matrix products: 50.2 us -> 0 us
  blocking collectives: 65.3 us -> 25.4 us
  Pallas kernels: 0 us -> 30.6 us
  starting transfers between devices: 15.5 us -> 38.8 us
  other arithmetic: 21.2 us -> 3.33 us
  between operations: 14.3 us -> 0.87 us
  waiting for transfers between devices: 9.54 us -> 22.4 us
  local copies, waits for them, and re-layouts: 7.97 us -> 5.52 us
    dot_general x11 -> x0, matrix products: 50.2 us -> none  [the longest x4 38.3 us: attend_block(): jnp.einsum('hqk,khd->qhd', probs.astype(jnp.bfloat16), surviving_contents...]
    psum x4 -> x0, blocking collectives: 38.2 us -> none  [by_axis(): x = lax.psum(x, axis)]
    pallas_call x0 -> x2, Pallas kernels: none -> 30.6 us  [the longest x1 26.2 us: layer(): pl.pallas_call(layer_kernel, in_specs=[smem(), smem(), vmem()] + [any_spa...]
    all_gather x2 -> x0, blocking collectives: 27.1 us -> none  [the longest x1 14.2 us: on_device(): lax.all_gather(query_ids, SEQ, axis=0, tiled=True)]
    all_to_all x0 -> x1, blocking collectives: none -> 25.4 us  [copy_for_each(): lax.all_to_all(jnp.broadcast_to(x[None], (length, *x.shape)), axis, 0, 0,...]
    ppermute x0 -> x15, starting transfers between devices: none -> 18.7 us  [the longest x9 11.6 us: from_other_core(): return lax.ppermute(x, 'seq_1', [(0, 1), (1, 0)])]
    all_to_all x1 -> x2, waiting for transfers between devices: 0.01 us -> 13.7 us  [copy_for_each(): lax.all_to_all(jnp.broadcast_to(x[None], (length, *x.shape)), axis, 0, 0,...]
    sub x4 -> x0, other arithmetic: 12.5 us -> none  [attend_block(): probs = jnp.where(same_image[None], jnp.exp(scores - highest), 0.0)]
  transfers between devices with their start and end apart: 4 -> 18, of which waited for: 1 -> 7; matrix products, arithmetic and copies ran while one was open for 38% -> 2% of each run, Pallas kernels for 0% -> 21%
where the time goes in v1:
time: 128 us; the launch traced here: 127 us
  starting transfers between devices  38.8 us (30%)
  Pallas kernels  30.6 us (24%)
  blocking collectives  25.4 us (20%)
  waiting for transfers between devices  22.4 us (18%)
  local copies, waits for them, and re-layouts  5.52 us (4%)
  other arithmetic  3.33 us (3%)
    pallas_call x1, Pallas kernels, layer(): pl.pallas_call(layer_kernel, in_specs=[smem(), smem(), vmem()] + [any_spa...  26.2 us
    all_to_all x1, blocking collectives, copy_for_each(): lax.all_to_all(jnp.broadcast_to(x[None], (length, *x.shape)), axis, 0, 0,...  25.4 us
    all_to_all x2, waiting for transfers between devices, copy_for_each(): lax.all_to_all(jnp.broadcast_to(x[None], (length, *x.shape)), axis, 0, 0,...  13.7 us
    all_to_all x2, starting transfers between devices, copy_for_each(): lax.all_to_all(jnp.broadcast_to(x[None], (length, *x.shape)), axis, 0, 0,...  13.2 us
    ppermute x9, starting transfers between devices, from_other_core(): return lax.ppermute(x, 'seq_1', [(0, 1), (1, 0)])  11.6 us
    ppermute x6, starting transfers between devices, from_step(): return lax.ppermute(x, axis, [(i, (i - k) % length) for i in range(length)])  7.16 us
    all_to_all x1, starting transfers between devices, on_device(): attended = lax.all_to_all(attended, SEQ, 0, 0, tiled=True)  6.89 us
    all_to_all x1, waiting for transfers between devices, on_device(): attended = lax.all_to_all(attended, SEQ, 0, 0, tiled=True)  6.82 us
  transfers between devices with their start and end apart: 18, of which 7 were waited for; matrix products, arithmetic and copies ran while one was open for 2% of the time, Pallas kernels for 21%

profile of v1, /device:TPU:1, one launch (start us, length us, event | category | flops | bytes accessed | tf_op | source)
XLA Modules:
  0.0 126.9 jit_solution(2970761262051936205)
XLA Ops:
  0.6 0.0 copy-start
  0.7 0.8 copy-done
  1.5 0.7 constant_dynamic-slice_fusion.3
  2.2 0.8 broadcast_in_dim.16
  3.0 9.0 %all-to-all-start = ((bf16[8,32,896]{2,1,0:T(8,128)(2,1)}), bf16[8,32,896]{2,1,0:T(8,128)(2,1)S(1)}, u32[]{:S(2)}, u32[]{:S(2)}) async-start(bf16[8,32,896]{2,1,0:T(8,128)(2,1)} %broadcast_in_dim.16), calls=%async_computation | async-start | bytes 917504 | tf_op jit(solution)/shard_map/all_to_all | solution.py:40
  12.0 0.0 copy-done.15
  12.1 0.0 copy-done.3
  12.1 0.0 copy-start.2
  12.1 2.8 %collective-permute-start.4 = (bf16[272,1024]{1,0:T(8,128)(2,1)S(1)}, bf16[272,1024]{1,0:T(8,128)(2,1)S(1)}, u32[]{:S(2)}, u32[]{:S(2)}) collective-permute-start(bf16[272,1024]{1,0:T(8,128)(2,1)S(1)} %fusion.1.refs_0_), channel_id=1, source_target_pairs={{0,6},{2,0},{4,2},{6,4},{1,7},{3,1},{5,3},{7,5},{8,14},{10,8},{12,... | collective-permute-start | bytes 1671176 | tf_op jit(solution)/shard_map/ppermute | solution.py:303
  14.9 0.0 collective-permute-start.6
  14.9 1.7 %collective-permute-start.8 = (bf16[272,1024]{1,0:T(8,128)(2,1)S(1)}, bf16[272,1024]{1,0:T(8,128)(2,1)}, u32[]{:S(2)}, u32[]{:S(2)}) collective-permute-start(bf16[272,1024]{1,0:T(8,128)(2,1)S(1)} %fusion.1.refs_0_), channel_id=1, source_target_pairs={{0,4},{2,6},{4,0},{6,2},{1,5},{3,7},{5,1},{7,3},{8,12},{10,14},{12... | collective-permute-start | bytes 1671176 | tf_op jit(solution)/shard_map/ppermute | solution.py:303
  16.6 11.9 %all-to-all-done = bf16[8,32,896]{2,1,0:T(8,128)(2,1)S(1)} async-done(((bf16[8,32,896]{2,1,0:T(8,128)(2,1)}), bf16[8,32,896]{2,1,0:T(8,128)(2,1)S(1)}, u32[]{:S(2)}, u32[]{:S(2)}) %all-to-all-start) | async-done | bytes 458784 | tf_op jit(solution)/shard_map/all_to_all | solution.py:40
  28.5 1.0 broadcast_in_dim.34
  29.5 4.1 %all-to-all-start.1 = ((bf16[4,8,32,384]{3,2,1,0:T(8,128)(2,1)}), bf16[4,8,32,384]{3,2,1,0:T(8,128)(2,1)S(1)}, u32[]{:S(2)}, u32[]{:S(2)}) async-start(bf16[4,8,32,384]{3,2,1,0:T(8,128)(2,1)} %broadcast_in_dim.34), calls=%async_computation.1 | async-start | bytes 1572864 | tf_op jit(solution)/shard_map/all_to_all | solution.py:40
  33.6 0.0 copy-done.2
  33.6 0.9 collective-permute-start.3
  34.5 0.0 collective-permute-done.4.refs_2_
  34.5 5.2 %collective-permute-start.5 = (bf16[272,1024]{1,0:T(8,128)(2,1)S(1)}, bf16[272,1024]{1,0:T(8,128)(2,1)}, u32[]{:S(2)}, u32[]{:S(2)}) collective-permute-start(bf16[272,1024]{1,0:T(8,128)(2,1)S(1)} %collective-permute-done.4.refs_2_), channel_id=1, source_target_pairs={{0,1},{1,0},{2,3},{3,2},{4,5},{5,4},{6,7},{7,6},{8,9},{9,8},{10,11... | collective-permute-start | bytes 1671176 | tf_op jit(solution)/shard_map/ppermute | solution.py:306
  39.7 0.0 collective-permute-done.6.refs_4_
  39.7 3.4 %collective-permute-start.7 = (bf16[272,1024]{1,0:T(8,128)(2,1)S(1)}, bf16[272,1024]{1,0:T(8,128)(2,1)}, u32[]{:S(2)}, u32[]{:S(2)}) collective-permute-start(bf16[272,1024]{1,0:T(8,128)(2,1)S(1)} %collective-permute-done.6.refs_4_), channel_id=1, source_target_pairs={{0,1},{1,0},{2,3},{3,2},{4,5},{5,4},{6,7},{7,6},{8,9},{9,8},{10,11... | collective-permute-start | bytes 1671176 | tf_op jit(solution)/shard_map/ppermute | solution.py:306
  43.1 0.0 collective-permute-done.8.refs_6_
  43.1 0.1 collective-permute-start.9
  43.3 1.8 %all-to-all-done.1.refs_8_ = bf16[4,8,32,384]{3,2,1,0:T(8,128)(2,1)S(1)} async-done(((bf16[4,8,32,384]{3,2,1,0:T(8,128)(2,1)}), bf16[4,8,32,384]{3,2,1,0:T(8,128)(2,1)S(1)}, u32[]{:S(2)}, u32[]{:S(2)}) %all-to-all-start.1) | async-done | bytes 786464 | tf_op jit(solution)/shard_map/all_to_all | solution.py:40
  45.1 1.0 collective-permute-start
  46.1 0.0 collective-permute-done.3.refs_1_
  46.1 1.7 %collective-permute-start.1 = (bf16[8,32,512]{2,1,0:T(8,128)(2,1)S(1)}, bf16[8,32,512]{2,1,0:T(8,128)(2,1)S(1)}, u32[]{:S(2)}, u32[]{:S(2)}) collective-permute-start(bf16[8,32,512]{2,1,0:T(8,128)(2,1)S(1)} %slice.8.refs_0_), channel_id=1, source_target_pairs={{0,24},{8,0},{16,8},{24,16},{1,25},{9,1},{17,9},{25,17},{2,26},{10... | collective-permute-start | bytes 786440 | tf_op jit(solution)/shard_map/ppermute | solution.py:303
  47.8 0.0 collective-permute-done.5.refs_3_
  47.8 0.0 collective-permute-start.2
  47.8 0.6 dynamic-slice_multiply_fusion.scale
  48.3 0.6 pad_add_fusion.at
  48.9 0.0 collective-permute-done.7.refs_5_
  48.9 0.0 collective-permute-done.9.refs_7_
  49.0 26.2 %layer.1 = bf16[8,256,128]{2,1,0:T(8,128)(2,1)} custom-call(s32[3]{0:T(128)} %pad_add_fusion.at, f32[2]{0:T(128)} %dynamic-slice_multiply_fusion.scale, f32[1,1024]{1,0:T(1,128)} %bitcast.15, bf16[272,1024]{1,0:T(8,128)(2,1)} %copy-done.2, bf16[272,1024]{1,0:T(8,128)(2,1)} %collective-permute-done.3.refs_1_, bf16[272,1024]{1,0:T(8,128)(2,1)} %copy-done.6, ...), custom_call_target="tpu_custom_call" | custom-call | tf_op jit(solution)/shard_map/layer/pallas_call | solution.py:207
  75.1 0.0 copy-start.16
  75.1 0.0 collective-permute-done.refs_1_
  75.2 0.0 collective-permute-done.1.refs_2_
  75.2 0.0 collective-permute-done.2.refs_3_
  75.2 6.9 %all-to-all-start.2 = ((bf16[8,256,128]{2,1,0:T(8,128)(2,1)}), bf16[8,256,128]{2,1,0:T(8,128)(2,1)S(1)}, u32[]{:S(2)}, u32[]{:S(2)}) async-start(bf16[8,256,128]{2,1,0:T(8,128)(2,1)} %layer.1), calls=%async_computation.2 | async-start | bytes 1048576 | tf_op jit(solution)/shard_map/all_to_all | solution.py:331
  82.1 0.1 collective-permute-start.10
  82.2 0.4 collective-permute-start.11
  82.6 0.1 collective-permute-start.12
  82.7 0.4 collective-permute-start.13
  83.1 0.0 copy-done.16
  83.1 0.7 copy.18.refs_10_
  83.8 0.0 collective-permute-done.10.refs_4_
  83.8 0.2 collective-permute-done.11.refs_5_
  84.0 0.4 collective-permute-done.12.refs_6_
  84.4 0.4 collective-permute-done.13.refs_7_
  84.8 6.8 %all-to-all-done.2.pieces = bf16[8,256,128]{2,1,0:T(8,128)(2,1)S(1)} async-done(((bf16[8,256,128]{2,1,0:T(8,128)(2,1)}), bf16[8,256,128]{2,1,0:T(8,128)(2,1)S(1)}, u32[]{:S(2)}, u32[]{:S(2)}) %all-to-all-start.2) | async-done | bytes 524320 | tf_op jit(solution)/shard_map/all_to_all | solution.py:331
  91.6 0.0 copy-done.9
  91.6 0.0 copy-done.11
  91.6 0.0 copy-done.12
  91.6 0.0 copy-done.13
  91.6 0.0 copy-done.14
  91.6 0.7 copy-done.4
  92.4 4.4 %finish.1 = (bf16[256,1024]{1,0:T(8,128)(2,1)}, f32[18,256]{1,0:T(8,128)}, f32[1,18]{1,0:T(1,128)}) custom-call(s32[3]{0:T(128)} %pad_add_fusion.at, bf16[8,256,128]{2,1,0:T(8,128)(2,1)} %copy-done.4, bf16[8,32,512]{2,1,0:T(8,128)(2,1)} %copy-done.5, bf16[8,32,512]{2,1,0:T(8,128)(2,1)} %copy-done.8, bf16[8,32,512]{2,1,0:T(8,128)(2,1)} %copy-done.9, ...), custom_call_target="tpu_custom_call" | custom-call | tf_op jit(solution)/shard_map/finish/pallas_call | solution.py:266
  96.8 1.0 collective-permute-start.14
  97.7 1.0 collective-permute-done.14
  98.7 0.7 add_bitcast_fusion
  99.4 25.4 %all_to_all.20 = f32[128,1,18]{2,1,0:T(1,128)S(1)} all-to-all(f32[128,1,18]{2,1,0:T(1,128)S(1)} %broadcast_in_dim.39), channel_id=1, replica_groups=mesh['dp_0'=8,'dp_1'=4,'seq_0'=4,'seq_1'=2] {'dp_0','dp_1','seq_0'}, dimensions={0} | all-to-all | bytes 18432 | tf_op jit(solution)/shard_map/all_to_all | solution.py:40
  124.8 0.2 reduce_sum.9
  125.0 0.5 fusion.3
  125.5 0.8 subtract_bitcast_fusion
  126.3 0.6 copy.20
  (29 shorter events, 0.2 us)
Async XLA Ops:
  0.6 0.8 copy-start
  2.2 9.8 %copy-start.15 = (s32[1,256]{1,0:T(1,128)S(1)}, s32[1,256]{1,0:T(1,128)}, u32[]{:S(2)}) copy-start(s32[1,256]{1,0:T(1,128)} %param.9) | copy-start | bytes 3076
  2.2 9.8 %copy-start.3 = (bf16[1,256,1024]{2,1,0:T(8,128)(2,1)S(1)}, bf16[1,256,1024]{2,1,0:T(8,128)(2,1)}, u32[]{:S(2)}) copy-start(bf16[1,256,1024]{2,1,0:T(8,128)(2,1)} %param.8) | copy-start | bytes 1572868
  3.0 25.5 %all-to-all-start = ((bf16[8,32,896]{2,1,0:T(8,128)(2,1)}), bf16[8,32,896]{2,1,0:T(8,128)(2,1)S(1)}, u32[]{:S(2)}, u32[]{:S(2)}) async-start(bf16[8,32,896]{2,1,0:T(8,128)(2,1)} %broadcast_in_dim.16), calls=%async_computation | async-start | bytes 917504 | tf_op jit(solution)/shard_map/all_to_all | solution.py:40
  12.1 21.5 %copy-start.2 = (bf16[272,1024]{1,0:T(8,128)(2,1)}, bf16[272,1024]{1,0:T(8,128)(2,1)S(1)}, u32[]{:S(2)}) copy-start(bf16[272,1024]{1,0:T(8,128)(2,1)S(1)} %fusion.1.refs_0_) | copy-start | bytes 1671172
  12.1 22.4 %collective-permute-start.4 = (bf16[272,1024]{1,0:T(8,128)(2,1)S(1)}, bf16[272,1024]{1,0:T(8,128)(2,1)S(1)}, u32[]{:S(2)}, u32[]{:S(2)}) collective-permute-start(bf16[272,1024]{1,0:T(8,128)(2,1)S(1)} %fusion.1.refs_0_), channel_id=1, source_target_pairs={{0,6},{2,0},{4,2},{6,4},{1,7},{3,1},{5,3},{7,5},{8,14},{10,8},{12,... | collective-permute-start | bytes 1671176 | tf_op jit(solution)/shard_map/ppermute | solution.py:303
  14.9 24.8 %collective-permute-start.6 = (bf16[272,1024]{1,0:T(8,128)(2,1)S(1)}, bf16[272,1024]{1,0:T(8,128)(2,1)S(1)}, u32[]{:S(2)}, u32[]{:S(2)}) collective-permute-start(bf16[272,1024]{1,0:T(8,128)(2,1)S(1)} %fusion.1.refs_0_), channel_id=1, source_target_pairs={{0,2},{2,4},{4,6},{6,0},{1,3},{3,5},{5,7},{7,1},{8,10},{10,12},{12... | collective-permute-start | bytes 1671176 | tf_op jit(solution)/shard_map/ppermute | solution.py:303
  14.9 28.2 %collective-permute-start.8 = (bf16[272,1024]{1,0:T(8,128)(2,1)S(1)}, bf16[272,1024]{1,0:T(8,128)(2,1)}, u32[]{:S(2)}, u32[]{:S(2)}) collective-permute-start(bf16[272,1024]{1,0:T(8,128)(2,1)S(1)} %fusion.1.refs_0_), channel_id=1, source_target_pairs={{0,4},{2,6},{4,0},{6,2},{1,5},{3,7},{5,1},{7,3},{8,12},{10,14},{12... | collective-permute-start | bytes 1671176 | tf_op jit(solution)/shard_map/ppermute | solution.py:303
  29.5 18.3 %copy-start.17 = (f32[16]{0:T(128)S(1)}, f32[16]{0:T(128)}, u32[]{:S(2)}) copy-start(f32[16]{0:T(128)} %param.12) | copy-start | bytes 196
  29.5 15.6 %all-to-all-start.1 = ((bf16[4,8,32,384]{3,2,1,0:T(8,128)(2,1)}), bf16[4,8,32,384]{3,2,1,0:T(8,128)(2,1)S(1)}, u32[]{:S(2)}, u32[]{:S(2)}) async-start(bf16[4,8,32,384]{3,2,1,0:T(8,128)(2,1)} %broadcast_in_dim.34), calls=%async_computation.1 | async-start | bytes 1572864 | tf_op jit(solution)/shard_map/all_to_all | solution.py:40
  33.6 12.5 %collective-permute-start.3 = (bf16[272,1024]{1,0:T(8,128)(2,1)S(1)}, bf16[272,1024]{1,0:T(8,128)(2,1)}, u32[]{:S(2)}, u32[]{:S(2)}) collective-permute-start(bf16[272,1024]{1,0:T(8,128)(2,1)S(1)} %fusion.1.refs_0_), channel_id=1, source_target_pairs={{0,1},{1,0},{2,3},{3,2},{4,5},{5,4},{6,7},{7,6},{8,9},{9,8},{10,11... | collective-permute-start | bytes 1671176 | tf_op jit(solution)/shard_map/ppermute | solution.py:306
  34.5 14.4 %copy-start.6 = (bf16[272,1024]{1,0:T(8,128)(2,1)}, bf16[272,1024]{1,0:T(8,128)(2,1)S(1)}, u32[]{:S(2)}) copy-start(bf16[272,1024]{1,0:T(8,128)(2,1)S(1)} %collective-permute-done.4.refs_2_) | copy-start | bytes 1671172
  34.5 13.3 %collective-permute-start.5 = (bf16[272,1024]{1,0:T(8,128)(2,1)S(1)}, bf16[272,1024]{1,0:T(8,128)(2,1)}, u32[]{:S(2)}, u32[]{:S(2)}) collective-permute-start(bf16[272,1024]{1,0:T(8,128)(2,1)S(1)} %collective-permute-done.4.refs_2_), channel_id=1, source_target_pairs={{0,1},{1,0},{2,3},{3,2},{4,5},{5,4},{6,7},{7,6},{8,9},{9,8},{10,11... | collective-permute-start | bytes 1671176 | tf_op jit(solution)/shard_map/ppermute | solution.py:306
  39.7 9.2 %copy-start.7 = (bf16[272,1024]{1,0:T(8,128)(2,1)}, bf16[272,1024]{1,0:T(8,128)(2,1)S(1)}, u32[]{:S(2)}) copy-start(bf16[272,1024]{1,0:T(8,128)(2,1)S(1)} %collective-permute-done.6.refs_4_) | copy-start | bytes 1671172
  39.7 9.2 %collective-permute-start.7 = (bf16[272,1024]{1,0:T(8,128)(2,1)S(1)}, bf16[272,1024]{1,0:T(8,128)(2,1)}, u32[]{:S(2)}, u32[]{:S(2)}) collective-permute-start(bf16[272,1024]{1,0:T(8,128)(2,1)S(1)} %collective-permute-done.6.refs_4_), channel_id=1, source_target_pairs={{0,1},{1,0},{2,3},{3,2},{4,5},{5,4},{6,7},{7,6},{8,9},{9,8},{10,11... | collective-permute-start | bytes 1671176 | tf_op jit(solution)/shard_map/ppermute | solution.py:306
  43.1 5.8 %collective-permute-start.9 = (bf16[272,1024]{1,0:T(8,128)(2,1)}, bf16[272,1024]{1,0:T(8,128)(2,1)}, u32[]{:S(2)}, u32[]{:S(2)}) collective-permute-start(bf16[272,1024]{1,0:T(8,128)(2,1)} %collective-permute-done.8.refs_6_), channel_id=1, source_target_pairs={{0,1},{1,0},{2,3},{3,2},{4,5},{5,4},{6,7},{7,6},{8,9},{9,8},{10,11... | collective-permute-start | bytes 1671176 | tf_op jit(solution)/shard_map/ppermute | solution.py:306
  43.3 38.8 %copy-start.5 = (bf16[8,32,512]{2,1,0:T(8,128)(2,1)}, bf16[8,32,512]{2,1,0:T(8,128)(2,1)S(1)}, u32[]{:S(2)}) copy-start(bf16[8,32,512]{2,1,0:T(8,128)(2,1)S(1)} %slice.8.refs_0_) | copy-start | bytes 786436
  45.1 3.9 %copy-start.1 = (bf16[4,8,32,384]{3,2,1,0:T(8,128)(2,1)}, bf16[4,8,32,384]{3,2,1,0:T(8,128)(2,1)S(1)}, u32[]{:S(2)}) copy-start(bf16[4,8,32,384]{3,2,1,0:T(8,128)(2,1)S(1)} %all-to-all-done.1.refs_8_) | copy-start | bytes 2359300
  45.1 30.1 %collective-permute-start = (bf16[8,32,512]{2,1,0:T(8,128)(2,1)S(1)}, bf16[8,32,512]{2,1,0:T(8,128)(2,1)S(1)}, u32[]{:S(2)}, u32[]{:S(2)}) collective-permute-start(bf16[8,32,512]{2,1,0:T(8,128)(2,1)S(1)} %slice.8.refs_0_), channel_id=1, source_target_pairs={{0,16},{8,24},{16,0},{24,8},{1,17},{9,25},{17,1},{25,9},{2,18},{10... | collective-permute-start | bytes 786440 | tf_op jit(solution)/shard_map/ppermute | solution.py:303
  46.1 29.0 %collective-permute-start.1 = (bf16[8,32,512]{2,1,0:T(8,128)(2,1)S(1)}, bf16[8,32,512]{2,1,0:T(8,128)(2,1)S(1)}, u32[]{:S(2)}, u32[]{:S(2)}) collective-permute-start(bf16[8,32,512]{2,1,0:T(8,128)(2,1)S(1)} %slice.8.refs_0_), channel_id=1, source_target_pairs={{0,24},{8,0},{16,8},{24,16},{1,25},{9,1},{17,9},{25,17},{2,26},{10... | collective-permute-start | bytes 786440 | tf_op jit(solution)/shard_map/ppermute | solution.py:303
  47.8 27.4 %collective-permute-start.2 = (bf16[8,32,512]{2,1,0:T(8,128)(2,1)S(1)}, bf16[8,32,512]{2,1,0:T(8,128)(2,1)S(1)}, u32[]{:S(2)}, u32[]{:S(2)}) collective-permute-start(bf16[8,32,512]{2,1,0:T(8,128)(2,1)S(1)} %slice.8.refs_0_), channel_id=1, source_target_pairs={{0,8},{8,16},{16,24},{24,0},{1,9},{9,17},{17,25},{25,1},{2,10},{10... | collective-permute-start | bytes 786440 | tf_op jit(solution)/shard_map/ppermute | solution.py:303
  75.1 8.0 %copy-start.16 = (f32[18]{0:T(128)S(1)}, f32[18]{0:T(128)}, u32[]{:S(2)}) copy-start(f32[18]{0:T(128)} %param.15) | copy-start | bytes 220
  75.2 16.4 %copy-start.8 = (bf16[8,32,512]{2,1,0:T(8,128)(2,1)}, bf16[8,32,512]{2,1,0:T(8,128)(2,1)S(1)}, u32[]{:S(2)}) copy-start(bf16[8,32,512]{2,1,0:T(8,128)(2,1)S(1)} %collective-permute-done.refs_1_) | copy-start | bytes 786436
  75.2 16.4 %copy-start.9 = (bf16[8,32,512]{2,1,0:T(8,128)(2,1)}, bf16[8,32,512]{2,1,0:T(8,128)(2,1)S(1)}, u32[]{:S(2)}) copy-start(bf16[8,32,512]{2,1,0:T(8,128)(2,1)S(1)} %collective-permute-done.1.refs_2_) | copy-start | bytes 786436
  75.2 16.4 %copy-start.10 = (bf16[8,32,512]{2,1,0:T(8,128)(2,1)}, bf16[8,32,512]{2,1,0:T(8,128)(2,1)S(1)}, u32[]{:S(2)}) copy-start(bf16[8,32,512]{2,1,0:T(8,128)(2,1)S(1)} %collective-permute-done.2.refs_3_) | copy-start | bytes 786436
  75.2 16.4 %all-to-all-start.2 = ((bf16[8,256,128]{2,1,0:T(8,128)(2,1)}), bf16[8,256,128]{2,1,0:T(8,128)(2,1)S(1)}, u32[]{:S(2)}, u32[]{:S(2)}) async-start(bf16[8,256,128]{2,1,0:T(8,128)(2,1)} %layer.1), calls=%async_computation.2 | async-start | bytes 1048576 | tf_op jit(solution)/shard_map/all_to_all | solution.py:331
  82.1 1.7 %collective-permute-start.10 = (bf16[8,32,512]{2,1,0:T(8,128)(2,1)S(1)}, bf16[8,32,512]{2,1,0:T(8,128)(2,1)S(1)}, u32[]{:S(2)}, u32[]{:S(2)}) collective-permute-start(bf16[8,32,512]{2,1,0:T(8,128)(2,1)S(1)} %slice.8.refs_0_), channel_id=1, source_target_pairs={{0,1},{1,0},{2,3},{3,2},{4,5},{5,4},{6,7},{7,6},{8,9},{9,8},{10,11... | collective-permute-start | bytes 786440 | tf_op jit(solution)/shard_map/ppermute | solution.py:306
  82.2 1.8 %collective-permute-start.11 = (bf16[8,32,512]{2,1,0:T(8,128)(2,1)S(1)}, bf16[8,32,512]{2,1,0:T(8,128)(2,1)S(1)}, u32[]{:S(2)}, u32[]{:S(2)}) collective-permute-start(bf16[8,32,512]{2,1,0:T(8,128)(2,1)S(1)} %collective-permute-done.refs_1_), channel_id=1, source_target_pairs={{0,1},{1,0},{2,3},{3,2},{4,5},{5,4},{6,7},{7,6},{8,9},{9,8},{10,11... | collective-permute-start | bytes 786440 | tf_op jit(solution)/shard_map/ppermute | solution.py:306
  82.6 1.8 %collective-permute-start.12 = (bf16[8,32,512]{2,1,0:T(8,128)(2,1)S(1)}, bf16[8,32,512]{2,1,0:T(8,128)(2,1)S(1)}, u32[]{:S(2)}, u32[]{:S(2)}) collective-permute-start(bf16[8,32,512]{2,1,0:T(8,128)(2,1)S(1)} %collective-permute-done.1.refs_2_), channel_id=1, source_target_pairs={{0,1},{1,0},{2,3},{3,2},{4,5},{5,4},{6,7},{7,6},{8,9},{9,8},{10,11... | collective-permute-start | bytes 786440 | tf_op jit(solution)/shard_map/ppermute | solution.py:306
  82.7 2.1 %collective-permute-start.13 = (bf16[8,32,512]{2,1,0:T(8,128)(2,1)S(1)}, bf16[8,32,512]{2,1,0:T(8,128)(2,1)S(1)}, u32[]{:S(2)}, u32[]{:S(2)}) collective-permute-start(bf16[8,32,512]{2,1,0:T(8,128)(2,1)S(1)} %collective-permute-done.2.refs_3_), channel_id=1, source_target_pairs={{0,1},{1,0},{2,3},{3,2},{4,5},{5,4},{6,7},{7,6},{8,9},{9,8},{10,11... | collective-permute-start | bytes 786440 | tf_op jit(solution)/shard_map/ppermute | solution.py:306
  83.8 7.8 %copy-start.11 = (bf16[8,32,512]{2,1,0:T(8,128)(2,1)}, bf16[8,32,512]{2,1,0:T(8,128)(2,1)S(1)}, u32[]{:S(2)}) copy-start(bf16[8,32,512]{2,1,0:T(8,128)(2,1)S(1)} %collective-permute-done.10.refs_4_) | copy-start | bytes 786436
  84.0 7.6 %copy-start.12 = (bf16[8,32,512]{2,1,0:T(8,128)(2,1)}, bf16[8,32,512]{2,1,0:T(8,128)(2,1)S(1)}, u32[]{:S(2)}) copy-start(bf16[8,32,512]{2,1,0:T(8,128)(2,1)S(1)} %collective-permute-done.11.refs_5_) | copy-start | bytes 786436
  84.4 7.2 %copy-start.13 = (bf16[8,32,512]{2,1,0:T(8,128)(2,1)}, bf16[8,32,512]{2,1,0:T(8,128)(2,1)S(1)}, u32[]{:S(2)}) copy-start(bf16[8,32,512]{2,1,0:T(8,128)(2,1)S(1)} %collective-permute-done.12.refs_6_) | copy-start | bytes 786436
  84.8 6.9 %copy-start.14 = (bf16[8,32,512]{2,1,0:T(8,128)(2,1)}, bf16[8,32,512]{2,1,0:T(8,128)(2,1)S(1)}, u32[]{:S(2)}) copy-start(bf16[8,32,512]{2,1,0:T(8,128)(2,1)S(1)} %collective-permute-done.13.refs_7_) | copy-start | bytes 786436
  91.6 0.8 copy-start.4
  96.8 1.9 %collective-permute-start.14 = (f32[1,18]{1,0:T(1,128)}, f32[1,18]{1,0:T(1,128)S(1)}, u32[]{:S(2)}, u32[]{:S(2)}) collective-permute-start(f32[1,18]{1,0:T(1,128)} %get-tuple-element.20), channel_id=1, source_target_pairs={{0,1},{1,0},{2,3},{3,2},{4,5},{5,4},{6,7},{7,6},{8,9},{9,8},{10,11... | collective-permute-start | bytes 224 | tf_op jit(solution)/shard_map/ppermute | solution.py:306

commit v2 on v1

--- a/solution.py
+++ b/solution.py
@@ -44,24 +44,22 @@
     return pl.BlockSpec(memory_space=pl.ANY)
 
 
-def layer_kernel(at, scale, gain, *refs):
+def layer_kernel(scales, gain, *refs):
     pieces, shards, out = refs[:8], refs[8], refs[9]
     held, weights, normed, labels, queries, keys, values, total, even, odd, table, sems = refs[10:]
-    core, chip = at[0], at[1]
+    core, chip = lax.axis_index("seq_1"), lax.axis_index("seq_0")
+    first = (2 * chip + core) * 2
+    scale = [scales[first] / math.sqrt(64), scales[first + 1] / math.sqrt(64)]
     rows = ROWS
     arrivals = [
         pltpu.make_async_copy(pieces[i], held.at[i // 2, i % 2], sems.at[i]) for i in range(8)
     ]
-    for i in range(4):
-        copy = pltpu.make_async_copy(shards.at[i], weights.at[:, i], sems.at[8 + i])
+    matrix = pltpu.make_async_copy(shards.at[:, pl.ds(0, 384)], weights, sems.at[8])
+    matrix.start()
+    for copy in arrivals:
         copy.start()
-        arrivals.append(copy)
-    for copy in arrivals[:8]:
-        copy.start()
-    for copy in arrivals[8:]:
-        copy.wait()
-    width, head = held.shape[3], 64
-    matrix = weights[...].reshape(width, 384)
+    matrix.wait()
+    head = 64
     lane = lax.broadcasted_iota(jnp.int32, (rows, 128), 1)
     spot = lax.broadcasted_iota(jnp.int32, (head, rows), 0)
     for pair in range(4):
@@ -71,7 +69,7 @@
             wide = held[pair, side, 0:rows].astype(F32)
             inv = lax.rsqrt(jnp.mean(wide * wide, axis=-1, keepdims=True) + EPS)
             normed[side * rows : (side + 1) * rows] = (wide * inv * gain[...]).astype(BF16)
-        both = jnp.dot(normed[...], matrix, preferred_element_type=F32).astype(BF16).astype(F32)
+        both = jnp.dot(normed[...], weights[...], preferred_element_type=F32).astype(BF16).astype(F32)
         for side in range(2):
             part = core if side == 0 else 1 - core
             block = 2 * lax.rem(chip + step, 4) + part
@@ -101,12 +99,12 @@
             ).astype(BF16)
 
     every = labels[...]
-    first, last = every[:, 0:1], every[:, rows - 1 : rows]
+    opening, closing = every[:, 0:1], every[:, rows - 1 : rows]
     below = jnp.zeros((8, rows), jnp.int32)
     upto = jnp.zeros((8, rows), jnp.int32)
     for b in range(8):
-        below += (every[b : b + 1] < first).astype(jnp.int32)
-        upto += (every[b : b + 1] <= last).astype(jnp.int32)
+        below += (every[b : b + 1] < opening).astype(jnp.int32)
+        upto += (every[b : b + 1] <= closing).astype(jnp.int32)
     low = jnp.sum(below, axis=1, keepdims=True)
     high = jnp.sum(upto, axis=1, keepdims=True)
     low = low & -128
@@ -149,7 +147,7 @@
                 preferred_element_type=F32,
             )
 
-    small = jnp.maximum(scale[0], scale[1]) * 8.0 <= SAFE
+    small = jnp.maximum(scales[first], scales[first + 1]) <= SAFE
 
     @pl.when(small)
     def _():
@@ -202,16 +200,16 @@
         out[b] = (over / under).astype(BF16)
 
 
-def layer(at, scale, gain, pieces, shard):
+def layer(scales, gain, pieces, shard):
     total = 8 * ROWS
     return pl.pallas_call(
         layer_kernel,
-        in_specs=[smem(), smem(), vmem()] + [any_space()] * 9,
+        in_specs=[smem(), vmem()] + [any_space()] * 9,
         out_specs=vmem(),
         out_shape=jax.ShapeDtypeStruct((8, ROWS, 128), BF16),
         scratch_shapes=[
             pltpu.VMEM((4, 2, *pieces[0].shape), BF16),
-            pltpu.VMEM((8, 4, 32, 384), BF16),
+            pltpu.VMEM((shard.shape[0], 384), BF16),
             pltpu.VMEM((2 * ROWS, pieces[0].shape[1]), BF16),
             pltpu.VMEM((8, ROWS), jnp.int32),
             pltpu.VMEM((2, total + ROWS, 128), BF16),
@@ -221,36 +219,34 @@
             pltpu.VMEM((2, ROWS, KEYS), F32),
             pltpu.VMEM((2, ROWS, KEYS), F32),
             pltpu.SMEM((2, 48), jnp.int32),
-            pltpu.SemaphoreType.DMA((12,)),
+            pltpu.SemaphoreType.DMA((9,)),
         ],
         compiler_params=params(),
         name="layer",
-    )(at, scale, gain, *pieces, shard)
-
-
-def finish_kernel(at, pieces, *refs):
+    )(scales, gain, *pieces, shard)
+
+
+def finish_kernel(pieces, *refs):
     shards, (rows, bits, offset, mixed, probs, sums, weights, joined, sems) = refs[:8], refs[8:]
+    core, chip = lax.axis_index("seq_1"), lax.axis_index("seq_0")
     copies = []
     for i in range(8):
-        part = at[0] if i < 4 else 1 - at[0]
-        place = lax.rem(at[2] + (0, 2, 1, 3)[i % 4], 4)
-        copies.append(pltpu.make_async_copy(shards[i], weights.at[part, :, place], sems.at[i]))
+        block = 2 * lax.rem(chip + i % 4, 4) + (core if i < 4 else 1 - core)
+        columns = pl.ds(pl.multiple_of(block * 128, 128), 128)
+        copies.append(pltpu.make_async_copy(shards[i], weights.at[:, columns], sems.at[i]))
         copies[i].start()
     for source in range(8):
         joined[:, source * 128 : (source + 1) * 128] = pieces[source]
     for copy in copies:
         copy.wait()
-    for part in range(2):
-        columns = slice(part * 512, part * 512 + 512)
-        moved = jnp.dot(
-            joined[...], weights[part].reshape(1024, 512), preferred_element_type=F32
-        )
-        mixed[:, columns] = (rows[:, columns].astype(F32) + moved).astype(BF16)
+    moved = jnp.dot(joined[...], weights[...], preferred_element_type=F32)
+    mixed[...] = (rows[...].astype(F32) + moved).astype(BF16)
     logits = lax.dot_general(
         bits[...], mixed[...], (((1,), (1,)), ((), ())), preferred_element_type=F32
     )
     chance = jax.nn.sigmoid(4.0 * (logits + offset[...]))
-    probs[...] = chance
+    for b in range(chance.shape[0]):
+        probs[b] = chance[b : b + 1]
     row = lax.dot_general(
         jnp.ones((8, chance.shape[1]), F32),
         chance,
@@ -261,25 +257,25 @@
     sums[...] = row[0:1]
 
 
-def finish(at, pieces, shards, rows, bits, offset):
+def finish(pieces, shards, rows, bits, offset):
     count = rows.shape[0]
     return pl.pallas_call(
         finish_kernel,
-        in_specs=[smem(), vmem()] + [any_space()] * 8 + [vmem()] * 3,
+        in_specs=[vmem()] + [any_space()] * 8 + [vmem()] * 3,
         out_specs=[vmem()] * 3,
         out_shape=[
             jax.ShapeDtypeStruct(rows.shape, BF16),
-            jax.ShapeDtypeStruct((bits.shape[0], count), F32),
+            jax.ShapeDtypeStruct((bits.shape[0], 1, count), F32),
             jax.ShapeDtypeStruct((1, bits.shape[0]), F32),
         ],
         scratch_shapes=[
-            pltpu.VMEM((2, 8, 4, 32, 512), BF16),
+            pltpu.VMEM((1024, 1024), BF16),
             pltpu.VMEM((count, 1024), BF16),
             pltpu.SemaphoreType.DMA((8,)),
         ],
         compiler_params=params(),
         name="finish",
-    )(at, pieces, *shards, rows, bits, offset)
+    )(pieces, *shards, rows, bits, offset)
 
 
 def on_device(
@@ -294,10 +290,7 @@
 ):
     rows = residual_tiles[0]
     count, width = rows.shape
-    core = lax.axis_index("seq_1")
     member = lax.axis_index(SEQ)
-    at = jnp.stack([core, lax.axis_index("seq_0"), lax.axis_index("dp_1")]).astype(jnp.int32)
-
     def from_step(x, k, axis="seq_0"):
         length = lax.axis_size(axis)
         return lax.ppermute(x, axis, [(i, (i - k) % length) for i in range(length)])
@@ -315,22 +308,18 @@
             lax.dynamic_slice_in_dim(triple_projector, member * 128 + 1024 * i, 128, 1)
             for i in range(3)
         ]
-        + [lax.dynamic_slice_in_dim(final_projector, core * 512, 512, 1)],
+        + [lax.dynamic_slice_in_dim(final_projector, member * 128, 128, 1)],
         axis=1,
     )
-    owned = copy_for_each(owned, "dp_0")
-    shard, mixing = owned[:, :, :384], owned[:, :, 384:]
-    shard = copy_for_each(shard, "dp_1")
-    mixing, _ = lax.optimization_barrier((mixing, shard))
-    mixings = [mixing] + [from_step(mixing, k, "dp_1") for k in (2, 1, 3)]
-
-    scale = lax.dynamic_slice_in_dim(logit_scaling, member * 2, 2, 0) / math.sqrt(64)
-    attended = layer(at, scale, prenorm_multiplier[None], pieces, shard)
+    shard = copy_for_each(owned, DP).reshape(width, 512)
+    mixing, _ = lax.optimization_barrier((shard[:, 384:], near))
+    mixings = [mixing] + [from_step(mixing, k) for k in (1, 2, 3)]
+
+    attended = layer(logit_scaling, prenorm_multiplier[None], pieces, shard)
     mixings, attended = lax.optimization_barrier((mixings, attended))
     mixings = mixings + [from_other_core(m) for m in mixings]
     attended = lax.all_to_all(attended, SEQ, 0, 0, tiled=True)
     mixed, probs, sums = finish(
-        at,
         attended,
         mixings,
         rows,
@@ -341,7 +330,7 @@
     sums = copy_for_each(sums, ("dp_0", "dp_1", "seq_0"))
     marginal = jnp.sum(sums, axis=(0, 1)) / (count * lax.axis_size(ALL))
     code_entropy = -(marginal * jnp.log(marginal) + (1.0 - marginal) * jnp.log(1.0 - marginal))
-    bit_codes = (probs - marginal[:, None])[None]
+    bit_codes = jnp.swapaxes(probs - marginal[:, None, None], 0, 1)
     return (mixed[None], bit_codes, code_entropy)
 
 

time: 128 us -> 131 us (1.023); the launches traced: 127 us -> 132 us
  Pallas kernels: 30.6 us -> 37.1 us
  starting transfers between devices: 38.8 us -> 43.9 us
  waiting for transfers between devices: 22.4 us -> 18 us
    all_to_all x2 -> x1, waiting for transfers between devices: 13.7 us -> 0.01 us  [copy_for_each(): lax.all_to_all(jnp.broadcast_to(x[None], (length, *x.shape)), axis, 0, 0,...]
    ppermute x6, waiting for transfers between devices: 0.02 us -> 8.57 us  [from_step(): return lax.ppermute(x, axis, [(i, (i - k) % length) for i in range(length)])]
    ppermute x9, starting transfers between devices: 11.6 us -> 20 us  [from_other_core(): return lax.ppermute(x, 'seq_1', [(0, 1), (1, 0)])]
    pallas_call x2, Pallas kernels: 30.6 us -> 37.1 us  [the longest x1 32.7 us: layer(): pl.pallas_call(layer_kernel, in_specs=[smem(), vmem()] + [any_space()] *...]
    transpose x0 -> x1, other arithmetic: none -> 1.41 us  [on_device(): bit_codes = jnp.swapaxes(probs - marginal[:, None, None], 0, 1)]
    all_to_all x2 -> x1, starting transfers between devices: 13.2 us -> 12 us  [copy_for_each(): lax.all_to_all(jnp.broadcast_to(x[None], (length, *x.shape)), axis, 0, 0,...]
  transfers between devices with their start and end apart: 18 -> 17, of which waited for: 7 -> 7; matrix products, arithmetic and copies ran while one was open for 2% -> 1% of each run, Pallas kernels for 21% -> 25%
where the time goes in v2:
time: 131 us; the launch traced here: 132 us
  starting transfers between devices  43.9 us (34%)
  Pallas kernels  37.1 us (28%)
  blocking collectives  24.8 us (19%)
  waiting for transfers between devices  18 us (14%)
  local copies, waits for them, and re-layouts  4.82 us (4%)
  other arithmetic  2.8 us (2%)
    pallas_call x1, Pallas kernels, layer(): pl.pallas_call(layer_kernel, in_specs=[smem(), vmem()] + [any_space()] *...  32.7 us
    all_to_all x1, blocking collectives, copy_for_each(): lax.all_to_all(jnp.broadcast_to(x[None], (length, *x.shape)), axis, 0, 0,...  24.8 us
    ppermute x9, starting transfers between devices, from_other_core(): return lax.ppermute(x, 'seq_1', [(0, 1), (1, 0)])  20 us
    all_to_all x1, starting transfers between devices, copy_for_each(): lax.all_to_all(jnp.broadcast_to(x[None], (length, *x.shape)), axis, 0, 0,...  12 us
    ppermute x6, waiting for transfers between devices, from_step(): return lax.ppermute(x, axis, [(i, (i - k) % length) for i in range(length)])  8.57 us
    all_to_all x1, waiting for transfers between devices, on_device(): attended = lax.all_to_all(attended, SEQ, 0, 0, tiled=True)  6.61 us
    ppermute x6, starting transfers between devices, from_step(): return lax.ppermute(x, axis, [(i, (i - k) % length) for i in range(length)])  6.08 us
    all_to_all x1, starting transfers between devices, on_device(): attended = lax.all_to_all(attended, SEQ, 0, 0, tiled=True)  5.73 us
  transfers between devices with their start and end apart: 17, of which 7 were waited for; matrix products, arithmetic and copies ran while one was open for 1% of the time, Pallas kernels for 25%

profile of v2, /device:TPU:1, one launch (start us, length us, event | category | flops | bytes accessed | tf_op | source)
XLA Modules:
  0.0 132.2 jit_solution(16402974963083676544)
XLA Ops:
  0.6 0.8 constant_dynamic-slice_fusion.3
  1.4 1.1 broadcast_in_dim.24
  2.5 12.0 %all-to-all-start = ((bf16[32,32,512]{2,1,0:T(8,128)(2,1)}), bf16[32,32,512]{2,1,0:T(8,128)(2,1)S(1)}, u32[]{:S(2)}, u32[]{:S(2)}) async-start(bf16[32,32,512]{2,1,0:T(8,128)(2,1)} %broadcast_in_dim.24), calls=%async_computation | async-start | bytes 2097152 | tf_op jit(solution)/shard_map/all_to_all | solution.py:40
  14.5 0.0 copy-done.16
  14.5 0.0 copy-done.2
  14.6 0.0 copy-start.1
  14.6 2.8 %collective-permute-start = (bf16[272,1024]{1,0:T(8,128)(2,1)S(1)}, bf16[272,1024]{1,0:T(8,128)(2,1)S(1)}, u32[]{:S(2)}, u32[]{:S(2)}) collective-permute-start(bf16[272,1024]{1,0:T(8,128)(2,1)S(1)} %fusion.1.refs_0_), channel_id=1, source_target_pairs={{0,6},{2,0},{4,2},{6,4},{1,7},{3,1},{5,3},{7,5},{8,14},{10,8},{12,... | collective-permute-start | bytes 1671176 | tf_op jit(solution)/shard_map/ppermute | solution.py:296
  17.4 0.0 collective-permute-start.1
  17.4 1.6 %collective-permute-start.2 = (bf16[272,1024]{1,0:T(8,128)(2,1)S(1)}, bf16[272,1024]{1,0:T(8,128)(2,1)S(1)}, u32[]{:S(2)}, u32[]{:S(2)}) collective-permute-start(bf16[272,1024]{1,0:T(8,128)(2,1)S(1)} %fusion.1.refs_0_), channel_id=1, source_target_pairs={{0,4},{2,6},{4,0},{6,2},{1,5},{3,7},{5,1},{7,3},{8,12},{10,14},{12... | collective-permute-start | bytes 1671176 | tf_op jit(solution)/shard_map/ppermute | solution.py:296
  19.1 1.8 %collective-permute-start.6 = (bf16[272,1024]{1,0:T(8,128)(2,1)S(1)}, bf16[272,1024]{1,0:T(8,128)(2,1)}, u32[]{:S(2)}, u32[]{:S(2)}) collective-permute-start(bf16[272,1024]{1,0:T(8,128)(2,1)S(1)} %fusion.1.refs_0_), channel_id=1, source_target_pairs={{0,1},{1,0},{2,3},{3,2},{4,5},{5,4},{6,7},{7,6},{8,9},{9,8},{10,11... | collective-permute-start | bytes 1671176 | tf_op jit(solution)/shard_map/ppermute | solution.py:299
  20.8 8.6 %collective-permute-done.refs_2_ = bf16[272,1024]{1,0:T(8,128)(2,1)S(1)} collective-permute-done((bf16[272,1024]{1,0:T(8,128)(2,1)S(1)}, bf16[272,1024]{1,0:T(8,128)(2,1)S(1)}, u32[]{:S(2)}, u32[]{:S(2)}) %collective-permute-start) | collective-permute-done | bytes 557088 | tf_op jit(solution)/shard_map/ppermute | solution.py:296
  29.4 12.8 %collective-permute-start.7 = (bf16[272,1024]{1,0:T(8,128)(2,1)S(1)}, bf16[272,1024]{1,0:T(8,128)(2,1)}, u32[]{:S(2)}, u32[]{:S(2)}) collective-permute-start(bf16[272,1024]{1,0:T(8,128)(2,1)S(1)} %collective-permute-done.refs_2_), channel_id=1, source_target_pairs={{0,1},{1,0},{2,3},{3,2},{4,5},{5,4},{6,7},{7,6},{8,9},{9,8},{10,11... | collective-permute-start | bytes 1671176 | tf_op jit(solution)/shard_map/ppermute | solution.py:299
  42.2 0.0 collective-permute-done.1.refs_4_
  42.2 3.4 %collective-permute-start.8 = (bf16[272,1024]{1,0:T(8,128)(2,1)S(1)}, bf16[272,1024]{1,0:T(8,128)(2,1)}, u32[]{:S(2)}, u32[]{:S(2)}) collective-permute-start(bf16[272,1024]{1,0:T(8,128)(2,1)S(1)} %collective-permute-done.1.refs_4_), channel_id=1, source_target_pairs={{0,1},{1,0},{2,3},{3,2},{4,5},{5,4},{6,7},{7,6},{8,9},{9,8},{10,11... | collective-permute-start | bytes 1671176 | tf_op jit(solution)/shard_map/ppermute | solution.py:299
  45.6 0.0 collective-permute-done.2.refs_6_
  45.6 0.1 collective-permute-start.9
  45.7 0.0 all-to-all-done
  45.7 0.0 copy-start.4
  45.8 0.5 collective-permute-start.3
  46.3 0.0 collective-permute-done.6.refs_1_
  46.3 0.0 collective-permute-start.4
  46.3 0.0 collective-permute-done.7.refs_3_
  46.3 1.1 collective-permute-start.5
  47.4 0.0 collective-permute-done.8.refs_5_
  47.4 0.7 collective-permute-done.9.refs_7_
  48.1 0.0 copy-done.1
  48.1 0.0 copy-done.5
  48.1 0.0 copy-done.6
  48.1 0.0 copy-done.7
  48.1 0.0 copy-done
  48.1 32.7 %layer.1 = bf16[8,256,128]{2,1,0:T(8,128)(2,1)} custom-call(f32[16]{0:T(128)} %scales.1, f32[1,1024]{1,0:T(1,128)} %bitcast.15, bf16[272,1024]{1,0:T(8,128)(2,1)} %copy-done.1, bf16[272,1024]{1,0:T(8,128)(2,1)} %collective-permute-done.6.refs_1_, bf16[272,1024]{1,0:T(8,128)(2,1)} %copy-done.5, bf16[272,1024]{1,0:T(8,128)(2,1)} %collective-permute-done.7.refs_3_, ...), custom_call_target="tpu_custom_call" | custom-call | tf_op jit(solution)/shard_map/layer/pallas_call | solution.py:205
  80.8 0.0 copy-start.17
  80.8 0.0 collective-permute-done.3.refs_1_
  80.8 0.0 copy-start.8
  80.8 0.0 collective-permute-done.4.refs_2_
  80.8 0.7 copy-done.8
  81.5 0.7 copy-done.10
  82.2 0.0 collective-permute-done.5.refs_3_
  82.2 5.7 %all-to-all-start.1 = ((bf16[8,256,128]{2,1,0:T(8,128)(2,1)}), bf16[8,256,128]{2,1,0:T(8,128)(2,1)S(1)}, u32[]{:S(2)}, u32[]{:S(2)}) async-start(bf16[8,256,128]{2,1,0:T(8,128)(2,1)} %layer.1), calls=%async_computation.1 | async-start | bytes 1048576 | tf_op jit(solution)/shard_map/all_to_all | solution.py:321
  88.0 0.0 copy-done.4
  88.0 0.1 collective-permute-start.10
  88.1 0.0 copy-done.9
  88.1 0.4 collective-permute-start.11
  88.5 0.0 copy-done.11
  88.5 0.1 collective-permute-start.12
  88.6 0.4 collective-permute-start.13
  89.0 0.0 copy-done.17
  89.0 0.7 copy.15.refs_10_
  89.7 0.0 collective-permute-done.10.refs_4_
  89.7 0.2 collective-permute-done.11.refs_5_
  89.9 0.7 collective-permute-done.12.refs_6_
  90.6 0.2 collective-permute-done.13.refs_7_
  90.8 6.6 %all-to-all-done.1.pieces = bf16[8,256,128]{2,1,0:T(8,128)(2,1)S(1)} async-done(((bf16[8,256,128]{2,1,0:T(8,128)(2,1)}), bf16[8,256,128]{2,1,0:T(8,128)(2,1)S(1)}, u32[]{:S(2)}, u32[]{:S(2)}) %all-to-all-start.1) | async-done | bytes 524320 | tf_op jit(solution)/shard_map/all_to_all | solution.py:321
  97.4 0.0 copy-done.13
  97.5 0.0 copy-done.15
  97.5 0.8 copy-done.3
  98.2 4.4 %finish.1 = (bf16[256,1024]{1,0:T(8,128)(2,1)}, f32[18,1,256]{2,1,0:T(1,128)}, f32[1,18]{1,0:T(1,128)}) custom-call(bf16[8,256,128]{2,1,0:T(8,128)(2,1)} %copy-done.3, bf16[1024,128]{1,0:T(8,128)(2,1)} %copy-done.4, bf16[1024,128]{1,0:T(8,128)(2,1)} %copy-done.8, bf16[1024,128]{1,0:T(8,128)(2,1)} %copy-done.10, ...), custom_call_target="tpu_custom_call" | custom-call | tf_op jit(solution)/shard_map/finish/pallas_call | solution.py:262
  102.6 1.0 collective-permute-start.14
  103.6 1.0 collective-permute-done.14
  104.5 0.7 add_bitcast_fusion
  105.2 24.8 %all_to_all.15 = f32[128,1,18]{2,1,0:T(1,128)S(1)} all-to-all(f32[128,1,18]{2,1,0:T(1,128)S(1)} %broadcast_in_dim.29), channel_id=1, replica_groups=mesh['dp_0'=8,'dp_1'=4,'seq_0'=4,'seq_1'=2] {'dp_0','dp_1','seq_0'}, dimensions={0} | all-to-all | bytes 18432 | tf_op jit(solution)/shard_map/all_to_all | solution.py:40
  130.1 0.2 reduce_sum.9
  130.2 0.5 fusion.3
  130.8 1.4 %subtract_bitcast_fusion = f32[1,18,256]{2,0,1:T(1,128)} fusion(f32[18,1,256]{2,1,0:T(1,128)} %get-tuple-element.19, f32[18]{0:T(128)S(1)} %get-tuple-element.25), kind=kLoop, calls=%fused_computation.4 | loop fusion | flops 4608 | bytes 36936 | tf_op jit(solution)/shard_map/transpose | solution.py:333
  (21 shorter events, 0.1 us)
Async XLA Ops:
  2.5 12.0 %copy-start.16 = (s32[1,256]{1,0:T(1,128)S(1)}, s32[1,256]{1,0:T(1,128)}, u32[]{:S(2)}) copy-start(s32[1,256]{1,0:T(1,128)} %param.9) | copy-start | bytes 3076
  2.5 12.0 %copy-start.2 = (bf16[1,256,1024]{2,1,0:T(8,128)(2,1)S(1)}, bf16[1,256,1024]{2,1,0:T(8,128)(2,1)}, u32[]{:S(2)}) copy-start(bf16[1,256,1024]{2,1,0:T(8,128)(2,1)} %param.8) | copy-start | bytes 1572868
  2.5 43.2 %all-to-all-start = ((bf16[32,32,512]{2,1,0:T(8,128)(2,1)}), bf16[32,32,512]{2,1,0:T(8,128)(2,1)S(1)}, u32[]{:S(2)}, u32[]{:S(2)}) async-start(bf16[32,32,512]{2,1,0:T(8,128)(2,1)} %broadcast_in_dim.24), calls=%async_computation | async-start | bytes 2097152 | tf_op jit(solution)/shard_map/all_to_all | solution.py:40
  14.6 33.5 %copy-start.1 = (bf16[272,1024]{1,0:T(8,128)(2,1)}, bf16[272,1024]{1,0:T(8,128)(2,1)S(1)}, u32[]{:S(2)}) copy-start(bf16[272,1024]{1,0:T(8,128)(2,1)S(1)} %fusion.1.refs_0_) | copy-start | bytes 1671172
  14.6 14.8 %collective-permute-start = (bf16[272,1024]{1,0:T(8,128)(2,1)S(1)}, bf16[272,1024]{1,0:T(8,128)(2,1)S(1)}, u32[]{:S(2)}, u32[]{:S(2)}) collective-permute-start(bf16[272,1024]{1,0:T(8,128)(2,1)S(1)} %fusion.1.refs_0_), channel_id=1, source_target_pairs={{0,6},{2,0},{4,2},{6,4},{1,7},{3,1},{5,3},{7,5},{8,14},{10,8},{12,... | collective-permute-start | bytes 1671176 | tf_op jit(solution)/shard_map/ppermute | solution.py:296
  17.4 24.8 %collective-permute-start.1 = (bf16[272,1024]{1,0:T(8,128)(2,1)S(1)}, bf16[272,1024]{1,0:T(8,128)(2,1)S(1)}, u32[]{:S(2)}, u32[]{:S(2)}) collective-permute-start(bf16[272,1024]{1,0:T(8,128)(2,1)S(1)} %fusion.1.refs_0_), channel_id=1, source_target_pairs={{0,2},{2,4},{4,6},{6,0},{1,3},{3,5},{5,7},{7,1},{8,10},{10,12},{12... | collective-permute-start | bytes 1671176 | tf_op jit(solution)/shard_map/ppermute | solution.py:296
  17.4 28.2 %collective-permute-start.2 = (bf16[272,1024]{1,0:T(8,128)(2,1)S(1)}, bf16[272,1024]{1,0:T(8,128)(2,1)S(1)}, u32[]{:S(2)}, u32[]{:S(2)}) collective-permute-start(bf16[272,1024]{1,0:T(8,128)(2,1)S(1)} %fusion.1.refs_0_), channel_id=1, source_target_pairs={{0,4},{2,6},{4,0},{6,2},{1,5},{3,7},{5,1},{7,3},{8,12},{10,14},{12... | collective-permute-start | bytes 1671176 | tf_op jit(solution)/shard_map/ppermute | solution.py:296
  19.1 27.2 %collective-permute-start.6 = (bf16[272,1024]{1,0:T(8,128)(2,1)S(1)}, bf16[272,1024]{1,0:T(8,128)(2,1)}, u32[]{:S(2)}, u32[]{:S(2)}) collective-permute-start(bf16[272,1024]{1,0:T(8,128)(2,1)S(1)} %fusion.1.refs_0_), channel_id=1, source_target_pairs={{0,1},{1,0},{2,3},{3,2},{4,5},{5,4},{6,7},{7,6},{8,9},{9,8},{10,11... | collective-permute-start | bytes 1671176 | tf_op jit(solution)/shard_map/ppermute | solution.py:299
  29.4 18.7 %copy-start.5 = (bf16[272,1024]{1,0:T(8,128)(2,1)}, bf16[272,1024]{1,0:T(8,128)(2,1)S(1)}, u32[]{:S(2)}) copy-start(bf16[272,1024]{1,0:T(8,128)(2,1)S(1)} %collective-permute-done.refs_2_) | copy-start | bytes 1671172
  29.4 16.9 %collective-permute-start.7 = (bf16[272,1024]{1,0:T(8,128)(2,1)S(1)}, bf16[272,1024]{1,0:T(8,128)(2,1)}, u32[]{:S(2)}, u32[]{:S(2)}) collective-permute-start(bf16[272,1024]{1,0:T(8,128)(2,1)S(1)} %collective-permute-done.refs_2_), channel_id=1, source_target_pairs={{0,1},{1,0},{2,3},{3,2},{4,5},{5,4},{6,7},{7,6},{8,9},{9,8},{10,11... | collective-permute-start | bytes 1671176 | tf_op jit(solution)/shard_map/ppermute | solution.py:299
  42.2 5.9 %copy-start.6 = (bf16[272,1024]{1,0:T(8,128)(2,1)}, bf16[272,1024]{1,0:T(8,128)(2,1)S(1)}, u32[]{:S(2)}) copy-start(bf16[272,1024]{1,0:T(8,128)(2,1)S(1)} %collective-permute-done.1.refs_4_) | copy-start | bytes 1671172
  42.2 5.2 %collective-permute-start.8 = (bf16[272,1024]{1,0:T(8,128)(2,1)S(1)}, bf16[272,1024]{1,0:T(8,128)(2,1)}, u32[]{:S(2)}, u32[]{:S(2)}) collective-permute-start(bf16[272,1024]{1,0:T(8,128)(2,1)S(1)} %collective-permute-done.1.refs_4_), channel_id=1, source_target_pairs={{0,1},{1,0},{2,3},{3,2},{4,5},{5,4},{6,7},{7,6},{8,9},{9,8},{10,11... | collective-permute-start | bytes 1671176 | tf_op jit(solution)/shard_map/ppermute | solution.py:299
  45.6 2.5 %copy-start.7 = (bf16[272,1024]{1,0:T(8,128)(2,1)}, bf16[272,1024]{1,0:T(8,128)(2,1)S(1)}, u32[]{:S(2)}) copy-start(bf16[272,1024]{1,0:T(8,128)(2,1)S(1)} %collective-permute-done.2.refs_6_) | copy-start | bytes 1671172
  45.6 2.5 %collective-permute-start.9 = (bf16[272,1024]{1,0:T(8,128)(2,1)S(1)}, bf16[272,1024]{1,0:T(8,128)(2,1)}, u32[]{:S(2)}, u32[]{:S(2)}) collective-permute-start(bf16[272,1024]{1,0:T(8,128)(2,1)S(1)} %collective-permute-done.2.refs_6_), channel_id=1, source_target_pairs={{0,1},{1,0},{2,3},{3,2},{4,5},{5,4},{6,7},{7,6},{8,9},{9,8},{10,11... | collective-permute-start | bytes 1671176 | tf_op jit(solution)/shard_map/ppermute | solution.py:299
  45.7 2.4 %copy-start = (bf16[32,32,512]{2,1,0:T(8,128)(2,1)}, bf16[32,32,512]{2,1,0:T(8,128)(2,1)S(1)}, u32[]{:S(2)}) copy-start(bf16[32,32,512]{2,1,0:T(8,128)(2,1)S(1)} %all-to-all-done) | copy-start | bytes 3145732
  45.7 42.2 %copy-start.4 = (bf16[1024,128]{1,0:T(8,128)(2,1)}, bf16[1024,128]{1,0:T(8,128)(2,1)S(1)}, u32[]{:S(2)}) copy-start(bf16[1024,128]{1,0:T(8,128)(2,1)S(1)} %slice.4.refs_0_) | copy-start | bytes 786436
  45.8 35.1 %collective-permute-start.3 = (bf16[1024,128]{1,0:T(8,128)(2,1)S(1)}, bf16[1024,128]{1,0:T(8,128)(2,1)S(1)}, u32[]{:S(2)}, u32[]{:S(2)}) collective-permute-start(bf16[1024,128]{1,0:T(8,128)(2,1)S(1)} %slice.4.refs_0_), channel_id=1, source_target_pairs={{0,6},{2,0},{4,2},{6,4},{1,7},{3,1},{5,3},{7,5},{8,14},{10,8},{12,... | collective-permute-start | bytes 786440 | tf_op jit(solution)/shard_map/ppermute | solution.py:296
  46.3 34.6 %collective-permute-start.4 = (bf16[1024,128]{1,0:T(8,128)(2,1)S(1)}, bf16[1024,128]{1,0:T(8,128)(2,1)S(1)}, u32[]{:S(2)}, u32[]{:S(2)}) collective-permute-start(bf16[1024,128]{1,0:T(8,128)(2,1)S(1)} %slice.4.refs_0_), channel_id=1, source_target_pairs={{0,4},{2,6},{4,0},{6,2},{1,5},{3,7},{5,1},{7,3},{8,12},{10,14},{12... | collective-permute-start | bytes 786440 | tf_op jit(solution)/shard_map/ppermute | solution.py:296
  46.3 36.0 %collective-permute-start.5 = (bf16[1024,128]{1,0:T(8,128)(2,1)S(1)}, bf16[1024,128]{1,0:T(8,128)(2,1)}, u32[]{:S(2)}, u32[]{:S(2)}) collective-permute-start(bf16[1024,128]{1,0:T(8,128)(2,1)S(1)} %slice.4.refs_0_), channel_id=1, source_target_pairs={{0,2},{2,4},{4,6},{6,0},{1,3},{3,5},{5,7},{7,1},{8,10},{10,12},{12... | collective-permute-start | bytes 786440 | tf_op jit(solution)/shard_map/ppermute | solution.py:296
  80.8 8.2 %copy-start.17 = (f32[18]{0:T(128)S(1)}, f32[18]{0:T(128)}, u32[]{:S(2)}) copy-start(f32[18]{0:T(128)} %param.15) | copy-start | bytes 220
  80.8 0.7 copy-start.8
  81.5 0.7 copy-start.10
  82.2 5.8 %copy-start.9 = (bf16[1024,128]{1,0:T(8,128)(2,1)S(1)}, bf16[1024,128]{1,0:T(8,128)(2,1)}, u32[]{:S(2)}) copy-start(bf16[1024,128]{1,0:T(8,128)(2,1)} %copy-done.8) | copy-start | bytes 786436
  82.2 6.2 %copy-start.11 = (bf16[1024,128]{1,0:T(8,128)(2,1)S(1)}, bf16[1024,128]{1,0:T(8,128)(2,1)}, u32[]{:S(2)}) copy-start(bf16[1024,128]{1,0:T(8,128)(2,1)} %copy-done.10) | copy-start | bytes 786436
  82.2 15.2 %all-to-all-start.1 = ((bf16[8,256,128]{2,1,0:T(8,128)(2,1)}), bf16[8,256,128]{2,1,0:T(8,128)(2,1)S(1)}, u32[]{:S(2)}, u32[]{:S(2)}) async-start(bf16[8,256,128]{2,1,0:T(8,128)(2,1)} %layer.1), calls=%async_computation.1 | async-start | bytes 1048576 | tf_op jit(solution)/shard_map/all_to_all | solution.py:321
  88.0 1.7 %collective-permute-start.10 = (bf16[1024,128]{1,0:T(8,128)(2,1)S(1)}, bf16[1024,128]{1,0:T(8,128)(2,1)S(1)}, u32[]{:S(2)}, u32[]{:S(2)}) collective-permute-start(bf16[1024,128]{1,0:T(8,128)(2,1)S(1)} %slice.4.refs_0_), channel_id=1, source_target_pairs={{0,1},{1,0},{2,3},{3,2},{4,5},{5,4},{6,7},{7,6},{8,9},{9,8},{10,11... | collective-permute-start | bytes 786440 | tf_op jit(solution)/shard_map/ppermute | solution.py:299
  88.1 1.8 %collective-permute-start.11 = (bf16[1024,128]{1,0:T(8,128)(2,1)S(1)}, bf16[1024,128]{1,0:T(8,128)(2,1)S(1)}, u32[]{:S(2)}, u32[]{:S(2)}) collective-permute-start(bf16[1024,128]{1,0:T(8,128)(2,1)S(1)} %copy-done.9), channel_id=1, source_target_pairs={{0,1},{1,0},{2,3},{3,2},{4,5},{5,4},{6,7},{7,6},{8,9},{9,8},{10,11... | collective-permute-start | bytes 786440 | tf_op jit(solution)/shard_map/ppermute | solution.py:299
  88.5 2.1 %collective-permute-start.12 = (bf16[1024,128]{1,0:T(8,128)(2,1)S(1)}, bf16[1024,128]{1,0:T(8,128)(2,1)S(1)}, u32[]{:S(2)}, u32[]{:S(2)}) collective-permute-start(bf16[1024,128]{1,0:T(8,128)(2,1)S(1)} %copy-done.11), channel_id=1, source_target_pairs={{0,1},{1,0},{2,3},{3,2},{4,5},{5,4},{6,7},{7,6},{8,9},{9,8},{10,11... | collective-permute-start | bytes 786440 | tf_op jit(solution)/shard_map/ppermute | solution.py:299
  88.6 2.3 %collective-permute-start.13 = (bf16[1024,128]{1,0:T(8,128)(2,1)}, bf16[1024,128]{1,0:T(8,128)(2,1)S(1)}, u32[]{:S(2)}, u32[]{:S(2)}) collective-permute-start(bf16[1024,128]{1,0:T(8,128)(2,1)} %collective-permute-done.5.refs_3_), channel_id=1, source_target_pairs={{0,1},{1,0},{2,3},{3,2},{4,5},{5,4},{6,7},{7,6},{8,9},{9,8},{10,11... | collective-permute-start | bytes 786440 | tf_op jit(solution)/shard_map/ppermute | solution.py:299
  89.7 7.8 %copy-start.12 = (bf16[1024,128]{1,0:T(8,128)(2,1)}, bf16[1024,128]{1,0:T(8,128)(2,1)S(1)}, u32[]{:S(2)}) copy-start(bf16[1024,128]{1,0:T(8,128)(2,1)S(1)} %collective-permute-done.10.refs_4_) | copy-start | bytes 786436
  89.9 7.6 %copy-start.13 = (bf16[1024,128]{1,0:T(8,128)(2,1)}, bf16[1024,128]{1,0:T(8,128)(2,1)S(1)}, u32[]{:S(2)}) copy-start(bf16[1024,128]{1,0:T(8,128)(2,1)S(1)} %collective-permute-done.11.refs_5_) | copy-start | bytes 786436
  90.6 6.8 %copy-start.14 = (bf16[1024,128]{1,0:T(8,128)(2,1)}, bf16[1024,128]{1,0:T(8,128)(2,1)S(1)}, u32[]{:S(2)}) copy-start(bf16[1024,128]{1,0:T(8,128)(2,1)S(1)} %collective-permute-done.12.refs_6_) | copy-start | bytes 786436
  90.8 6.6 %copy-start.15 = (bf16[1024,128]{1,0:T(8,128)(2,1)}, bf16[1024,128]{1,0:T(8,128)(2,1)S(1)}, u32[]{:S(2)}) copy-start(bf16[1024,128]{1,0:T(8,128)(2,1)S(1)} %collective-permute-done.13.refs_7_) | copy-start | bytes 786436
  97.4 0.8 copy-start.3
  102.6 1.9 %collective-permute-start.14 = (f32[1,18]{1,0:T(1,128)}, f32[1,18]{1,0:T(1,128)S(1)}, u32[]{:S(2)}, u32[]{:S(2)}) collective-permute-start(f32[1,18]{1,0:T(1,128)} %get-tuple-element.20), channel_id=1, source_target_pairs={{0,1},{1,0},{2,3},{3,2},{4,5},{5,4},{6,7},{7,6},{8,9},{9,8},{10,11... | collective-permute-start | bytes 224 | tf_op jit(solution)/shard_map/ppermute | solution.py:299

commit v3 on v2

--- a/solution.py
+++ b/solution.py
@@ -18,7 +18,7 @@
 KEYS = 512
 ROWS = 256
 SAFE = 8.0
-LIMIT = 60 * 1024 * 1024
+LIMIT = 28 * 1024 * 1024
 F32 = jnp.float32
 BF16 = jnp.bfloat16
 
@@ -33,6 +33,10 @@
 
 def smem():
     return pl.BlockSpec(memory_space=pltpu.SMEM)
+
+
+def in_vmem(tree):
+    return jax.tree.map(lambda x: pltpu.with_memory_space_constraint(x, pltpu.VMEM), tree)
 
 
 def copy_for_each(x, axis):
@@ -40,42 +44,32 @@
     return lax.all_to_all(jnp.broadcast_to(x[None], (length, *x.shape)), axis, 0, 0, tiled=True)
 
 
-def any_space():
-    return pl.BlockSpec(memory_space=pl.ANY)
-
-
 def layer_kernel(scales, gain, *refs):
     pieces, shards, out = refs[:8], refs[8], refs[9]
-    held, weights, normed, labels, queries, keys, values, total, even, odd, table, sems = refs[10:]
+    weights, normed, labels, queries, keys, values, total, even, odd, table = refs[10:]
     core, chip = lax.axis_index("seq_1"), lax.axis_index("seq_0")
     first = (2 * chip + core) * 2
     scale = [scales[first] / math.sqrt(64), scales[first + 1] / math.sqrt(64)]
     rows = ROWS
-    arrivals = [
-        pltpu.make_async_copy(pieces[i], held.at[i // 2, i % 2], sems.at[i]) for i in range(8)
-    ]
-    matrix = pltpu.make_async_copy(shards.at[:, pl.ds(0, 384)], weights, sems.at[8])
-    matrix.start()
-    for copy in arrivals:
-        copy.start()
-    matrix.wait()
+    for i in range(4):
+        weights[:, i] = shards[i]
     head = 64
+    matrix = weights[...].reshape(normed.shape[1], 384)
     lane = lax.broadcasted_iota(jnp.int32, (rows, 128), 1)
     spot = lax.broadcasted_iota(jnp.int32, (head, rows), 0)
     for pair in range(4):
         step = (0, 1, 3, 2)[pair]
         for side in range(2):
-            arrivals[2 * pair + side].wait()
-            wide = held[pair, side, 0:rows].astype(F32)
+            wide = pieces[2 * pair + side][0:rows].astype(F32)
             inv = lax.rsqrt(jnp.mean(wide * wide, axis=-1, keepdims=True) + EPS)
             normed[side * rows : (side + 1) * rows] = (wide * inv * gain[...]).astype(BF16)
-        both = jnp.dot(normed[...], weights[...], preferred_element_type=F32).astype(BF16).astype(F32)
+        both = jnp.dot(normed[...], matrix, preferred_element_type=F32).astype(BF16).astype(F32)
         for side in range(2):
             part = core if side == 0 else 1 - core
             block = 2 * lax.rem(chip + step, 4) + part
             start = pl.multiple_of(block * rows, rows)
             joined = both[side * rows : (side + 1) * rows]
-            ids = held[pair, side, rows : rows + 8, 0:rows].astype(F32)[0:1].astype(jnp.int32)
+            ids = pieces[2 * pair + side][rows : rows + 8, 0:rows].astype(F32)[0:1].astype(jnp.int32)
             labels[pl.ds(block, 1), :] = ids
             same = spot == ids
             bars = jnp.where(same, 0.0, EXCLUDED).astype(F32)
@@ -204,12 +198,11 @@
     total = 8 * ROWS
     return pl.pallas_call(
         layer_kernel,
-        in_specs=[smem(), vmem()] + [any_space()] * 9,
+        in_specs=[smem()] + [vmem()] * 10,
         out_specs=vmem(),
         out_shape=jax.ShapeDtypeStruct((8, ROWS, 128), BF16),
         scratch_shapes=[
-            pltpu.VMEM((4, 2, *pieces[0].shape), BF16),
-            pltpu.VMEM((shard.shape[0], 384), BF16),
+            pltpu.VMEM((8, 4, 32, 384), BF16),
             pltpu.VMEM((2 * ROWS, pieces[0].shape[1]), BF16),
             pltpu.VMEM((8, ROWS), jnp.int32),
             pltpu.VMEM((2, total + ROWS, 128), BF16),
@@ -219,7 +212,6 @@
             pltpu.VMEM((2, ROWS, KEYS), F32),
             pltpu.VMEM((2, ROWS, KEYS), F32),
             pltpu.SMEM((2, 48), jnp.int32),
-            pltpu.SemaphoreType.DMA((9,)),
         ],
         compiler_params=params(),
         name="layer",
@@ -227,26 +219,25 @@
 
 
 def finish_kernel(pieces, *refs):
-    shards, (rows, bits, offset, mixed, probs, sums, weights, joined, sems) = refs[:8], refs[8:]
-    core, chip = lax.axis_index("seq_1"), lax.axis_index("seq_0")
-    copies = []
+    shards, (rows, bits, offset, mixed, probs, sums, weights, joined) = refs[:8], refs[8:]
+    core, across = lax.axis_index("seq_1"), lax.axis_index("dp_1")
     for i in range(8):
-        block = 2 * lax.rem(chip + i % 4, 4) + (core if i < 4 else 1 - core)
-        columns = pl.ds(pl.multiple_of(block * 128, 128), 128)
-        copies.append(pltpu.make_async_copy(shards[i], weights.at[:, columns], sems.at[i]))
-        copies[i].start()
+        part = core if i < 4 else 1 - core
+        place = lax.rem(across + (0, 2, 1, 3)[i % 4], 4)
+        weights[part, :, place] = shards[i][...]
     for source in range(8):
         joined[:, source * 128 : (source + 1) * 128] = pieces[source]
-    for copy in copies:
-        copy.wait()
-    moved = jnp.dot(joined[...], weights[...], preferred_element_type=F32)
-    mixed[...] = (rows[...].astype(F32) + moved).astype(BF16)
+    for part in range(2):
+        columns = slice(part * 512, part * 512 + 512)
+        moved = jnp.dot(
+            joined[...], weights[part].reshape(1024, 512), preferred_element_type=F32
+        )
+        mixed[:, columns] = (rows[:, columns].astype(F32) + moved).astype(BF16)
     logits = lax.dot_general(
         bits[...], mixed[...], (((1,), (1,)), ((), ())), preferred_element_type=F32
     )
     chance = jax.nn.sigmoid(4.0 * (logits + offset[...]))
-    for b in range(chance.shape[0]):
-        probs[b] = chance[b : b + 1]
+    probs[...] = chance
     row = lax.dot_general(
         jnp.ones((8, chance.shape[1]), F32),
         chance,
@@ -261,17 +252,16 @@
     count = rows.shape[0]
     return pl.pallas_call(
         finish_kernel,
-        in_specs=[vmem()] + [any_space()] * 8 + [vmem()] * 3,
+        in_specs=[vmem()] * 12,
         out_specs=[vmem()] * 3,
         out_shape=[
             jax.ShapeDtypeStruct(rows.shape, BF16),
-            jax.ShapeDtypeStruct((bits.shape[0], 1, count), F32),
+            jax.ShapeDtypeStruct((bits.shape[0], count), F32),
             jax.ShapeDtypeStruct((1, bits.shape[0]), F32),
         ],
         scratch_shapes=[
-            pltpu.VMEM((1024, 1024), BF16),
+            pltpu.VMEM((2, 8, 4, 32, 512), BF16),
             pltpu.VMEM((count, 1024), BF16),
-            pltpu.SemaphoreType.DMA((8,)),
         ],
         compiler_params=params(),
         name="finish",
@@ -290,6 +280,7 @@
 ):
     rows = residual_tiles[0]
     count, width = rows.shape
+    core = lax.axis_index("seq_1")
     member = lax.axis_index(SEQ)
     def from_step(x, k, axis="seq_0"):
         length = lax.axis_size(axis)
@@ -308,29 +299,32 @@
             lax.dynamic_slice_in_dim(triple_projector, member * 128 + 1024 * i, 128, 1)
             for i in range(3)
         ]
-        + [lax.dynamic_slice_in_dim(final_projector, member * 128, 128, 1)],
+        + [lax.dynamic_slice_in_dim(final_projector, core * 512, 512, 1)],
         axis=1,
     )
-    shard = copy_for_each(owned, DP).reshape(width, 512)
-    mixing, _ = lax.optimization_barrier((shard[:, 384:], near))
-    mixings = [mixing] + [from_step(mixing, k) for k in (1, 2, 3)]
-
+    owned = copy_for_each(owned, "dp_0")
+    shard, mixing = owned[:, :, :384], owned[:, :, 384:]
+    shard = copy_for_each(shard, "dp_1")
+    mixing, _ = lax.optimization_barrier((mixing, shard))
+    mixings = [mixing] + [from_step(mixing, k, "dp_1") for k in (2, 1, 3)]
+
+    pieces, shard = in_vmem((pieces, shard))
     attended = layer(logit_scaling, prenorm_multiplier[None], pieces, shard)
     mixings, attended = lax.optimization_barrier((mixings, attended))
-    mixings = mixings + [from_other_core(m) for m in mixings]
+    mixings = in_vmem(mixings)
+    mixings = in_vmem(mixings + [from_other_core(m) for m in mixings])
     attended = lax.all_to_all(attended, SEQ, 0, 0, tiled=True)
     mixed, probs, sums = finish(
-        attended,
+        in_vmem(attended),
         mixings,
         rows,
         binarizer_projector.T,
         binarizer_offset[:, None],
     )
-    sums = sums + from_other_core(sums)
-    sums = copy_for_each(sums, ("dp_0", "dp_1", "seq_0"))
-    marginal = jnp.sum(sums, axis=(0, 1)) / (count * lax.axis_size(ALL))
+    sums = jnp.sum(copy_for_each(sums, ("dp_0", "dp_1", "seq_0")), axis=(0, 1))
+    marginal = (sums + from_other_core(sums)) / (count * lax.axis_size(ALL))
     code_entropy = -(marginal * jnp.log(marginal) + (1.0 - marginal) * jnp.log(1.0 - marginal))
-    bit_codes = jnp.swapaxes(probs - marginal[:, None, None], 0, 1)
+    bit_codes = (probs - marginal[:, None])[None]
     return (mixed[None], bit_codes, code_entropy)
 
 

time: 131 us -> 125 us (0.954); the launches traced: 132 us -> 123 us
  blocking collectives: 24.8 us -> 18.6 us
  starting transfers between devices: 43.9 us -> 37.7 us
  waiting for transfers between devices: 18 us -> 22.9 us
  local copies, waits for them, and re-layouts: 4.82 us -> 7.28 us
  Pallas kernels: 37.1 us -> 34.9 us
  other arithmetic: 2.8 us -> 0.8 us
    all_to_all x1 -> x2, waiting for transfers between devices: 0.01 us -> 13.7 us  [copy_for_each(): lax.all_to_all(jnp.broadcast_to(x[None], (length, *x.shape)), axis, 0, 0,...]
    ppermute x6, waiting for transfers between devices: 8.57 us -> 0.02 us  [from_step(): return lax.ppermute(x, axis, [(i, (i - k) % length) for i in range(length)])]
    ppermute x9, starting transfers between devices: 20 us -> 12.1 us  [from_other_core(): return lax.ppermute(x, 'seq_1', [(0, 1), (1, 0)])]
    all_to_all x1, blocking collectives: 24.8 us -> 18.6 us  [copy_for_each(): lax.all_to_all(jnp.broadcast_to(x[None], (length, *x.shape)), axis, 0, 0,...]
    pallas_call x2, Pallas kernels: 37.1 us -> 34.9 us  [the longest x1 32.2 us: layer(): pl.pallas_call(layer_kernel, in_specs=[smem()] + [vmem()] * 10, out_specs...]
    unnamed x36 -> x25, local copies, waits for them, and re-layouts: 2.2 us -> 3.63 us
    transpose x1 -> x0, other arithmetic: 1.41 us -> none  [on_device(): bit_codes = jnp.swapaxes(probs - marginal[:, None, None], 0, 1)]
    all_to_all x1 -> x2, starting transfers between devices: 12 us -> 13.2 us  [copy_for_each(): lax.all_to_all(jnp.broadcast_to(x[None], (length, *x.shape)), axis, 0, 0,...]
  transfers between devices with their start and end apart: 17 -> 18, of which waited for: 7 -> 8; matrix products, arithmetic and copies ran while one was open for 1% -> 2% of each run, Pallas kernels for 25% -> 26%
where the time goes in v3:
time: 125 us; the launch traced here: 123 us
  starting transfers between devices  37.7 us (30%)
  Pallas kernels  34.9 us (28%)
  waiting for transfers between devices  22.9 us (18%)
  blocking collectives  18.6 us (15%)
  local copies, waits for them, and re-layouts  7.28 us (6%)
    pallas_call x1, Pallas kernels, layer(): pl.pallas_call(layer_kernel, in_specs=[smem()] + [vmem()] * 10, out_specs...  32.2 us
    all_to_all x1, blocking collectives, copy_for_each(): lax.all_to_all(jnp.broadcast_to(x[None], (length, *x.shape)), axis, 0, 0,...  18.6 us
    all_to_all x2, waiting for transfers between devices, copy_for_each(): lax.all_to_all(jnp.broadcast_to(x[None], (length, *x.shape)), axis, 0, 0,...  13.7 us
    all_to_all x2, starting transfers between devices, copy_for_each(): lax.all_to_all(jnp.broadcast_to(x[None], (length, *x.shape)), axis, 0, 0,...  13.2 us
    ppermute x9, starting transfers between devices, from_other_core(): return lax.ppermute(x, 'seq_1', [(0, 1), (1, 0)])  12.1 us
    ppermute x6, starting transfers between devices, from_step(): return lax.ppermute(x, axis, [(i, (i - k) % length) for i in range(length)])  7.14 us
    all_to_all x1, waiting for transfers between devices, on_device(): attended = lax.all_to_all(attended, SEQ, 0, 0, tiled=True)  6.61 us
    all_to_all x1, starting transfers between devices, on_device(): attended = lax.all_to_all(attended, SEQ, 0, 0, tiled=True)  5.3 us
  transfers between devices with their start and end apart: 18, of which 8 were waited for; matrix products, arithmetic and copies ran while one was open for 2% of the time, Pallas kernels for 26%

profile of v3, /device:TPU:1, one launch (start us, length us, event | category | flops | bytes accessed | tf_op | source)
XLA Modules:
  0.0 122.9 jit_solution(11693334389344550006)
XLA Ops:
  0.6 0.0 copy-start
  0.7 0.8 copy-done
  1.5 0.7 constant_dynamic-slice_fusion.3
  2.2 0.0 copy-start.10
  2.2 0.0 copy-start.1
  2.2 0.8 broadcast_in_dim.16
  3.0 9.0 %all-to-all-start = ((bf16[8,32,896]{2,1,0:T(8,128)(2,1)}), bf16[8,32,896]{2,1,0:T(8,128)(2,1)S(1)}, u32[]{:S(2)}, u32[]{:S(2)}) async-start(bf16[8,32,896]{2,1,0:T(8,128)(2,1)} %broadcast_in_dim.16), calls=%async_computation | async-start | bytes 917504 | tf_op jit(solution)/shard_map/all_to_all | solution.py:44
  12.0 0.0 copy-done.10
  12.1 0.0 copy-done.1
  12.1 2.8 %collective-permute-start.4 = (bf16[272,1024]{1,0:T(8,128)(2,1)S(1)}, bf16[272,1024]{1,0:T(8,128)(2,1)S(1)}, u32[]{:S(2)}, u32[]{:S(2)}) collective-permute-start(bf16[272,1024]{1,0:T(8,128)(2,1)S(1)} %fusion.1.refs_0_), channel_id=1, source_target_pairs={{0,6},{2,0},{4,2},{6,4},{1,7},{3,1},{5,3},{7,5},{8,14},{10,8},{12,... | collective-permute-start | bytes 1671176 | tf_op jit(solution)/shard_map/ppermute | solution.py:287
  14.9 0.0 collective-permute-start.6
  14.9 1.6 %collective-permute-start.8 = (bf16[272,1024]{1,0:T(8,128)(2,1)S(1)}, bf16[272,1024]{1,0:T(8,128)(2,1)}, u32[]{:S(2)}, u32[]{:S(2)}) collective-permute-start(bf16[272,1024]{1,0:T(8,128)(2,1)S(1)} %fusion.1.refs_0_), channel_id=1, source_target_pairs={{0,4},{2,6},{4,0},{6,2},{1,5},{3,7},{5,1},{7,3},{8,12},{10,14},{12... | collective-permute-start | bytes 1671176 | tf_op jit(solution)/shard_map/ppermute | solution.py:287
  16.6 11.9 %all-to-all-done = bf16[8,32,896]{2,1,0:T(8,128)(2,1)S(1)} async-done(((bf16[8,32,896]{2,1,0:T(8,128)(2,1)}), bf16[8,32,896]{2,1,0:T(8,128)(2,1)S(1)}, u32[]{:S(2)}, u32[]{:S(2)}) %all-to-all-start) | async-done | bytes 458784 | tf_op jit(solution)/shard_map/all_to_all | solution.py:44
  28.5 0.7 copy-done.9
  29.3 1.0 broadcast_in_dim.34
  30.3 4.1 %all-to-all-start.1 = ((bf16[4,8,32,384]{3,2,1,0:T(8,128)(2,1)}), bf16[4,8,32,384]{3,2,1,0:T(8,128)(2,1)S(1)}, u32[]{:S(2)}, u32[]{:S(2)}) async-start(bf16[4,8,32,384]{3,2,1,0:T(8,128)(2,1)} %broadcast_in_dim.34), calls=%async_computation.1 | async-start | bytes 1572864 | tf_op jit(solution)/shard_map/all_to_all | solution.py:44
  34.4 0.9 collective-permute-start.3
  35.3 0.0 collective-permute-done.4.refs_2_
  35.3 4.4 %collective-permute-start.5 = (bf16[272,1024]{1,0:T(8,128)(2,1)S(1)}, bf16[272,1024]{1,0:T(8,128)(2,1)}, u32[]{:S(2)}, u32[]{:S(2)}) collective-permute-start(bf16[272,1024]{1,0:T(8,128)(2,1)S(1)} %collective-permute-done.4.refs_2_), channel_id=1, source_target_pairs={{0,1},{1,0},{2,3},{3,2},{4,5},{5,4},{6,7},{7,6},{8,9},{9,8},{10,11... | collective-permute-start | bytes 1671176 | tf_op jit(solution)/shard_map/ppermute | solution.py:290
  39.7 0.0 collective-permute-done.6.refs_4_
  39.7 3.4 %collective-permute-start.7 = (bf16[272,1024]{1,0:T(8,128)(2,1)S(1)}, bf16[272,1024]{1,0:T(8,128)(2,1)}, u32[]{:S(2)}, u32[]{:S(2)}) collective-permute-start(bf16[272,1024]{1,0:T(8,128)(2,1)S(1)} %collective-permute-done.6.refs_4_), channel_id=1, source_target_pairs={{0,1},{1,0},{2,3},{3,2},{4,5},{5,4},{6,7},{7,6},{8,9},{9,8},{10,11... | collective-permute-start | bytes 1671176 | tf_op jit(solution)/shard_map/ppermute | solution.py:290
  43.1 0.0 collective-permute-done.8.refs_6_
  43.1 0.0 collective-permute-start.9
  43.1 1.0 slice.8.refs_0_
  44.1 1.8 %all-to-all-done.1.refs_8_ = bf16[4,8,32,384]{3,2,1,0:T(8,128)(2,1)S(1)} async-done(((bf16[4,8,32,384]{3,2,1,0:T(8,128)(2,1)}), bf16[4,8,32,384]{3,2,1,0:T(8,128)(2,1)S(1)}, u32[]{:S(2)}, u32[]{:S(2)}) %all-to-all-start.1) | async-done | bytes 786464 | tf_op jit(solution)/shard_map/all_to_all | solution.py:44
  45.9 1.1 collective-permute-start
  46.9 0.0 collective-permute-done.3.refs_1_
  46.9 1.6 %collective-permute-start.1 = (bf16[8,32,512]{2,1,0:T(8,128)(2,1)S(1)}, bf16[8,32,512]{2,1,0:T(8,128)(2,1)S(1)}, u32[]{:S(2)}, u32[]{:S(2)}) collective-permute-start(bf16[8,32,512]{2,1,0:T(8,128)(2,1)S(1)} %slice.8.refs_0_), channel_id=1, source_target_pairs={{0,24},{8,0},{16,8},{24,16},{1,25},{9,1},{17,9},{25,17},{2,26},{10... | collective-permute-start | bytes 786440 | tf_op jit(solution)/shard_map/ppermute | solution.py:287
  48.6 0.0 collective-permute-done.5.refs_3_
  48.6 0.0 collective-permute-start.2
  48.6 0.0 collective-permute-done.7.refs_5_
  48.6 0.0 collective-permute-done.9.refs_7_
  48.6 0.0 copy-done.7
  48.6 0.0 copy-done.8
  48.6 32.2 %layer.1 = bf16[8,256,128]{2,1,0:T(8,128)(2,1)} custom-call(f32[16]{0:T(128)S(1)} %copy-done.8, f32[1,1024]{1,0:T(1,128)S(1)} %bitcast.11, bf16[272,1024]{1,0:T(8,128)(2,1)S(1)} %fusion.1.refs_0_, bf16[272,1024]{1,0:T(8,128)(2,1)} %collective-permute-done.3.refs_1_, bf16[272,1024]{1,0:T(8,128)(2,1)S(1)} %collective-permute-done.4.refs_2_, ...), custom_call_target="tpu_custom_call" | custom-call | tf_op jit(solution)/shard_map/layer/pallas_call | solution.py:199
  80.9 0.0 collective-permute-done.refs_1_
  80.9 0.0 copy-start.2
  80.9 0.0 collective-permute-done.1.refs_2_
  80.9 0.7 copy-done.2
  81.6 0.7 copy-done.4
  82.3 0.0 collective-permute-done.2.refs_3_
  82.3 5.3 %all-to-all-start.2 = ((bf16[8,256,128]{2,1,0:T(8,128)(2,1)}), bf16[8,256,128]{2,1,0:T(8,128)(2,1)S(1)}, u32[]{:S(2)}, u32[]{:S(2)}) async-start(bf16[8,256,128]{2,1,0:T(8,128)(2,1)} %layer.1), calls=%async_computation.2 | async-start | bytes 1048576 | tf_op jit(solution)/shard_map/all_to_all | solution.py:316
  87.6 0.0 collective-permute-start.10
  87.6 0.0 copy-done.3
  87.6 0.5 collective-permute-start.11
  88.1 0.0 copy-done.5
  88.1 0.1 collective-permute-start.12
  88.2 0.4 collective-permute-start.13
  88.6 0.0 copy-done.11
  88.6 0.1 copy.18.refs_10_
  88.7 0.4 collective-permute-done.10.refs_4_
  89.1 0.4 collective-permute-done.11.refs_5_
  89.5 0.7 collective-permute-done.12.refs_6_
  90.2 0.2 collective-permute-done.13.refs_7_
  90.5 6.6 %all-to-all-done.2.pieces = bf16[8,256,128]{2,1,0:T(8,128)(2,1)S(1)} async-done(((bf16[8,256,128]{2,1,0:T(8,128)(2,1)}), bf16[8,256,128]{2,1,0:T(8,128)(2,1)S(1)}, u32[]{:S(2)}, u32[]{:S(2)}) %all-to-all-start.2) | async-done | bytes 524320 | tf_op jit(solution)/shard_map/all_to_all | solution.py:316
  97.1 0.0 copy-done.6
  97.1 2.7 %finish.1 = (bf16[256,1024]{1,0:T(8,128)(2,1)}, f32[18,256]{1,0:T(8,128)S(1)}, f32[1,18]{1,0:T(1,128)S(1)}) custom-call(bf16[8,256,128]{2,1,0:T(8,128)(2,1)S(1)} %all-to-all-done.2.pieces, bf16[8,32,512]{2,1,0:T(8,128)(2,1)S(1)} %slice.8.refs_0_, bf16[8,32,512]{2,1,0:T(8,128)(2,1)S(1)} %copy-done.3, bf16[8,32,512]{2,1,0:T(8,128)(2,1)S(1)} %copy-done.5, ...), custom_call_target="tpu_custom_call" | custom-call | tf_op jit(solution)/shard_map/finish/pallas_call | solution.py:253
  99.8 18.6 %all_to_all.20 = f32[128,1,18]{2,1,0:T(1,128)S(1)} all-to-all(f32[128,1,18]{2,1,0:T(1,128)S(1)} %broadcast_in_dim.39), channel_id=1, replica_groups=mesh['dp_0'=8,'dp_1'=4,'seq_0'=4,'seq_1'=2] {'dp_0','dp_1','seq_0'}, dimensions={0} | all-to-all | bytes 18432 | tf_op jit(solution)/shard_map/all_to_all | solution.py:44
  118.4 0.2 reduce_sum.9
  118.5 2.4 %collective-permute-start.14 = (f32[18]{0:T(128)S(1)}, f32[18]{0:T(128)S(1)}, u32[]{:S(2)}, u32[]{:S(2)}) collective-permute-start(f32[18]{0:T(128)S(1)} %reduce_sum.9), channel_id=1, source_target_pairs={{0,1},{1,0},{2,3},{3,2},{4,5},{5,4},{6,7},{7,6},{8,9},{9,8},{10,11... | collective-permute-start | bytes 224 | tf_op jit(solution)/shard_map/ppermute | solution.py:290
  120.9 0.8 collective-permute-done.14
  121.7 0.5 fusion.3
  122.2 0.1 subtract_bitcast_fusion
  122.3 0.6 copy.20
  (14 shorter events, 0.1 us)
Async XLA Ops:
  0.6 0.8 copy-start
  2.2 9.8 %copy-start.10 = (s32[1,256]{1,0:T(1,128)S(1)}, s32[1,256]{1,0:T(1,128)}, u32[]{:S(2)}) copy-start(s32[1,256]{1,0:T(1,128)} %param.9) | copy-start | bytes 3076
  2.2 9.8 %copy-start.1 = (bf16[1,256,1024]{2,1,0:T(8,128)(2,1)S(1)}, bf16[1,256,1024]{2,1,0:T(8,128)(2,1)}, u32[]{:S(2)}) copy-start(bf16[1,256,1024]{2,1,0:T(8,128)(2,1)} %param.8) | copy-start | bytes 1572868
  3.0 25.5 %all-to-all-start = ((bf16[8,32,896]{2,1,0:T(8,128)(2,1)}), bf16[8,32,896]{2,1,0:T(8,128)(2,1)S(1)}, u32[]{:S(2)}, u32[]{:S(2)}) async-start(bf16[8,32,896]{2,1,0:T(8,128)(2,1)} %broadcast_in_dim.16), calls=%async_computation | async-start | bytes 917504 | tf_op jit(solution)/shard_map/all_to_all | solution.py:44
  12.1 23.2 %collective-permute-start.4 = (bf16[272,1024]{1,0:T(8,128)(2,1)S(1)}, bf16[272,1024]{1,0:T(8,128)(2,1)S(1)}, u32[]{:S(2)}, u32[]{:S(2)}) collective-permute-start(bf16[272,1024]{1,0:T(8,128)(2,1)S(1)} %fusion.1.refs_0_), channel_id=1, source_target_pairs={{0,6},{2,0},{4,2},{6,4},{1,7},{3,1},{5,3},{7,5},{8,14},{10,8},{12,... | collective-permute-start | bytes 1671176 | tf_op jit(solution)/shard_map/ppermute | solution.py:287
  14.9 24.8 %collective-permute-start.6 = (bf16[272,1024]{1,0:T(8,128)(2,1)S(1)}, bf16[272,1024]{1,0:T(8,128)(2,1)S(1)}, u32[]{:S(2)}, u32[]{:S(2)}) collective-permute-start(bf16[272,1024]{1,0:T(8,128)(2,1)S(1)} %fusion.1.refs_0_), channel_id=1, source_target_pairs={{0,2},{2,4},{4,6},{6,0},{1,3},{3,5},{5,7},{7,1},{8,10},{10,12},{12... | collective-permute-start | bytes 1671176 | tf_op jit(solution)/shard_map/ppermute | solution.py:287
  14.9 28.2 %collective-permute-start.8 = (bf16[272,1024]{1,0:T(8,128)(2,1)S(1)}, bf16[272,1024]{1,0:T(8,128)(2,1)}, u32[]{:S(2)}, u32[]{:S(2)}) collective-permute-start(bf16[272,1024]{1,0:T(8,128)(2,1)S(1)} %fusion.1.refs_0_), channel_id=1, source_target_pairs={{0,4},{2,6},{4,0},{6,2},{1,5},{3,7},{5,1},{7,3},{8,12},{10,14},{12... | collective-permute-start | bytes 1671176 | tf_op jit(solution)/shard_map/ppermute | solution.py:287
  28.5 0.8 copy-start.9
  30.3 18.3 %copy-start.7 = (f32[1024]{0:T(1024)S(1)}, f32[1024]{0:T(1024)}, u32[]{:S(2)}) copy-start(f32[1024]{0:T(1024)} %param.10) | copy-start | bytes 12292
  30.3 18.3 %copy-start.8 = (f32[16]{0:T(128)S(1)}, f32[16]{0:T(128)}, u32[]{:S(2)}) copy-start(f32[16]{0:T(128)} %scales.1) | copy-start | bytes 196
  30.3 15.6 %all-to-all-start.1 = ((bf16[4,8,32,384]{3,2,1,0:T(8,128)(2,1)}), bf16[4,8,32,384]{3,2,1,0:T(8,128)(2,1)S(1)}, u32[]{:S(2)}, u32[]{:S(2)}) async-start(bf16[4,8,32,384]{3,2,1,0:T(8,128)(2,1)} %broadcast_in_dim.34), calls=%async_computation.1 | async-start | bytes 1572864 | tf_op jit(solution)/shard_map/all_to_all | solution.py:44
  34.4 12.5 %collective-permute-start.3 = (bf16[272,1024]{1,0:T(8,128)(2,1)S(1)}, bf16[272,1024]{1,0:T(8,128)(2,1)}, u32[]{:S(2)}, u32[]{:S(2)}) collective-permute-start(bf16[272,1024]{1,0:T(8,128)(2,1)S(1)} %fusion.1.refs_0_), channel_id=1, source_target_pairs={{0,1},{1,0},{2,3},{3,2},{4,5},{5,4},{6,7},{7,6},{8,9},{9,8},{10,11... | collective-permute-start | bytes 1671176 | tf_op jit(solution)/shard_map/ppermute | solution.py:290
  35.3 13.3 %collective-permute-start.5 = (bf16[272,1024]{1,0:T(8,128)(2,1)S(1)}, bf16[272,1024]{1,0:T(8,128)(2,1)}, u32[]{:S(2)}, u32[]{:S(2)}) collective-permute-start(bf16[272,1024]{1,0:T(8,128)(2,1)S(1)} %collective-permute-done.4.refs_2_), channel_id=1, source_target_pairs={{0,1},{1,0},{2,3},{3,2},{4,5},{5,4},{6,7},{7,6},{8,9},{9,8},{10,11... | collective-permute-start | bytes 1671176 | tf_op jit(solution)/shard_map/ppermute | solution.py:290
  39.7 8.9 %collective-permute-start.7 = (bf16[272,1024]{1,0:T(8,128)(2,1)S(1)}, bf16[272,1024]{1,0:T(8,128)(2,1)}, u32[]{:S(2)}, u32[]{:S(2)}) collective-permute-start(bf16[272,1024]{1,0:T(8,128)(2,1)S(1)} %collective-permute-done.6.refs_4_), channel_id=1, source_target_pairs={{0,1},{1,0},{2,3},{3,2},{4,5},{5,4},{6,7},{7,6},{8,9},{9,8},{10,11... | collective-permute-start | bytes 1671176 | tf_op jit(solution)/shard_map/ppermute | solution.py:290
  43.1 5.5 %collective-permute-start.9 = (bf16[272,1024]{1,0:T(8,128)(2,1)}, bf16[272,1024]{1,0:T(8,128)(2,1)}, u32[]{:S(2)}, u32[]{:S(2)}) collective-permute-start(bf16[272,1024]{1,0:T(8,128)(2,1)} %collective-permute-done.8.refs_6_), channel_id=1, source_target_pairs={{0,1},{1,0},{2,3},{3,2},{4,5},{5,4},{6,7},{7,6},{8,9},{9,8},{10,11... | collective-permute-start | bytes 1671176 | tf_op jit(solution)/shard_map/ppermute | solution.py:290
  45.9 35.0 %collective-permute-start = (bf16[8,32,512]{2,1,0:T(8,128)(2,1)S(1)}, bf16[8,32,512]{2,1,0:T(8,128)(2,1)S(1)}, u32[]{:S(2)}, u32[]{:S(2)}) collective-permute-start(bf16[8,32,512]{2,1,0:T(8,128)(2,1)S(1)} %slice.8.refs_0_), channel_id=1, source_target_pairs={{0,16},{8,24},{16,0},{24,8},{1,17},{9,25},{17,1},{25,9},{2,18},{10... | collective-permute-start | bytes 786440 | tf_op jit(solution)/shard_map/ppermute | solution.py:287
  46.9 33.9 %collective-permute-start.1 = (bf16[8,32,512]{2,1,0:T(8,128)(2,1)S(1)}, bf16[8,32,512]{2,1,0:T(8,128)(2,1)S(1)}, u32[]{:S(2)}, u32[]{:S(2)}) collective-permute-start(bf16[8,32,512]{2,1,0:T(8,128)(2,1)S(1)} %slice.8.refs_0_), channel_id=1, source_target_pairs={{0,24},{8,0},{16,8},{24,16},{1,25},{9,1},{17,9},{25,17},{2,26},{10... | collective-permute-start | bytes 786440 | tf_op jit(solution)/shard_map/ppermute | solution.py:287
  48.6 33.7 %collective-permute-start.2 = (bf16[8,32,512]{2,1,0:T(8,128)(2,1)S(1)}, bf16[8,32,512]{2,1,0:T(8,128)(2,1)}, u32[]{:S(2)}, u32[]{:S(2)}) collective-permute-start(bf16[8,32,512]{2,1,0:T(8,128)(2,1)S(1)} %slice.8.refs_0_), channel_id=1, source_target_pairs={{0,8},{8,16},{16,24},{24,0},{1,9},{9,17},{17,25},{25,1},{2,10},{10... | collective-permute-start | bytes 786440 | tf_op jit(solution)/shard_map/ppermute | solution.py:287
  80.8 7.8 %copy-start.11 = (f32[18]{0:T(128)S(1)}, f32[18]{0:T(128)}, u32[]{:S(2)}) copy-start(f32[18]{0:T(128)} %param.15) | copy-start | bytes 220
  80.9 16.2 %copy-start.6 = (bf16[1024,18]{0,1:T(8,128)(2,1)S(1)}, bf16[1024,18]{0,1:T(8,128)(2,1)}, u32[]{:S(2)}) copy-start(bf16[1024,18]{0,1:T(8,128)(2,1)} %param.14) | copy-start | bytes 110596
  80.9 0.7 copy-start.2
  81.6 0.7 copy-start.4
  82.3 5.3 %copy-start.3 = (bf16[8,32,512]{2,1,0:T(8,128)(2,1)S(1)}, bf16[8,32,512]{2,1,0:T(8,128)(2,1)}, u32[]{:S(2)}) copy-start(bf16[8,32,512]{2,1,0:T(8,128)(2,1)} %copy-done.2) | copy-start | bytes 786436
  82.3 5.8 %copy-start.5 = (bf16[8,32,512]{2,1,0:T(8,128)(2,1)S(1)}, bf16[8,32,512]{2,1,0:T(8,128)(2,1)}, u32[]{:S(2)}) copy-start(bf16[8,32,512]{2,1,0:T(8,128)(2,1)} %copy-done.4) | copy-start | bytes 786436
  82.3 14.8 %all-to-all-start.2 = ((bf16[8,256,128]{2,1,0:T(8,128)(2,1)}), bf16[8,256,128]{2,1,0:T(8,128)(2,1)S(1)}, u32[]{:S(2)}, u32[]{:S(2)}) async-start(bf16[8,256,128]{2,1,0:T(8,128)(2,1)} %layer.1), calls=%async_computation.2 | async-start | bytes 1048576 | tf_op jit(solution)/shard_map/all_to_all | solution.py:316
  87.6 1.5 %collective-permute-start.10 = (bf16[8,32,512]{2,1,0:T(8,128)(2,1)S(1)}, bf16[8,32,512]{2,1,0:T(8,128)(2,1)S(1)}, u32[]{:S(2)}, u32[]{:S(2)}) collective-permute-start(bf16[8,32,512]{2,1,0:T(8,128)(2,1)S(1)} %slice.8.refs_0_), channel_id=1, source_target_pairs={{0,1},{1,0},{2,3},{3,2},{4,5},{5,4},{6,7},{7,6},{8,9},{9,8},{10,11... | collective-permute-start | bytes 786440 | tf_op jit(solution)/shard_map/ppermute | solution.py:290
  87.6 1.9 %collective-permute-start.11 = (bf16[8,32,512]{2,1,0:T(8,128)(2,1)S(1)}, bf16[8,32,512]{2,1,0:T(8,128)(2,1)S(1)}, u32[]{:S(2)}, u32[]{:S(2)}) collective-permute-start(bf16[8,32,512]{2,1,0:T(8,128)(2,1)S(1)} %copy-done.3), channel_id=1, source_target_pairs={{0,1},{1,0},{2,3},{3,2},{4,5},{5,4},{6,7},{7,6},{8,9},{9,8},{10,11... | collective-permute-start | bytes 786440 | tf_op jit(solution)/shard_map/ppermute | solution.py:290
  88.1 2.1 %collective-permute-start.12 = (bf16[8,32,512]{2,1,0:T(8,128)(2,1)S(1)}, bf16[8,32,512]{2,1,0:T(8,128)(2,1)S(1)}, u32[]{:S(2)}, u32[]{:S(2)}) collective-permute-start(bf16[8,32,512]{2,1,0:T(8,128)(2,1)S(1)} %copy-done.5), channel_id=1, source_target_pairs={{0,1},{1,0},{2,3},{3,2},{4,5},{5,4},{6,7},{7,6},{8,9},{9,8},{10,11... | collective-permute-start | bytes 786440 | tf_op jit(solution)/shard_map/ppermute | solution.py:290
  88.2 2.3 %collective-permute-start.13 = (bf16[8,32,512]{2,1,0:T(8,128)(2,1)}, bf16[8,32,512]{2,1,0:T(8,128)(2,1)S(1)}, u32[]{:S(2)}, u32[]{:S(2)}) collective-permute-start(bf16[8,32,512]{2,1,0:T(8,128)(2,1)} %collective-permute-done.2.refs_3_), channel_id=1, source_target_pairs={{0,1},{1,0},{2,3},{3,2},{4,5},{5,4},{6,7},{7,6},{8,9},{9,8},{10,11... | collective-permute-start | bytes 786440 | tf_op jit(solution)/shard_map/ppermute | solution.py:290
  118.5 3.2 %collective-permute-start.14 = (f32[18]{0:T(128)S(1)}, f32[18]{0:T(128)S(1)}, u32[]{:S(2)}, u32[]{:S(2)}) collective-permute-start(f32[18]{0:T(128)S(1)} %reduce_sum.9), channel_id=1, source_target_pairs={{0,1},{1,0},{2,3},{3,2},{4,5},{5,4},{6,7},{7,6},{8,9},{9,8},{10,11... | collective-permute-start | bytes 224 | tf_op jit(solution)/shard_map/ppermute | solution.py:290

commit v4 on v3

--- a/solution.py
+++ b/solution.py
@@ -219,16 +219,25 @@
 
 
 def finish_kernel(pieces, *refs):
-    shards, (rows, bits, offset, mixed, probs, sums, weights, joined) = refs[:8], refs[8:]
+    shards, (rows, bits, offset, mixed, probs, sums, weights, joined, sems) = refs[:8], refs[8:]
     core, across = lax.axis_index("seq_1"), lax.axis_index("dp_1")
-    for i in range(8):
-        part = core if i < 4 else 1 - core
-        place = lax.rem(across + (0, 2, 1, 3)[i % 4], 4)
-        weights[part, :, place] = shards[i][...]
+    copies = []
+    for i in range(4):
+        place = lax.rem(across + (0, 2, 1, 3)[i], 4)
+        copies.append(
+            pltpu.make_async_copy(shards[i], weights.at[core, :, place], sems.at[i])
+        )
+        copies[i].start()
+    for i in range(4):
+        place = lax.rem(across + (0, 2, 1, 3)[i], 4)
+        weights[1 - core, :, place] = shards[4 + i][...]
     for source in range(8):
         joined[:, source * 128 : (source + 1) * 128] = pieces[source]
-    for part in range(2):
-        columns = slice(part * 512, part * 512 + 512)
+    for turn, part in ((0, 1 - core), (1, core)):
+        if turn:
+            for copy in copies:
+                copy.wait()
+        columns = pl.ds(pl.multiple_of(part * 512, 512), 512)
         moved = jnp.dot(
             joined[...], weights[part].reshape(1024, 512), preferred_element_type=F32
         )
@@ -252,7 +261,7 @@
     count = rows.shape[0]
     return pl.pallas_call(
         finish_kernel,
-        in_specs=[vmem()] * 12,
+        in_specs=[vmem()] + [pl.BlockSpec(memory_space=pl.ANY)] * 4 + [vmem()] * 7,
         out_specs=[vmem()] * 3,
         out_shape=[
             jax.ShapeDtypeStruct(rows.shape, BF16),
@@ -262,6 +271,7 @@
         scratch_shapes=[
             pltpu.VMEM((2, 8, 4, 32, 512), BF16),
             pltpu.VMEM((count, 1024), BF16),
+            pltpu.SemaphoreType.DMA((4,)),
         ],
         compiler_params=params(),
         name="finish",
@@ -292,7 +302,6 @@
     marked = jnp.pad(picture_label_tile.astype(BF16), ((0, 15), (0, width - count)))
     load = jnp.concatenate([rows, marked], axis=0)
     near = [load] + [from_step(load, k) for k in (1, 3, 2)]
-    pieces = [x for own in near for x in (own, from_other_core(own))]
 
     owned = jnp.concatenate(
         [
@@ -305,14 +314,16 @@
     owned = copy_for_each(owned, "dp_0")
     shard, mixing = owned[:, :, :384], owned[:, :, 384:]
     shard = copy_for_each(shard, "dp_1")
+    near[1], mixing = lax.optimization_barrier((near[1], mixing))
+    pieces = [x for own in near for x in (own, from_other_core(own))]
     mixing, _ = lax.optimization_barrier((mixing, shard))
     mixings = [mixing] + [from_step(mixing, k, "dp_1") for k in (2, 1, 3)]
 
     pieces, shard = in_vmem((pieces, shard))
     attended = layer(logit_scaling, prenorm_multiplier[None], pieces, shard)
     mixings, attended = lax.optimization_barrier((mixings, attended))
-    mixings = in_vmem(mixings)
-    mixings = in_vmem(mixings + [from_other_core(m) for m in mixings])
+    mixings = [pltpu.with_memory_space_constraint(m, pltpu.HBM) for m in mixings]
+    mixings = mixings + in_vmem([from_other_core(m) for m in mixings])
     attended = lax.all_to_all(attended, SEQ, 0, 0, tiled=True)
     mixed, probs, sums = finish(
         in_vmem(attended),

time: 125 us -> 124 us (level); the launches traced: 123 us -> 123 us
  Pallas kernels: 34.9 us -> 16.8 us
  starting transfers between devices: 37.7 us -> 50.6 us
  waiting for transfers between devices: 22.9 us -> 28.4 us
  blocking collectives: 18.6 us -> 21.1 us
  local copies, waits for them, and re-layouts: 7.28 us -> 4.88 us
    all_to_all x1, starting transfers between devices: 5.3 us -> 23.5 us  [on_device(): attended = lax.all_to_all(attended, SEQ, 0, 0, tiled=True)]
    pallas_call x1, Pallas kernels: 32.2 us -> 14.3 us  [layer(): pl.pallas_call(layer_kernel, in_specs=[smem()] + [vmem()] * 10, out_specs...]
    ppermute x9, starting transfers between devices: 12.1 us -> 6.24 us  [from_other_core(): return lax.ppermute(x, 'seq_1', [(0, 1), (1, 0)])]
    ppermute x6, waiting for transfers between devices: 0.02 us -> 5.14 us  [from_step(): return lax.ppermute(x, axis, [(i, (i - k) % length) for i in range(length)])]
    all_to_all x1, blocking collectives: 18.6 us -> 21.1 us  [copy_for_each(): lax.all_to_all(jnp.broadcast_to(x[None], (length, *x.shape)), axis, 0, 0,...]
    unnamed x25 -> x19, local copies, waits for them, and re-layouts: 3.63 us -> 1.49 us
  transfers between devices with their start and end apart: 18 -> 18, of which waited for: 8 -> 9; matrix products, arithmetic and copies ran while one was open for 2% -> 2% of each run, Pallas kernels for 26% -> 12%
where the time goes in v4:
time: 124 us; the launch traced here: 123 us
  starting transfers between devices  50.6 us (41%)
  waiting for transfers between devices  28.4 us (23%)
  blocking collectives  21.1 us (17%)
  Pallas kernels  16.8 us (14%)
  local copies, waits for them, and re-layouts  4.88 us (4%)
    all_to_all x1, starting transfers between devices, on_device(): attended = lax.all_to_all(attended, SEQ, 0, 0, tiled=True)  23.5 us
    all_to_all x1, blocking collectives, copy_for_each(): lax.all_to_all(jnp.broadcast_to(x[None], (length, *x.shape)), axis, 0, 0,...  21.1 us
    pallas_call x1, Pallas kernels, layer(): pl.pallas_call(layer_kernel, in_specs=[smem()] + [vmem()] * 10, out_specs...  14.3 us
    all_to_all x2, waiting for transfers between devices, copy_for_each(): lax.all_to_all(jnp.broadcast_to(x[None], (length, *x.shape)), axis, 0, 0,...  14.1 us
    all_to_all x2, starting transfers between devices, copy_for_each(): lax.all_to_all(jnp.broadcast_to(x[None], (length, *x.shape)), axis, 0, 0,...  13.2 us
    ppermute x6, starting transfers between devices, from_step(): return lax.ppermute(x, axis, [(i, (i - k) % length) for i in range(length)])  7.74 us
    all_to_all x1, waiting for transfers between devices, on_device(): attended = lax.all_to_all(attended, SEQ, 0, 0, tiled=True)  6.61 us
    ppermute x9, starting transfers between devices, from_other_core(): return lax.ppermute(x, 'seq_1', [(0, 1), (1, 0)])  6.24 us
  transfers between devices with their start and end apart: 18, of which 9 were waited for; matrix products, arithmetic and copies ran while one was open for 2% of the time, Pallas kernels for 12%

profile of v4, /device:TPU:1, one launch (start us, length us, event | category | flops | bytes accessed | tf_op | source)
XLA Modules:
  0.0 123.5 jit_solution(14051394348476051083)
XLA Ops:
  0.6 0.0 copy-start
  0.7 0.8 copy-done
  1.5 0.7 constant_dynamic-slice_fusion.3
  2.2 0.0 copy-start.7
  2.2 0.0 copy-start.1
  2.2 0.8 broadcast_in_dim.16
  3.0 9.0 %all-to-all-start = ((bf16[8,32,896]{2,1,0:T(8,128)(2,1)}), bf16[8,32,896]{2,1,0:T(8,128)(2,1)S(1)}, u32[]{:S(2)}, u32[]{:S(2)}) async-start(bf16[8,32,896]{2,1,0:T(8,128)(2,1)} %broadcast_in_dim.16), calls=%async_computation | async-start | bytes 917504 | tf_op jit(solution)/shard_map/all_to_all | solution.py:44
  12.0 0.0 copy-done.7
  12.1 0.0 copy-done.1
  12.1 1.4 %collective-permute-start.6 = (bf16[272,1024]{1,0:T(8,128)(2,1)S(1)}, bf16[272,1024]{1,0:T(8,128)(2,1)S(1)}, u32[]{:S(2)}, u32[]{:S(2)}) collective-permute-start(bf16[272,1024]{1,0:T(8,128)(2,1)S(1)} %fusion.1.refs_0_), channel_id=1, source_target_pairs={{0,2},{2,4},{4,6},{6,0},{1,3},{3,5},{5,7},{7,1},{8,10},{10,12},{12... | collective-permute-start | bytes 1671176 | tf_op jit(solution)/shard_map/ppermute | solution.py:297
  13.5 2.6 %collective-permute-start.8 = (bf16[272,1024]{1,0:T(8,128)(2,1)S(1)}, bf16[272,1024]{1,0:T(8,128)(2,1)S(1)}, u32[]{:S(2)}, u32[]{:S(2)}) collective-permute-start(bf16[272,1024]{1,0:T(8,128)(2,1)S(1)} %fusion.1.refs_0_), channel_id=1, source_target_pairs={{0,4},{2,6},{4,0},{6,2},{1,5},{3,7},{5,1},{7,3},{8,12},{10,14},{12... | collective-permute-start | bytes 1671176 | tf_op jit(solution)/shard_map/ppermute | solution.py:297
  16.1 1.1 collective-permute-start
  17.2 11.3 %all-to-all-done = bf16[8,32,896]{2,1,0:T(8,128)(2,1)S(1)} async-done(((bf16[8,32,896]{2,1,0:T(8,128)(2,1)}), bf16[8,32,896]{2,1,0:T(8,128)(2,1)S(1)}, u32[]{:S(2)}, u32[]{:S(2)}) %all-to-all-start) | async-done | bytes 458784 | tf_op jit(solution)/shard_map/all_to_all | solution.py:44
  28.5 1.0 broadcast_in_dim.34
  29.5 0.0 copy-start.3
  29.5 0.0 copy-start.4
  29.5 4.1 %all-to-all-start.1 = ((bf16[4,8,32,384]{3,2,1,0:T(8,128)(2,1)}), bf16[4,8,32,384]{3,2,1,0:T(8,128)(2,1)S(1)}, u32[]{:S(2)}, u32[]{:S(2)}) async-start(bf16[4,8,32,384]{3,2,1,0:T(8,128)(2,1)} %broadcast_in_dim.34), calls=%async_computation.1 | async-start | bytes 1572864 | tf_op jit(solution)/shard_map/all_to_all | solution.py:44
  33.7 0.9 collective-permute-start.4
  34.5 0.0 collective-permute-done.6.refs_4_
  34.5 0.1 collective-permute-start.7
  34.6 5.1 %collective-permute-done.8.refs_6_ = bf16[272,1024]{1,0:T(8,128)(2,1)S(1)} collective-permute-done((bf16[272,1024]{1,0:T(8,128)(2,1)S(1)}, bf16[272,1024]{1,0:T(8,128)(2,1)S(1)}, u32[]{:S(2)}, u32[]{:S(2)}) %collective-permute-start.8) | collective-permute-done | bytes 557088 | tf_op jit(solution)/shard_map/ppermute | solution.py:297
  39.8 1.9 %collective-permute-start.9 = (bf16[272,1024]{1,0:T(8,128)(2,1)S(1)}, bf16[272,1024]{1,0:T(8,128)(2,1)}, u32[]{:S(2)}, u32[]{:S(2)}) collective-permute-start(bf16[272,1024]{1,0:T(8,128)(2,1)S(1)} %collective-permute-done.8.refs_6_), channel_id=1, source_target_pairs={{0,1},{1,0},{2,3},{3,2},{4,5},{5,4},{6,7},{7,6},{8,9},{9,8},{10,11... | collective-permute-start | bytes 1671176 | tf_op jit(solution)/shard_map/ppermute | solution.py:300
  41.6 0.7 slice.8.refs_0_
  42.3 0.0 collective-permute-done.refs_2_
  42.3 0.0 collective-permute-start.5
  42.4 2.8 %all-to-all-done.1.refs_8_ = bf16[4,8,32,384]{3,2,1,0:T(8,128)(2,1)S(1)} async-done(((bf16[4,8,32,384]{3,2,1,0:T(8,128)(2,1)}), bf16[4,8,32,384]{3,2,1,0:T(8,128)(2,1)S(1)}, u32[]{:S(2)}, u32[]{:S(2)}) %all-to-all-start.1) | async-done | bytes 786464 | tf_op jit(solution)/shard_map/all_to_all | solution.py:44
  45.1 0.4 collective-permute-start.1
  45.5 0.0 collective-permute-done.4.refs_1_
  45.5 2.3 %collective-permute-start.2 = (bf16[8,32,512]{2,1,0:T(8,128)(2,1)}, bf16[8,32,512]{2,1,0:T(8,128)(2,1)}, u32[]{:S(2)}, u32[]{:S(2)}) collective-permute-start(bf16[8,32,512]{2,1,0:T(8,128)(2,1)} %slice.8.refs_0_), channel_id=1, source_target_pairs={{0,24},{8,0},{16,8},{24,16},{1,25},{9,1},{17,9},{25,17},{2,26},{10... | collective-permute-start | bytes 786440 | tf_op jit(solution)/shard_map/ppermute | solution.py:297
  47.8 0.0 collective-permute-done.7.refs_5_
  47.8 0.0 collective-permute-start.3
  47.8 0.0 collective-permute-done.9.refs_7_
  47.8 0.0 collective-permute-done.5.refs_3_
  47.8 0.0 copy-done.3
  47.9 0.0 copy-done.4
  47.9 14.3 %layer.1 = bf16[8,256,128]{2,1,0:T(8,128)(2,1)} custom-call(f32[16]{0:T(128)S(1)} %copy-done.4, f32[1,1024]{1,0:T(1,128)S(1)} %bitcast.11, bf16[272,1024]{1,0:T(8,128)(2,1)S(1)} %fusion.1.refs_0_, bf16[272,1024]{1,0:T(8,128)(2,1)} %collective-permute-done.4.refs_1_, bf16[272,1024]{1,0:T(8,128)(2,1)} %collective-permute-done.refs_2_, ...), custom_call_target="tpu_custom_call" | custom-call | tf_op jit(solution)/shard_map/layer/pallas_call | solution.py:199
  62.2 0.0 copy-start.5
  62.2 0.0 collective-permute-done.1.refs_1_
  62.2 0.0 copy-start.6
  62.2 0.0 collective-permute-done.2.refs_2_
  62.3 0.0 collective-permute-done.3.refs_3_
  62.3 23.5 %all-to-all-start.2 = ((bf16[8,256,128]{2,1,0:T(8,128)(2,1)}), bf16[8,256,128]{2,1,0:T(8,128)(2,1)S(1)}, u32[]{:S(2)}, u32[]{:S(2)}) async-start(bf16[8,256,128]{2,1,0:T(8,128)(2,1)} %layer.1), calls=%async_computation.2 | async-start | bytes 1048576 | tf_op jit(solution)/shard_map/all_to_all | solution.py:327
  85.7 0.0 copy-done.5
  85.7 0.1 collective-permute-start.10
  85.8 0.4 collective-permute-start.11
  86.3 0.1 collective-permute-start.12
  86.3 0.4 collective-permute-start.13
  86.8 0.0 copy-done.8
  86.8 0.1 copy.18.refs_10_
  86.9 0.4 collective-permute-done.10.refs_4_
  87.3 0.4 collective-permute-done.11.refs_5_
  87.7 0.6 collective-permute-done.12.refs_6_
  88.2 0.4 collective-permute-done.13.refs_7_
  88.6 6.6 %all-to-all-done.2.pieces = bf16[8,256,128]{2,1,0:T(8,128)(2,1)S(1)} async-done(((bf16[8,256,128]{2,1,0:T(8,128)(2,1)}), bf16[8,256,128]{2,1,0:T(8,128)(2,1)S(1)}, u32[]{:S(2)}, u32[]{:S(2)}) %all-to-all-start.2) | async-done | bytes 524320 | tf_op jit(solution)/shard_map/all_to_all | solution.py:327
  95.2 0.0 copy-done.6
  95.2 0.0 copy-done.2
  95.2 2.5 %finish.1 = (bf16[256,1024]{1,0:T(8,128)(2,1)}, f32[18,256]{1,0:T(8,128)S(1)}, f32[1,18]{1,0:T(1,128)S(1)}) custom-call(bf16[8,256,128]{2,1,0:T(8,128)(2,1)S(1)} %all-to-all-done.2.pieces, bf16[8,32,512]{2,1,0:T(8,128)(2,1)} %slice.8.refs_0_, bf16[8,32,512]{2,1,0:T(8,128)(2,1)} %copy-done.6, bf16[8,32,512]{2,1,0:T(8,128)(2,1)} %collective-permute-done.2.refs_2_, ...), custom_call_target="tpu_custom_call" | custom-call | tf_op jit(solution)/shard_map/finish/pallas_call | solution.py:262
  97.8 21.1 %all_to_all.20 = f32[128,1,18]{2,1,0:T(1,128)S(1)} all-to-all(f32[128,1,18]{2,1,0:T(1,128)S(1)} %broadcast_in_dim.39), channel_id=1, replica_groups=mesh['dp_0'=8,'dp_1'=4,'seq_0'=4,'seq_1'=2] {'dp_0','dp_1','seq_0'}, dimensions={0} | all-to-all | bytes 18432 | tf_op jit(solution)/shard_map/all_to_all | solution.py:44
  118.9 0.2 reduce_sum.9
  119.0 2.4 %collective-permute-start.14 = (f32[18]{0:T(128)S(1)}, f32[18]{0:T(128)S(1)}, u32[]{:S(2)}, u32[]{:S(2)}) collective-permute-start(f32[18]{0:T(128)S(1)} %reduce_sum.9), channel_id=1, source_target_pairs={{0,1},{1,0},{2,3},{3,2},{4,5},{5,4},{6,7},{7,6},{8,9},{9,8},{10,11... | collective-permute-start | bytes 224 | tf_op jit(solution)/shard_map/ppermute | solution.py:300
  121.4 0.8 collective-permute-done.14
  122.3 0.5 fusion.3
  122.8 0.1 subtract_bitcast_fusion
  122.9 0.6 copy.20
  (8 shorter events, 0.1 us)
Async XLA Ops:
  0.6 0.8 copy-start
  2.2 9.8 %copy-start.7 = (s32[1,256]{1,0:T(1,128)S(1)}, s32[1,256]{1,0:T(1,128)}, u32[]{:S(2)}) copy-start(s32[1,256]{1,0:T(1,128)} %param.9) | copy-start | bytes 3076
  2.2 9.8 %copy-start.1 = (bf16[1,256,1024]{2,1,0:T(8,128)(2,1)S(1)}, bf16[1,256,1024]{2,1,0:T(8,128)(2,1)}, u32[]{:S(2)}) copy-start(bf16[1,256,1024]{2,1,0:T(8,128)(2,1)} %param.8) | copy-start | bytes 1572868
  3.0 25.5 %all-to-all-start = ((bf16[8,32,896]{2,1,0:T(8,128)(2,1)}), bf16[8,32,896]{2,1,0:T(8,128)(2,1)S(1)}, u32[]{:S(2)}, u32[]{:S(2)}) async-start(bf16[8,32,896]{2,1,0:T(8,128)(2,1)} %broadcast_in_dim.16), calls=%async_computation | async-start | bytes 917504 | tf_op jit(solution)/shard_map/all_to_all | solution.py:44
  12.1 22.4 %collective-permute-start.6 = (bf16[272,1024]{1,0:T(8,128)(2,1)S(1)}, bf16[272,1024]{1,0:T(8,128)(2,1)S(1)}, u32[]{:S(2)}, u32[]{:S(2)}) collective-permute-start(bf16[272,1024]{1,0:T(8,128)(2,1)S(1)} %fusion.1.refs_0_), channel_id=1, source_target_pairs={{0,2},{2,4},{4,6},{6,0},{1,3},{3,5},{5,7},{7,1},{8,10},{10,12},{12... | collective-permute-start | bytes 1671176 | tf_op jit(solution)/shard_map/ppermute | solution.py:297
  13.5 26.3 %collective-permute-start.8 = (bf16[272,1024]{1,0:T(8,128)(2,1)S(1)}, bf16[272,1024]{1,0:T(8,128)(2,1)S(1)}, u32[]{:S(2)}, u32[]{:S(2)}) collective-permute-start(bf16[272,1024]{1,0:T(8,128)(2,1)S(1)} %fusion.1.refs_0_), channel_id=1, source_target_pairs={{0,4},{2,6},{4,0},{6,2},{1,5},{3,7},{5,1},{7,3},{8,12},{10,14},{12... | collective-permute-start | bytes 1671176 | tf_op jit(solution)/shard_map/ppermute | solution.py:297
  16.1 26.2 %collective-permute-start = (bf16[272,1024]{1,0:T(8,128)(2,1)S(1)}, bf16[272,1024]{1,0:T(8,128)(2,1)}, u32[]{:S(2)}, u32[]{:S(2)}) collective-permute-start(bf16[272,1024]{1,0:T(8,128)(2,1)S(1)} %fusion.1.refs_0_), channel_id=1, source_target_pairs={{0,6},{2,0},{4,2},{6,4},{1,7},{3,1},{5,3},{7,5},{8,14},{10,8},{12,... | collective-permute-start | bytes 1671176 | tf_op jit(solution)/shard_map/ppermute | solution.py:297
  29.5 18.3 %copy-start.3 = (f32[1024]{0:T(1024)S(1)}, f32[1024]{0:T(1024)}, u32[]{:S(2)}) copy-start(f32[1024]{0:T(1024)} %param.10) | copy-start | bytes 12292
  29.5 18.3 %copy-start.4 = (f32[16]{0:T(128)S(1)}, f32[16]{0:T(128)}, u32[]{:S(2)}) copy-start(f32[16]{0:T(128)} %scales.1) | copy-start | bytes 196
  29.5 15.6 %all-to-all-start.1 = ((bf16[4,8,32,384]{3,2,1,0:T(8,128)(2,1)}), bf16[4,8,32,384]{3,2,1,0:T(8,128)(2,1)S(1)}, u32[]{:S(2)}, u32[]{:S(2)}) async-start(bf16[4,8,32,384]{3,2,1,0:T(8,128)(2,1)} %broadcast_in_dim.34), calls=%async_computation.1 | async-start | bytes 1572864 | tf_op jit(solution)/shard_map/all_to_all | solution.py:44
  33.7 11.8 %collective-permute-start.4 = (bf16[272,1024]{1,0:T(8,128)(2,1)S(1)}, bf16[272,1024]{1,0:T(8,128)(2,1)}, u32[]{:S(2)}, u32[]{:S(2)}) collective-permute-start(bf16[272,1024]{1,0:T(8,128)(2,1)S(1)} %fusion.1.refs_0_), channel_id=1, source_target_pairs={{0,1},{1,0},{2,3},{3,2},{4,5},{5,4},{6,7},{7,6},{8,9},{9,8},{10,11... | collective-permute-start | bytes 1671176 | tf_op jit(solution)/shard_map/ppermute | solution.py:300
  34.5 13.3 %collective-permute-start.7 = (bf16[272,1024]{1,0:T(8,128)(2,1)S(1)}, bf16[272,1024]{1,0:T(8,128)(2,1)}, u32[]{:S(2)}, u32[]{:S(2)}) collective-permute-start(bf16[272,1024]{1,0:T(8,128)(2,1)S(1)} %collective-permute-done.6.refs_4_), channel_id=1, source_target_pairs={{0,1},{1,0},{2,3},{3,2},{4,5},{5,4},{6,7},{7,6},{8,9},{9,8},{10,11... | collective-permute-start | bytes 1671176 | tf_op jit(solution)/shard_map/ppermute | solution.py:300
  39.8 8.1 %collective-permute-start.9 = (bf16[272,1024]{1,0:T(8,128)(2,1)S(1)}, bf16[272,1024]{1,0:T(8,128)(2,1)}, u32[]{:S(2)}, u32[]{:S(2)}) collective-permute-start(bf16[272,1024]{1,0:T(8,128)(2,1)S(1)} %collective-permute-done.8.refs_6_), channel_id=1, source_target_pairs={{0,1},{1,0},{2,3},{3,2},{4,5},{5,4},{6,7},{7,6},{8,9},{9,8},{10,11... | collective-permute-start | bytes 1671176 | tf_op jit(solution)/shard_map/ppermute | solution.py:300
  42.3 5.5 %collective-permute-start.5 = (bf16[272,1024]{1,0:T(8,128)(2,1)}, bf16[272,1024]{1,0:T(8,128)(2,1)}, u32[]{:S(2)}, u32[]{:S(2)}) collective-permute-start(bf16[272,1024]{1,0:T(8,128)(2,1)} %collective-permute-done.refs_2_), channel_id=1, source_target_pairs={{0,1},{1,0},{2,3},{3,2},{4,5},{5,4},{6,7},{7,6},{8,9},{9,8},{10,11... | collective-permute-start | bytes 1671176 | tf_op jit(solution)/shard_map/ppermute | solution.py:300
  45.1 17.1 %collective-permute-start.1 = (bf16[8,32,512]{2,1,0:T(8,128)(2,1)}, bf16[8,32,512]{2,1,0:T(8,128)(2,1)S(1)}, u32[]{:S(2)}, u32[]{:S(2)}) collective-permute-start(bf16[8,32,512]{2,1,0:T(8,128)(2,1)} %slice.8.refs_0_), channel_id=1, source_target_pairs={{0,16},{8,24},{16,0},{24,8},{1,17},{9,25},{17,1},{25,9},{2,18},{10... | collective-permute-start | bytes 786440 | tf_op jit(solution)/shard_map/ppermute | solution.py:297
  45.5 16.7 %collective-permute-start.2 = (bf16[8,32,512]{2,1,0:T(8,128)(2,1)}, bf16[8,32,512]{2,1,0:T(8,128)(2,1)}, u32[]{:S(2)}, u32[]{:S(2)}) collective-permute-start(bf16[8,32,512]{2,1,0:T(8,128)(2,1)} %slice.8.refs_0_), channel_id=1, source_target_pairs={{0,24},{8,0},{16,8},{24,16},{1,25},{9,1},{17,9},{25,17},{2,26},{10... | collective-permute-start | bytes 786440 | tf_op jit(solution)/shard_map/ppermute | solution.py:297
  47.8 14.4 %collective-permute-start.3 = (bf16[8,32,512]{2,1,0:T(8,128)(2,1)}, bf16[8,32,512]{2,1,0:T(8,128)(2,1)}, u32[]{:S(2)}, u32[]{:S(2)}) collective-permute-start(bf16[8,32,512]{2,1,0:T(8,128)(2,1)} %slice.8.refs_0_), channel_id=1, source_target_pairs={{0,8},{8,16},{16,24},{24,0},{1,9},{9,17},{17,25},{25,1},{2,10},{10... | collective-permute-start | bytes 786440 | tf_op jit(solution)/shard_map/ppermute | solution.py:297
  62.2 23.5 %copy-start.5 = (bf16[8,32,512]{2,1,0:T(8,128)(2,1)S(1)}, bf16[8,32,512]{2,1,0:T(8,128)(2,1)}, u32[]{:S(2)}) copy-start(bf16[8,32,512]{2,1,0:T(8,128)(2,1)} %slice.8.refs_0_) | copy-start | bytes 786436
  62.2 24.6 %copy-start.8 = (f32[18]{0:T(128)S(1)}, f32[18]{0:T(128)}, u32[]{:S(2)}) copy-start(f32[18]{0:T(128)} %param.15) | copy-start | bytes 220
  62.2 33.0 %copy-start.2 = (bf16[1024,18]{0,1:T(8,128)(2,1)S(1)}, bf16[1024,18]{0,1:T(8,128)(2,1)}, u32[]{:S(2)}) copy-start(bf16[1024,18]{0,1:T(8,128)(2,1)} %param.14) | copy-start | bytes 110596
  62.2 33.0 %copy-start.6 = (bf16[8,32,512]{2,1,0:T(8,128)(2,1)}, bf16[8,32,512]{2,1,0:T(8,128)(2,1)S(1)}, u32[]{:S(2)}) copy-start(bf16[8,32,512]{2,1,0:T(8,128)(2,1)S(1)} %collective-permute-done.1.refs_1_) | copy-start | bytes 786436
  62.3 33.0 %all-to-all-start.2 = ((bf16[8,256,128]{2,1,0:T(8,128)(2,1)}), bf16[8,256,128]{2,1,0:T(8,128)(2,1)S(1)}, u32[]{:S(2)}, u32[]{:S(2)}) async-start(bf16[8,256,128]{2,1,0:T(8,128)(2,1)} %layer.1), calls=%async_computation.2 | async-start | bytes 1048576 | tf_op jit(solution)/shard_map/all_to_all | solution.py:327
  85.7 1.5 %collective-permute-start.10 = (bf16[8,32,512]{2,1,0:T(8,128)(2,1)S(1)}, bf16[8,32,512]{2,1,0:T(8,128)(2,1)S(1)}, u32[]{:S(2)}, u32[]{:S(2)}) collective-permute-start(bf16[8,32,512]{2,1,0:T(8,128)(2,1)S(1)} %copy-done.5), channel_id=1, source_target_pairs={{0,1},{1,0},{2,3},{3,2},{4,5},{5,4},{6,7},{7,6},{8,9},{9,8},{10,11... | collective-permute-start | bytes 786440 | tf_op jit(solution)/shard_map/ppermute | solution.py:300
  85.8 1.8 %collective-permute-start.11 = (bf16[8,32,512]{2,1,0:T(8,128)(2,1)S(1)}, bf16[8,32,512]{2,1,0:T(8,128)(2,1)S(1)}, u32[]{:S(2)}, u32[]{:S(2)}) collective-permute-start(bf16[8,32,512]{2,1,0:T(8,128)(2,1)S(1)} %collective-permute-done.1.refs_1_), channel_id=1, source_target_pairs={{0,1},{1,0},{2,3},{3,2},{4,5},{5,4},{6,7},{7,6},{8,9},{9,8},{10,11... | collective-permute-start | bytes 786440 | tf_op jit(solution)/shard_map/ppermute | solution.py:300
  86.3 2.0 %collective-permute-start.12 = (bf16[8,32,512]{2,1,0:T(8,128)(2,1)}, bf16[8,32,512]{2,1,0:T(8,128)(2,1)S(1)}, u32[]{:S(2)}, u32[]{:S(2)}) collective-permute-start(bf16[8,32,512]{2,1,0:T(8,128)(2,1)} %collective-permute-done.2.refs_2_), channel_id=1, source_target_pairs={{0,1},{1,0},{2,3},{3,2},{4,5},{5,4},{6,7},{7,6},{8,9},{9,8},{10,11... | collective-permute-start | bytes 786440 | tf_op jit(solution)/shard_map/ppermute | solution.py:300
  86.3 2.3 %collective-permute-start.13 = (bf16[8,32,512]{2,1,0:T(8,128)(2,1)}, bf16[8,32,512]{2,1,0:T(8,128)(2,1)S(1)}, u32[]{:S(2)}, u32[]{:S(2)}) collective-permute-start(bf16[8,32,512]{2,1,0:T(8,128)(2,1)} %collective-permute-done.3.refs_3_), channel_id=1, source_target_pairs={{0,1},{1,0},{2,3},{3,2},{4,5},{5,4},{6,7},{7,6},{8,9},{9,8},{10,11... | collective-permute-start | bytes 786440 | tf_op jit(solution)/shard_map/ppermute | solution.py:300
  119.0 3.2 %collective-permute-start.14 = (f32[18]{0:T(128)S(1)}, f32[18]{0:T(128)S(1)}, u32[]{:S(2)}, u32[]{:S(2)}) collective-permute-start(f32[18]{0:T(128)S(1)} %reduce_sum.9), channel_id=1, source_target_pairs={{0,1},{1,0},{2,3},{3,2},{4,5},{5,4},{6,7},{7,6},{8,9},{9,8},{10,11... | collective-permute-start | bytes 224 | tf_op jit(solution)/shard_map/ppermute | solution.py:300

commit v5 on v4

--- a/solution.py
+++ b/solution.py
@@ -42,6 +42,46 @@
 def copy_for_each(x, axis):
     length = lax.axis_size(axis)
     return lax.all_to_all(jnp.broadcast_to(x[None], (length, *x.shape)), axis, 0, 0, tiled=True)
+
+
+def pack_kernel(triple, final, out, held, sems):
+    chip, core = lax.axis_index("seq_0"), lax.axis_index("seq_1")
+    member = 2 * chip + core
+    copies = [
+        pltpu.make_async_copy(
+            triple.at[:, pl.ds(pl.multiple_of(1024 * i + member * 128, 128), 128)],
+            held.at[:, pl.ds(128 * i, 128)],
+            sems.at[i],
+        )
+        for i in range(3)
+    ]
+    copies.append(
+        pltpu.make_async_copy(
+            final.at[:, pl.ds(pl.multiple_of(core * 512, 512), 512)],
+            held.at[:, pl.ds(384, 512)],
+            sems.at[3],
+        )
+    )
+    for copy in copies:
+        copy.start()
+    for copy in copies:
+        copy.wait()
+    for i in range(out.shape[0]):
+        out[i] = held[...]
+
+
+def pack(triple, final, length):
+    shard = triple.shape[0]
+    anywhere = pl.BlockSpec(memory_space=pltpu.HBM)
+    return pl.pallas_call(
+        pack_kernel,
+        in_specs=[anywhere, anywhere],
+        out_specs=vmem(),
+        out_shape=jax.ShapeDtypeStruct((length, shard, 896), BF16),
+        scratch_shapes=[pltpu.VMEM((shard, 896), BF16), pltpu.SemaphoreType.DMA((4,))],
+        compiler_params=params(),
+        name="pack",
+    )(triple, final)
 
 
 def layer_kernel(scales, gain, *refs):
@@ -303,18 +343,12 @@
     load = jnp.concatenate([rows, marked], axis=0)
     near = [load] + [from_step(load, k) for k in (1, 3, 2)]
 
-    owned = jnp.concatenate(
-        [
-            lax.dynamic_slice_in_dim(triple_projector, member * 128 + 1024 * i, 128, 1)
-            for i in range(3)
-        ]
-        + [lax.dynamic_slice_in_dim(final_projector, core * 512, 512, 1)],
-        axis=1,
-    )
-    owned = copy_for_each(owned, "dp_0")
+    in_hbm = lambda x: pltpu.with_memory_space_constraint(x, pltpu.HBM)
+    owned = pack(in_hbm(triple_projector), in_hbm(final_projector), lax.axis_size("dp_0"))
+    owned = lax.all_to_all(owned, "dp_0", 0, 0, tiled=True)
     shard, mixing = owned[:, :, :384], owned[:, :, 384:]
+    shard, mixing = lax.optimization_barrier((shard, mixing))
     shard = copy_for_each(shard, "dp_1")
-    near[1], mixing = lax.optimization_barrier((near[1], mixing))
     pieces = [x for own in near for x in (own, from_other_core(own))]
     mixing, _ = lax.optimization_barrier((mixing, shard))
     mixings = [mixing] + [from_step(mixing, k, "dp_1") for k in (2, 1, 3)]
@@ -322,7 +356,7 @@
     pieces, shard = in_vmem((pieces, shard))
     attended = layer(logit_scaling, prenorm_multiplier[None], pieces, shard)
     mixings, attended = lax.optimization_barrier((mixings, attended))
-    mixings = [pltpu.with_memory_space_constraint(m, pltpu.HBM) for m in mixings]
+    mixings = [in_hbm(m) for m in mixings]
     mixings = mixings + in_vmem([from_other_core(m) for m in mixings])
     attended = lax.all_to_all(attended, SEQ, 0, 0, tiled=True)
     mixed, probs, sums = finish(

time: 124 us -> 121 us (0.976)
  starting transfers between devices: 50.6 us -> 56.3 us
  waiting for transfers between devices: 28.4 us -> 23.8 us
  blocking collectives: 21.1 us -> 16.9 us
  Pallas kernels: 16.8 us -> 19.2 us
  local copies, waits for them, and re-layouts: 4.88 us -> 2.5 us
    all_to_all x0 -> x1, waiting for transfers between devices: none -> 11.9 us  [on_device(): owned = lax.all_to_all(owned, 'dp_0', 0, 0, tiled=True)]
    all_to_all x2 -> x1, waiting for transfers between devices: 14.1 us -> 2.72 us  [copy_for_each(): lax.all_to_all(jnp.broadcast_to(x[None], (length, *x.shape)), axis, 0, 0,...]
    all_to_all x0 -> x1, starting transfers between devices: none -> 9.03 us  [on_device(): owned = lax.all_to_all(owned, 'dp_0', 0, 0, tiled=True)]
    all_to_all x2 -> x1, starting transfers between devices: 13.2 us -> 4.14 us  [copy_for_each(): lax.all_to_all(jnp.broadcast_to(x[None], (length, *x.shape)), axis, 0, 0,...]
    ppermute x9, starting transfers between devices: 6.24 us -> 12.2 us  [from_other_core(): return lax.ppermute(x, 'seq_1', [(0, 1), (1, 0)])]
    ppermute x6, waiting for transfers between devices: 5.14 us -> 0.02 us  [from_step(): return lax.ppermute(x, axis, [(i, (i - k) % length) for i in range(length)])]
    all_to_all x1, blocking collectives: 21.1 us -> 16.9 us  [copy_for_each(): lax.all_to_all(jnp.broadcast_to(x[None], (length, *x.shape)), axis, 0, 0,...]
    pallas_call x0 -> x1, Pallas kernels: none -> 1.71 us  [pack(): pl.pallas_call(pack_kernel, in_specs=[anywhere, anywhere], out_specs=vmem...]
  transfers between devices with their start and end apart: 18 -> 18, of which waited for: 9 -> 8; matrix products, arithmetic and copies ran while one was open for 2% -> 2% of each run, Pallas kernels for 12% -> 12%
where the time goes in v5:
time: 121 us; the launch traced here: 120 us
  starting transfers between devices  56.3 us (47%)
  waiting for transfers between devices  23.8 us (20%)
  Pallas kernels  19.2 us (16%)
  blocking collectives  16.9 us (14%)
  local copies, waits for them, and re-layouts  2.5 us (2%)
    all_to_all x1, starting transfers between devices, on_device(): attended = lax.all_to_all(attended, SEQ, 0, 0, tiled=True)  23.8 us
    all_to_all x1, blocking collectives, copy_for_each(): lax.all_to_all(jnp.broadcast_to(x[None], (length, *x.shape)), axis, 0, 0,...  16.9 us
    pallas_call x1, Pallas kernels, layer(): pl.pallas_call(layer_kernel, in_specs=[smem()] + [vmem()] * 10, out_specs...  15 us
    ppermute x9, starting transfers between devices, from_other_core(): return lax.ppermute(x, 'seq_1', [(0, 1), (1, 0)])  12.2 us
    all_to_all x1, waiting for transfers between devices, on_device(): owned = lax.all_to_all(owned, 'dp_0', 0, 0, tiled=True)  11.9 us
    all_to_all x1, starting transfers between devices, on_device(): owned = lax.all_to_all(owned, 'dp_0', 0, 0, tiled=True)  9.03 us
    ppermute x6, starting transfers between devices, from_step(): return lax.ppermute(x, axis, [(i, (i - k) % length) for i in range(length)])  7.14 us
    all_to_all x1, waiting for transfers between devices, on_device(): attended = lax.all_to_all(attended, SEQ, 0, 0, tiled=True)  6.61 us
  transfers between devices with their start and end apart: 18, of which 8 were waited for; matrix products, arithmetic and copies ran while one was open for 2% of the time, Pallas kernels for 12%

profile of v5, /device:TPU:1, one launch (start us, length us, event | category | flops | bytes accessed | tf_op | source)
XLA Modules:
  0.0 120.2 jit_solution(9869241114638359542)
XLA Ops:
  0.6 0.0 copy-start.5
  0.6 0.0 copy-start
  0.7 1.7 %pack.1 = bf16[8,32,896]{2,1,0:T(8,128)(2,1)} custom-call(bf16[32,3072]{1,0:T(8,128)(2,1)} %triple.1, bf16[32,1024]{1,0:T(8,128)(2,1)} %final.1), custom_call_target="tpu_custom_call" | custom-call | tf_op jit(solution)/shard_map/pack/pallas_call | solution.py:76
  2.4 9.0 %all-to-all-start = ((bf16[8,32,896]{2,1,0:T(8,128)(2,1)}), bf16[8,32,896]{2,1,0:T(8,128)(2,1)S(1)}, u32[]{:S(2)}, u32[]{:S(2)}) async-start(bf16[8,32,896]{2,1,0:T(8,128)(2,1)} %pack.1), calls=%async_computation | async-start | bytes 917504 | tf_op jit(solution)/shard_map/all_to_all | solution.py:348
  11.4 0.0 copy-done.5
  11.4 0.0 copy-done
  11.5 2.8 %collective-permute-start.4 = (bf16[272,1024]{1,0:T(8,128)(2,1)S(1)}, bf16[272,1024]{1,0:T(8,128)(2,1)S(1)}, u32[]{:S(2)}, u32[]{:S(2)}) collective-permute-start(bf16[272,1024]{1,0:T(8,128)(2,1)S(1)} %fusion.1.refs_0_), channel_id=1, source_target_pairs={{0,6},{2,0},{4,2},{6,4},{1,7},{3,1},{5,3},{7,5},{8,14},{10,8},{12,... | collective-permute-start | bytes 1671176 | tf_op jit(solution)/shard_map/ppermute | solution.py:337
  14.3 0.0 collective-permute-start.6
  14.3 1.6 %collective-permute-start.8 = (bf16[272,1024]{1,0:T(8,128)(2,1)S(1)}, bf16[272,1024]{1,0:T(8,128)(2,1)S(1)}, u32[]{:S(2)}, u32[]{:S(2)}) collective-permute-start(bf16[272,1024]{1,0:T(8,128)(2,1)S(1)} %fusion.1.refs_0_), channel_id=1, source_target_pairs={{0,4},{2,6},{4,0},{6,2},{1,5},{3,7},{5,1},{7,3},{8,12},{10,14},{12... | collective-permute-start | bytes 1671176 | tf_op jit(solution)/shard_map/ppermute | solution.py:337
  15.9 11.9 %all-to-all-done = bf16[8,32,896]{2,1,0:T(8,128)(2,1)S(1)} async-done(((bf16[8,32,896]{2,1,0:T(8,128)(2,1)}), bf16[8,32,896]{2,1,0:T(8,128)(2,1)S(1)}, u32[]{:S(2)}, u32[]{:S(2)}) %all-to-all-start) | async-done | bytes 458784 | tf_op jit(solution)/shard_map/all_to_all | solution.py:348
  27.9 0.7 slice.9.refs_0_
  28.6 1.0 broadcast_in_dim.27
  29.6 0.0 copy-start.2
  29.6 0.0 copy-start.3
  29.6 4.1 %all-to-all-start.1 = ((bf16[4,8,32,384]{3,2,1,0:T(8,128)(2,1)}), bf16[4,8,32,384]{3,2,1,0:T(8,128)(2,1)S(1)}, u32[]{:S(2)}, u32[]{:S(2)}) async-start(bf16[4,8,32,384]{3,2,1,0:T(8,128)(2,1)} %broadcast_in_dim.27), calls=%async_computation.1 | async-start | bytes 1572864 | tf_op jit(solution)/shard_map/all_to_all | solution.py:44
  33.7 0.9 collective-permute-start.3
  34.6 0.0 collective-permute-done.4.refs_2_
  34.6 4.5 %collective-permute-start.5 = (bf16[272,1024]{1,0:T(8,128)(2,1)S(1)}, bf16[272,1024]{1,0:T(8,128)(2,1)}, u32[]{:S(2)}, u32[]{:S(2)}) collective-permute-start(bf16[272,1024]{1,0:T(8,128)(2,1)S(1)} %collective-permute-done.4.refs_2_), channel_id=1, source_target_pairs={{0,1},{1,0},{2,3},{3,2},{4,5},{5,4},{6,7},{7,6},{8,9},{9,8},{10,11... | collective-permute-start | bytes 1671176 | tf_op jit(solution)/shard_map/ppermute | solution.py:340
  39.1 0.0 collective-permute-done.6.refs_4_
  39.1 3.4 %collective-permute-start.7 = (bf16[272,1024]{1,0:T(8,128)(2,1)S(1)}, bf16[272,1024]{1,0:T(8,128)(2,1)}, u32[]{:S(2)}, u32[]{:S(2)}) collective-permute-start(bf16[272,1024]{1,0:T(8,128)(2,1)S(1)} %collective-permute-done.6.refs_4_), channel_id=1, source_target_pairs={{0,1},{1,0},{2,3},{3,2},{4,5},{5,4},{6,7},{7,6},{8,9},{9,8},{10,11... | collective-permute-start | bytes 1671176 | tf_op jit(solution)/shard_map/ppermute | solution.py:340
  42.5 0.0 collective-permute-done.8.refs_6_
  42.5 0.0 collective-permute-start.9
  42.5 2.7 %all-to-all-done.1.refs_8_ = bf16[4,8,32,384]{3,2,1,0:T(8,128)(2,1)S(1)} async-done(((bf16[4,8,32,384]{3,2,1,0:T(8,128)(2,1)}), bf16[4,8,32,384]{3,2,1,0:T(8,128)(2,1)S(1)}, u32[]{:S(2)}, u32[]{:S(2)}) %all-to-all-start.1) | async-done | bytes 786464 | tf_op jit(solution)/shard_map/all_to_all | solution.py:44
  45.2 0.4 collective-permute-start
  45.6 0.0 collective-permute-done.3.refs_1_
  45.6 2.3 %collective-permute-start.1 = (bf16[8,32,512]{2,1,0:T(8,128)(2,1)}, bf16[8,32,512]{2,1,0:T(8,128)(2,1)}, u32[]{:S(2)}, u32[]{:S(2)}) collective-permute-start(bf16[8,32,512]{2,1,0:T(8,128)(2,1)} %slice.9.refs_0_), channel_id=1, source_target_pairs={{0,24},{8,0},{16,8},{24,16},{1,25},{9,1},{17,9},{25,17},{2,26},{10... | collective-permute-start | bytes 786440 | tf_op jit(solution)/shard_map/ppermute | solution.py:337
  47.9 0.0 collective-permute-done.5.refs_3_
  47.9 0.0 collective-permute-start.2
  47.9 0.0 collective-permute-done.7.refs_5_
  47.9 0.0 collective-permute-done.9.refs_7_
  47.9 0.0 copy-done.2
  47.9 0.0 copy-done.3
  47.9 15.0 %layer.1 = bf16[8,256,128]{2,1,0:T(8,128)(2,1)} custom-call(f32[16]{0:T(128)S(1)} %copy-done.3, f32[1,1024]{1,0:T(1,128)S(1)} %bitcast.11, bf16[272,1024]{1,0:T(8,128)(2,1)S(1)} %fusion.1.refs_0_, bf16[272,1024]{1,0:T(8,128)(2,1)} %collective-permute-done.3.refs_1_, bf16[272,1024]{1,0:T(8,128)(2,1)S(1)} %collective-permute-done.4.refs_2_, ...), custom_call_target="tpu_custom_call" | custom-call | tf_op jit(solution)/shard_map/layer/pallas_call | solution.py:239
  62.9 0.0 copy-start.4
  62.9 0.0 copy-start.6
  62.9 0.0 copy-start.1
  62.9 0.0 collective-permute-done.refs_1_
  62.9 0.0 collective-permute-done.1.refs_2_
  62.9 0.0 collective-permute-done.2.refs_3_
  62.9 23.8 %all-to-all-start.2 = ((bf16[8,256,128]{2,1,0:T(8,128)(2,1)}), bf16[8,256,128]{2,1,0:T(8,128)(2,1)S(1)}, u32[]{:S(2)}, u32[]{:S(2)}) async-start(bf16[8,256,128]{2,1,0:T(8,128)(2,1)} %layer.1), calls=%async_computation.2 | async-start | bytes 1048576 | tf_op jit(solution)/shard_map/all_to_all | solution.py:361
  86.7 0.0 copy-done.4
  86.7 0.1 collective-permute-start.10
  86.8 0.4 collective-permute-start.11
  87.3 0.1 collective-permute-start.12
  87.3 0.4 collective-permute-start.13
  87.8 0.0 copy-done.6
  87.8 0.1 copy.18.refs_10_
  87.9 0.4 collective-permute-done.10.refs_4_
  88.3 0.6 collective-permute-done.11.refs_5_
  88.9 0.4 collective-permute-done.12.refs_6_
  89.2 0.4 collective-permute-done.13.refs_7_
  89.6 6.6 %all-to-all-done.2.pieces = bf16[8,256,128]{2,1,0:T(8,128)(2,1)S(1)} async-done(((bf16[8,256,128]{2,1,0:T(8,128)(2,1)}), bf16[8,256,128]{2,1,0:T(8,128)(2,1)S(1)}, u32[]{:S(2)}, u32[]{:S(2)}) %all-to-all-start.2) | async-done | bytes 524320 | tf_op jit(solution)/shard_map/all_to_all | solution.py:361
  96.2 0.0 copy-done.1
  96.2 2.5 %finish.1 = (bf16[256,1024]{1,0:T(8,128)(2,1)}, f32[18,256]{1,0:T(8,128)S(1)}, f32[1,18]{1,0:T(1,128)S(1)}) custom-call(bf16[8,256,128]{2,1,0:T(8,128)(2,1)S(1)} %all-to-all-done.2.pieces, bf16[8,32,512]{2,1,0:T(8,128)(2,1)} %slice.9.refs_0_, bf16[8,32,512]{2,1,0:T(8,128)(2,1)} %collective-permute-done.refs_1_, ...), custom_call_target="tpu_custom_call" | custom-call | tf_op jit(solution)/shard_map/finish/pallas_call | solution.py:302
  98.8 16.9 %all_to_all.20 = f32[128,1,18]{2,1,0:T(1,128)S(1)} all-to-all(f32[128,1,18]{2,1,0:T(1,128)S(1)} %broadcast_in_dim.32), channel_id=1, replica_groups=mesh['dp_0'=8,'dp_1'=4,'seq_0'=4,'seq_1'=2] {'dp_0','dp_1','seq_0'}, dimensions={0} | all-to-all | bytes 18432 | tf_op jit(solution)/shard_map/all_to_all | solution.py:44
  115.6 0.2 reduce_sum.9
  115.8 2.4 %collective-permute-start.14 = (f32[18]{0:T(128)S(1)}, f32[18]{0:T(128)S(1)}, u32[]{:S(2)}, u32[]{:S(2)}) collective-permute-start(f32[18]{0:T(128)S(1)} %reduce_sum.9), channel_id=1, source_target_pairs={{0,1},{1,0},{2,3},{3,2},{4,5},{5,4},{6,7},{7,6},{8,9},{9,8},{10,11... | collective-permute-start | bytes 224 | tf_op jit(solution)/shard_map/ppermute | solution.py:340
  118.2 0.8 collective-permute-done.14
  119.0 0.5 fusion.3
  119.5 0.1 subtract_bitcast_fusion
  119.6 0.6 copy.20
  (4 shorter events, 0.1 us)
Async XLA Ops:
  0.6 10.8 %copy-start.5 = (s32[1,256]{1,0:T(1,128)S(1)}, s32[1,256]{1,0:T(1,128)}, u32[]{:S(2)}) copy-start(s32[1,256]{1,0:T(1,128)} %param.9) | copy-start | bytes 3076
  0.6 10.8 %copy-start = (bf16[1,256,1024]{2,1,0:T(8,128)(2,1)S(1)}, bf16[1,256,1024]{2,1,0:T(8,128)(2,1)}, u32[]{:S(2)}) copy-start(bf16[1,256,1024]{2,1,0:T(8,128)(2,1)} %param.8) | copy-start | bytes 1572868
  2.4 25.5 %all-to-all-start = ((bf16[8,32,896]{2,1,0:T(8,128)(2,1)}), bf16[8,32,896]{2,1,0:T(8,128)(2,1)S(1)}, u32[]{:S(2)}, u32[]{:S(2)}) async-start(bf16[8,32,896]{2,1,0:T(8,128)(2,1)} %pack.1), calls=%async_computation | async-start | bytes 917504 | tf_op jit(solution)/shard_map/all_to_all | solution.py:348
  11.5 23.1 %collective-permute-start.4 = (bf16[272,1024]{1,0:T(8,128)(2,1)S(1)}, bf16[272,1024]{1,0:T(8,128)(2,1)S(1)}, u32[]{:S(2)}, u32[]{:S(2)}) collective-permute-start(bf16[272,1024]{1,0:T(8,128)(2,1)S(1)} %fusion.1.refs_0_), channel_id=1, source_target_pairs={{0,6},{2,0},{4,2},{6,4},{1,7},{3,1},{5,3},{7,5},{8,14},{10,8},{12,... | collective-permute-start | bytes 1671176 | tf_op jit(solution)/shard_map/ppermute | solution.py:337
  14.3 24.8 %collective-permute-start.6 = (bf16[272,1024]{1,0:T(8,128)(2,1)S(1)}, bf16[272,1024]{1,0:T(8,128)(2,1)S(1)}, u32[]{:S(2)}, u32[]{:S(2)}) collective-permute-start(bf16[272,1024]{1,0:T(8,128)(2,1)S(1)} %fusion.1.refs_0_), channel_id=1, source_target_pairs={{0,2},{2,4},{4,6},{6,0},{1,3},{3,5},{5,7},{7,1},{8,10},{10,12},{12... | collective-permute-start | bytes 1671176 | tf_op jit(solution)/shard_map/ppermute | solution.py:337
  14.3 28.2 %collective-permute-start.8 = (bf16[272,1024]{1,0:T(8,128)(2,1)S(1)}, bf16[272,1024]{1,0:T(8,128)(2,1)S(1)}, u32[]{:S(2)}, u32[]{:S(2)}) collective-permute-start(bf16[272,1024]{1,0:T(8,128)(2,1)S(1)} %fusion.1.refs_0_), channel_id=1, source_target_pairs={{0,4},{2,6},{4,0},{6,2},{1,5},{3,7},{5,1},{7,3},{8,12},{10,14},{12... | collective-permute-start | bytes 1671176 | tf_op jit(solution)/shard_map/ppermute | solution.py:337
  29.6 18.3 %copy-start.2 = (f32[1024]{0:T(1024)S(1)}, f32[1024]{0:T(1024)}, u32[]{:S(2)}) copy-start(f32[1024]{0:T(1024)} %param.10) | copy-start | bytes 12292
  29.6 18.3 %copy-start.3 = (f32[16]{0:T(128)S(1)}, f32[16]{0:T(128)}, u32[]{:S(2)}) copy-start(f32[16]{0:T(128)} %scales.1) | copy-start | bytes 196
  29.6 15.6 %all-to-all-start.1 = ((bf16[4,8,32,384]{3,2,1,0:T(8,128)(2,1)}), bf16[4,8,32,384]{3,2,1,0:T(8,128)(2,1)S(1)}, u32[]{:S(2)}, u32[]{:S(2)}) async-start(bf16[4,8,32,384]{3,2,1,0:T(8,128)(2,1)} %broadcast_in_dim.27), calls=%async_computation.1 | async-start | bytes 1572864 | tf_op jit(solution)/shard_map/all_to_all | solution.py:44
  33.7 11.8 %collective-permute-start.3 = (bf16[272,1024]{1,0:T(8,128)(2,1)S(1)}, bf16[272,1024]{1,0:T(8,128)(2,1)}, u32[]{:S(2)}, u32[]{:S(2)}) collective-permute-start(bf16[272,1024]{1,0:T(8,128)(2,1)S(1)} %fusion.1.refs_0_), channel_id=1, source_target_pairs={{0,1},{1,0},{2,3},{3,2},{4,5},{5,4},{6,7},{7,6},{8,9},{9,8},{10,11... | collective-permute-start | bytes 1671176 | tf_op jit(solution)/shard_map/ppermute | solution.py:340
  34.6 13.3 %collective-permute-start.5 = (bf16[272,1024]{1,0:T(8,128)(2,1)S(1)}, bf16[272,1024]{1,0:T(8,128)(2,1)}, u32[]{:S(2)}, u32[]{:S(2)}) collective-permute-start(bf16[272,1024]{1,0:T(8,128)(2,1)S(1)} %collective-permute-done.4.refs_2_), channel_id=1, source_target_pairs={{0,1},{1,0},{2,3},{3,2},{4,5},{5,4},{6,7},{7,6},{8,9},{9,8},{10,11... | collective-permute-start | bytes 1671176 | tf_op jit(solution)/shard_map/ppermute | solution.py:340
  39.1 8.8 %collective-permute-start.7 = (bf16[272,1024]{1,0:T(8,128)(2,1)S(1)}, bf16[272,1024]{1,0:T(8,128)(2,1)}, u32[]{:S(2)}, u32[]{:S(2)}) collective-permute-start(bf16[272,1024]{1,0:T(8,128)(2,1)S(1)} %collective-permute-done.6.refs_4_), channel_id=1, source_target_pairs={{0,1},{1,0},{2,3},{3,2},{4,5},{5,4},{6,7},{7,6},{8,9},{9,8},{10,11... | collective-permute-start | bytes 1671176 | tf_op jit(solution)/shard_map/ppermute | solution.py:340
  42.5 5.4 %collective-permute-start.9 = (bf16[272,1024]{1,0:T(8,128)(2,1)S(1)}, bf16[272,1024]{1,0:T(8,128)(2,1)}, u32[]{:S(2)}, u32[]{:S(2)}) collective-permute-start(bf16[272,1024]{1,0:T(8,128)(2,1)S(1)} %collective-permute-done.8.refs_6_), channel_id=1, source_target_pairs={{0,1},{1,0},{2,3},{3,2},{4,5},{5,4},{6,7},{7,6},{8,9},{9,8},{10,11... | collective-permute-start | bytes 1671176 | tf_op jit(solution)/shard_map/ppermute | solution.py:340
  45.2 17.7 %collective-permute-start = (bf16[8,32,512]{2,1,0:T(8,128)(2,1)}, bf16[8,32,512]{2,1,0:T(8,128)(2,1)}, u32[]{:S(2)}, u32[]{:S(2)}) collective-permute-start(bf16[8,32,512]{2,1,0:T(8,128)(2,1)} %slice.9.refs_0_), channel_id=1, source_target_pairs={{0,16},{8,24},{16,0},{24,8},{1,17},{9,25},{17,1},{25,9},{2,18},{10... | collective-permute-start | bytes 786440 | tf_op jit(solution)/shard_map/ppermute | solution.py:337
  45.6 17.4 %collective-permute-start.1 = (bf16[8,32,512]{2,1,0:T(8,128)(2,1)}, bf16[8,32,512]{2,1,0:T(8,128)(2,1)}, u32[]{:S(2)}, u32[]{:S(2)}) collective-permute-start(bf16[8,32,512]{2,1,0:T(8,128)(2,1)} %slice.9.refs_0_), channel_id=1, source_target_pairs={{0,24},{8,0},{16,8},{24,16},{1,25},{9,1},{17,9},{25,17},{2,26},{10... | collective-permute-start | bytes 786440 | tf_op jit(solution)/shard_map/ppermute | solution.py:337
  47.9 15.1 %collective-permute-start.2 = (bf16[8,32,512]{2,1,0:T(8,128)(2,1)}, bf16[8,32,512]{2,1,0:T(8,128)(2,1)}, u32[]{:S(2)}, u32[]{:S(2)}) collective-permute-start(bf16[8,32,512]{2,1,0:T(8,128)(2,1)} %slice.9.refs_0_), channel_id=1, source_target_pairs={{0,8},{8,16},{16,24},{24,0},{1,9},{9,17},{17,25},{25,1},{2,10},{10... | collective-permute-start | bytes 786440 | tf_op jit(solution)/shard_map/ppermute | solution.py:337
  62.9 23.8 %copy-start.4 = (bf16[8,32,512]{2,1,0:T(8,128)(2,1)S(1)}, bf16[8,32,512]{2,1,0:T(8,128)(2,1)}, u32[]{:S(2)}) copy-start(bf16[8,32,512]{2,1,0:T(8,128)(2,1)} %slice.9.refs_0_) | copy-start | bytes 786436
  62.9 24.9 %copy-start.6 = (f32[18]{0:T(128)S(1)}, f32[18]{0:T(128)}, u32[]{:S(2)}) copy-start(f32[18]{0:T(128)} %param.15) | copy-start | bytes 220
  62.9 33.3 %copy-start.1 = (bf16[1024,18]{0,1:T(8,128)(2,1)S(1)}, bf16[1024,18]{0,1:T(8,128)(2,1)}, u32[]{:S(2)}) copy-start(bf16[1024,18]{0,1:T(8,128)(2,1)} %param.14) | copy-start | bytes 110596
  62.9 33.3 %all-to-all-start.2 = ((bf16[8,256,128]{2,1,0:T(8,128)(2,1)}), bf16[8,256,128]{2,1,0:T(8,128)(2,1)S(1)}, u32[]{:S(2)}, u32[]{:S(2)}) async-start(bf16[8,256,128]{2,1,0:T(8,128)(2,1)} %layer.1), calls=%async_computation.2 | async-start | bytes 1048576 | tf_op jit(solution)/shard_map/all_to_all | solution.py:361
  86.7 1.5 %collective-permute-start.10 = (bf16[8,32,512]{2,1,0:T(8,128)(2,1)S(1)}, bf16[8,32,512]{2,1,0:T(8,128)(2,1)S(1)}, u32[]{:S(2)}, u32[]{:S(2)}) collective-permute-start(bf16[8,32,512]{2,1,0:T(8,128)(2,1)S(1)} %copy-done.4), channel_id=1, source_target_pairs={{0,1},{1,0},{2,3},{3,2},{4,5},{5,4},{6,7},{7,6},{8,9},{9,8},{10,11... | collective-permute-start | bytes 786440 | tf_op jit(solution)/shard_map/ppermute | solution.py:340
  86.8 2.0 %collective-permute-start.11 = (bf16[8,32,512]{2,1,0:T(8,128)(2,1)}, bf16[8,32,512]{2,1,0:T(8,128)(2,1)S(1)}, u32[]{:S(2)}, u32[]{:S(2)}) collective-permute-start(bf16[8,32,512]{2,1,0:T(8,128)(2,1)} %collective-permute-done.refs_1_), channel_id=1, source_target_pairs={{0,1},{1,0},{2,3},{3,2},{4,5},{5,4},{6,7},{7,6},{8,9},{9,8},{10,11... | collective-permute-start | bytes 786440 | tf_op jit(solution)/shard_map/ppermute | solution.py:340
  87.3 2.0 %collective-permute-start.12 = (bf16[8,32,512]{2,1,0:T(8,128)(2,1)}, bf16[8,32,512]{2,1,0:T(8,128)(2,1)S(1)}, u32[]{:S(2)}, u32[]{:S(2)}) collective-permute-start(bf16[8,32,512]{2,1,0:T(8,128)(2,1)} %collective-permute-done.1.refs_2_), channel_id=1, source_target_pairs={{0,1},{1,0},{2,3},{3,2},{4,5},{5,4},{6,7},{7,6},{8,9},{9,8},{10,11... | collective-permute-start | bytes 786440 | tf_op jit(solution)/shard_map/ppermute | solution.py:340
  87.3 2.3 %collective-permute-start.13 = (bf16[8,32,512]{2,1,0:T(8,128)(2,1)}, bf16[8,32,512]{2,1,0:T(8,128)(2,1)S(1)}, u32[]{:S(2)}, u32[]{:S(2)}) collective-permute-start(bf16[8,32,512]{2,1,0:T(8,128)(2,1)} %collective-permute-done.2.refs_3_), channel_id=1, source_target_pairs={{0,1},{1,0},{2,3},{3,2},{4,5},{5,4},{6,7},{7,6},{8,9},{9,8},{10,11... | collective-permute-start | bytes 786440 | tf_op jit(solution)/shard_map/ppermute | solution.py:340
  115.8 3.2 %collective-permute-start.14 = (f32[18]{0:T(128)S(1)}, f32[18]{0:T(128)S(1)}, u32[]{:S(2)}, u32[]{:S(2)}) collective-permute-start(f32[18]{0:T(128)S(1)} %reduce_sum.9), channel_id=1, source_target_pairs={{0,1},{1,0},{2,3},{3,2},{4,5},{5,4},{6,7},{7,6},{8,9},{9,8},{10,11... | collective-permute-start | bytes 224 | tf_op jit(solution)/shard_map/ppermute | solution.py:340

commit v6 on v5

--- a/solution.py
+++ b/solution.py
@@ -82,6 +82,27 @@
         compiler_params=params(),
         name="pack",
     )(triple, final)
+
+
+def spread_kernel(both, shard, mixing):
+    for i in range(shard.shape[0]):
+        shard[i] = both[:, :, 0:384]
+    mixing[...] = both[:, :, 384:896]
+
+
+def spread(both, length):
+    lead = both.shape[:2]
+    return pl.pallas_call(
+        spread_kernel,
+        in_specs=[vmem()],
+        out_specs=[vmem()] * 2,
+        out_shape=[
+            jax.ShapeDtypeStruct((length, *lead, 384), BF16),
+            jax.ShapeDtypeStruct((*lead, 512), BF16),
+        ],
+        compiler_params=params(),
+        name="spread",
+    )(both)
 
 
 def layer_kernel(scales, gain, *refs):
@@ -346,9 +367,9 @@
     in_hbm = lambda x: pltpu.with_memory_space_constraint(x, pltpu.HBM)
     owned = pack(in_hbm(triple_projector), in_hbm(final_projector), lax.axis_size("dp_0"))
     owned = lax.all_to_all(owned, "dp_0", 0, 0, tiled=True)
-    shard, mixing = owned[:, :, :384], owned[:, :, 384:]
-    shard, mixing = lax.optimization_barrier((shard, mixing))
-    shard = copy_for_each(shard, "dp_1")
+    shard, mixing = spread(in_vmem(owned), lax.axis_size("dp_1"))
+    shard, mixing = in_hbm(shard), in_hbm(mixing)
+    shard = lax.all_to_all(shard, "dp_1", 0, 0, tiled=True)
     pieces = [x for own in near for x in (own, from_other_core(own))]
     mixing, _ = lax.optimization_barrier((mixing, shard))
     mixings = [mixing] + [from_step(mixing, k, "dp_1") for k in (2, 1, 3)]

time: 121 us -> 121 us (level)
  transfers between devices with their start and end apart: 18 -> 18, of which waited for: 8 -> 8; matrix products, arithmetic and copies ran while one was open for 2% -> 0% of each run, Pallas kernels for 12% -> 13%
where the time goes in v6:
time: 121 us
  starting transfers between devices  56.4 us (47%)
  waiting for transfers between devices  23.8 us (20%)
  Pallas kernels  20.1 us (17%)
  blocking collectives  17.7 us (15%)
  local copies, waits for them, and re-layouts  1.47 us (1%)
    all_to_all x1, starting transfers between devices, on_device(): attended = lax.all_to_all(attended, SEQ, 0, 0, tiled=True)  23.9 us
    all_to_all x1, blocking collectives, copy_for_each(): lax.all_to_all(jnp.broadcast_to(x[None], (length, *x.shape)), axis, 0, 0,...  17.7 us
    pallas_call x1, Pallas kernels, layer(): pl.pallas_call(layer_kernel, in_specs=[smem()] + [vmem()] * 10, out_specs...  15 us
    ppermute x9, starting transfers between devices, from_other_core(): return lax.ppermute(x, 'seq_1', [(0, 1), (1, 0)])  12.2 us
    all_to_all x1, waiting for transfers between devices, on_device(): owned = lax.all_to_all(owned, 'dp_0', 0, 0, tiled=True)  11.9 us
    all_to_all x1, starting transfers between devices, on_device(): owned = lax.all_to_all(owned, 'dp_0', 0, 0, tiled=True)  9.03 us
    ppermute x6, starting transfers between devices, from_step(): return lax.ppermute(x, axis, [(i, (i - k) % length) for i in range(length)])  7.14 us
    all_to_all x1, waiting for transfers between devices, on_device(): attended = lax.all_to_all(attended, SEQ, 0, 0, tiled=True)  6.61 us
  transfers between devices with their start and end apart: 18, of which 8 were waited for; matrix products, arithmetic and copies ran while one was open for 0% of the time, Pallas kernels for 13%

profile of v6, /device:TPU:1, one launch (start us, length us, event | category | flops | bytes accessed | tf_op | source)
XLA Modules:
  0.0 121.1 jit_solution(13431727065324533781)
XLA Ops:
  0.6 0.0 copy-start.6
  0.6 0.0 copy-start
  0.7 1.7 %pack.1 = bf16[8,32,896]{2,1,0:T(8,128)(2,1)} custom-call(bf16[32,3072]{1,0:T(8,128)(2,1)} %triple.1, bf16[32,1024]{1,0:T(8,128)(2,1)} %final.1), custom_call_target="tpu_custom_call" | custom-call | tf_op jit(solution)/shard_map/pack/pallas_call | solution.py:76
  2.4 9.0 %all-to-all-start = ((bf16[8,32,896]{2,1,0:T(8,128)(2,1)}), bf16[8,32,896]{2,1,0:T(8,128)(2,1)S(1)}, u32[]{:S(2)}, u32[]{:S(2)}) async-start(bf16[8,32,896]{2,1,0:T(8,128)(2,1)} %pack.1), calls=%async_computation | async-start | bytes 917504 | tf_op jit(solution)/shard_map/all_to_all | solution.py:369
  11.4 0.0 copy-done.6
  11.4 0.0 copy-done
  11.5 2.8 %collective-permute-start.4 = (bf16[272,1024]{1,0:T(8,128)(2,1)S(1)}, bf16[272,1024]{1,0:T(8,128)(2,1)S(1)}, u32[]{:S(2)}, u32[]{:S(2)}) collective-permute-start(bf16[272,1024]{1,0:T(8,128)(2,1)S(1)} %fusion.1.refs_0_), channel_id=1, source_target_pairs={{0,6},{2,0},{4,2},{6,4},{1,7},{3,1},{5,3},{7,5},{8,14},{10,8},{12,... | collective-permute-start | bytes 1671176 | tf_op jit(solution)/shard_map/ppermute | solution.py:358
  14.3 0.0 collective-permute-start.6
  14.3 1.6 %collective-permute-start.8 = (bf16[272,1024]{1,0:T(8,128)(2,1)S(1)}, bf16[272,1024]{1,0:T(8,128)(2,1)S(1)}, u32[]{:S(2)}, u32[]{:S(2)}) collective-permute-start(bf16[272,1024]{1,0:T(8,128)(2,1)S(1)} %fusion.1.refs_0_), channel_id=1, source_target_pairs={{0,4},{2,6},{4,0},{6,2},{1,5},{3,7},{5,1},{7,3},{8,12},{10,14},{12... | collective-permute-start | bytes 1671176 | tf_op jit(solution)/shard_map/ppermute | solution.py:358
  15.9 11.9 %all-to-all-done.both = bf16[8,32,896]{2,1,0:T(8,128)(2,1)S(1)} async-done(((bf16[8,32,896]{2,1,0:T(8,128)(2,1)}), bf16[8,32,896]{2,1,0:T(8,128)(2,1)S(1)}, u32[]{:S(2)}, u32[]{:S(2)}) %all-to-all-start) | async-done | bytes 458784 | tf_op jit(solution)/shard_map/all_to_all | solution.py:369
  27.9 1.0 spread.1
  28.8 0.0 copy-start.1
  28.8 0.7 copy-done.1
  29.5 0.0 copy-start.4
  29.5 0.0 copy-start.5
  29.5 4.1 %all-to-all-start.1 = ((bf16[4,8,32,384]{3,2,1,0:T(8,128)(2,1)}), bf16[4,8,32,384]{3,2,1,0:T(8,128)(2,1)S(1)}, u32[]{:S(2)}, u32[]{:S(2)}) async-start(bf16[4,8,32,384]{3,2,1,0:T(8,128)(2,1)} %get-tuple-element.15), calls=%async_computation.1 | async-start | bytes 1572864 | tf_op jit(solution)/shard_map/all_to_all | solution.py:372
  33.7 0.9 collective-permute-start.3
  34.5 0.0 collective-permute-done.4.refs_2_
  34.5 4.5 %collective-permute-start.5 = (bf16[272,1024]{1,0:T(8,128)(2,1)S(1)}, bf16[272,1024]{1,0:T(8,128)(2,1)}, u32[]{:S(2)}, u32[]{:S(2)}) collective-permute-start(bf16[272,1024]{1,0:T(8,128)(2,1)S(1)} %collective-permute-done.4.refs_2_), channel_id=1, source_target_pairs={{0,1},{1,0},{2,3},{3,2},{4,5},{5,4},{6,7},{7,6},{8,9},{9,8},{10,11... | collective-permute-start | bytes 1671176 | tf_op jit(solution)/shard_map/ppermute | solution.py:361
  39.1 0.0 collective-permute-done.6.refs_4_
  39.1 3.4 %collective-permute-start.7 = (bf16[272,1024]{1,0:T(8,128)(2,1)S(1)}, bf16[272,1024]{1,0:T(8,128)(2,1)}, u32[]{:S(2)}, u32[]{:S(2)}) collective-permute-start(bf16[272,1024]{1,0:T(8,128)(2,1)S(1)} %collective-permute-done.6.refs_4_), channel_id=1, source_target_pairs={{0,1},{1,0},{2,3},{3,2},{4,5},{5,4},{6,7},{7,6},{8,9},{9,8},{10,11... | collective-permute-start | bytes 1671176 | tf_op jit(solution)/shard_map/ppermute | solution.py:361
  42.5 0.0 collective-permute-done.8.refs_6_
  42.5 0.0 collective-permute-start.9
  42.5 2.7 %all-to-all-done.1.refs_8_ = bf16[4,8,32,384]{3,2,1,0:T(8,128)(2,1)S(1)} async-done(((bf16[4,8,32,384]{3,2,1,0:T(8,128)(2,1)}), bf16[4,8,32,384]{3,2,1,0:T(8,128)(2,1)S(1)}, u32[]{:S(2)}, u32[]{:S(2)}) %all-to-all-start.1) | async-done | bytes 786464 | tf_op jit(solution)/shard_map/all_to_all | solution.py:372
  45.1 0.4 collective-permute-start
  45.5 0.0 collective-permute-done.3.refs_1_
  45.5 2.3 %collective-permute-start.1 = (bf16[8,32,512]{2,1,0:T(8,128)(2,1)}, bf16[8,32,512]{2,1,0:T(8,128)(2,1)}, u32[]{:S(2)}, u32[]{:S(2)}) collective-permute-start(bf16[8,32,512]{2,1,0:T(8,128)(2,1)} %copy-done.1), channel_id=1, source_target_pairs={{0,24},{8,0},{16,8},{24,16},{1,25},{9,1},{17,9},{25,17},{2,26},{10... | collective-permute-start | bytes 786440 | tf_op jit(solution)/shard_map/ppermute | solution.py:358
  47.8 0.0 collective-permute-done.5.refs_3_
  47.8 0.0 collective-permute-start.2
  47.8 0.0 collective-permute-done.7.refs_5_
  47.8 0.0 collective-permute-done.9.refs_7_
  47.8 0.0 copy-done.4
  47.9 0.0 copy-done.5
  47.9 15.0 %layer.1 = bf16[8,256,128]{2,1,0:T(8,128)(2,1)} custom-call(f32[16]{0:T(128)S(1)} %copy-done.5, f32[1,1024]{1,0:T(1,128)S(1)} %bitcast.11, bf16[272,1024]{1,0:T(8,128)(2,1)S(1)} %fusion.1.refs_0_, bf16[272,1024]{1,0:T(8,128)(2,1)} %collective-permute-done.3.refs_1_, bf16[272,1024]{1,0:T(8,128)(2,1)S(1)} %collective-permute-done.4.refs_2_, ...), custom_call_target="tpu_custom_call" | custom-call | tf_op jit(solution)/shard_map/layer/pallas_call | solution.py:260
  62.8 0.0 copy-start.2
  62.8 0.0 copy-start.7
  62.8 0.0 copy-start.3
  62.9 0.0 collective-permute-done.refs_1_
  62.9 0.0 collective-permute-done.1.refs_2_
  62.9 0.0 collective-permute-done.2.refs_3_
  62.9 23.9 %all-to-all-start.2 = ((bf16[8,256,128]{2,1,0:T(8,128)(2,1)}), bf16[8,256,128]{2,1,0:T(8,128)(2,1)S(1)}, u32[]{:S(2)}, u32[]{:S(2)}) async-start(bf16[8,256,128]{2,1,0:T(8,128)(2,1)} %layer.1), calls=%async_computation.2 | async-start | bytes 1048576 | tf_op jit(solution)/shard_map/all_to_all | solution.py:382
  86.8 0.0 copy-done.2
  86.8 0.1 collective-permute-start.10
  86.9 0.4 collective-permute-start.11
  87.3 0.1 collective-permute-start.12
  87.4 0.4 collective-permute-start.13
  87.8 0.0 copy-done.7
  87.8 0.1 copy.18.refs_10_
  87.9 0.4 collective-permute-done.10.refs_4_
  88.4 0.6 collective-permute-done.11.refs_5_
  88.9 0.4 collective-permute-done.12.refs_6_
  89.3 0.4 collective-permute-done.13.refs_7_
  89.7 6.6 %all-to-all-done.2.pieces = bf16[8,256,128]{2,1,0:T(8,128)(2,1)S(1)} async-done(((bf16[8,256,128]{2,1,0:T(8,128)(2,1)}), bf16[8,256,128]{2,1,0:T(8,128)(2,1)S(1)}, u32[]{:S(2)}, u32[]{:S(2)}) %all-to-all-start.2) | async-done | bytes 524320 | tf_op jit(solution)/shard_map/all_to_all | solution.py:382
  96.3 0.0 copy-done.3
  96.3 2.5 %finish.1 = (bf16[256,1024]{1,0:T(8,128)(2,1)}, f32[18,256]{1,0:T(8,128)S(1)}, f32[1,18]{1,0:T(1,128)S(1)}) custom-call(bf16[8,256,128]{2,1,0:T(8,128)(2,1)S(1)} %all-to-all-done.2.pieces, bf16[8,32,512]{2,1,0:T(8,128)(2,1)} %copy-done.1, bf16[8,32,512]{2,1,0:T(8,128)(2,1)} %collective-permute-done.refs_1_, ...), custom_call_target="tpu_custom_call" | custom-call | tf_op jit(solution)/shard_map/finish/pallas_call | solution.py:323
  98.8 17.7 %all_to_all.20 = f32[128,1,18]{2,1,0:T(1,128)S(1)} all-to-all(f32[128,1,18]{2,1,0:T(1,128)S(1)} %broadcast_in_dim.25), channel_id=1, replica_groups=mesh['dp_0'=8,'dp_1'=4,'seq_0'=4,'seq_1'=2] {'dp_0','dp_1','seq_0'}, dimensions={0} | all-to-all | bytes 18432 | tf_op jit(solution)/shard_map/all_to_all | solution.py:44
  116.5 0.2 reduce_sum.9
  116.7 2.4 %collective-permute-start.14 = (f32[18]{0:T(128)S(1)}, f32[18]{0:T(128)S(1)}, u32[]{:S(2)}, u32[]{:S(2)}) collective-permute-start(f32[18]{0:T(128)S(1)} %reduce_sum.9), channel_id=1, source_target_pairs={{0,1},{1,0},{2,3},{3,2},{4,5},{5,4},{6,7},{7,6},{8,9},{9,8},{10,11... | collective-permute-start | bytes 224 | tf_op jit(solution)/shard_map/ppermute | solution.py:361
  119.0 0.8 collective-permute-done.14
  119.9 0.5 fusion.3
  120.4 0.1 subtract_bitcast_fusion
  120.5 0.6 copy.20
  (3 shorter events, 0.1 us)
Async XLA Ops:
  0.6 10.8 %copy-start.6 = (s32[1,256]{1,0:T(1,128)S(1)}, s32[1,256]{1,0:T(1,128)}, u32[]{:S(2)}) copy-start(s32[1,256]{1,0:T(1,128)} %param.9) | copy-start | bytes 3076
  0.6 10.8 %copy-start = (bf16[1,256,1024]{2,1,0:T(8,128)(2,1)S(1)}, bf16[1,256,1024]{2,1,0:T(8,128)(2,1)}, u32[]{:S(2)}) copy-start(bf16[1,256,1024]{2,1,0:T(8,128)(2,1)} %param.8) | copy-start | bytes 1572868
  2.4 25.5 %all-to-all-start = ((bf16[8,32,896]{2,1,0:T(8,128)(2,1)}), bf16[8,32,896]{2,1,0:T(8,128)(2,1)S(1)}, u32[]{:S(2)}, u32[]{:S(2)}) async-start(bf16[8,32,896]{2,1,0:T(8,128)(2,1)} %pack.1), calls=%async_computation | async-start | bytes 917504 | tf_op jit(solution)/shard_map/all_to_all | solution.py:369
  11.5 23.1 %collective-permute-start.4 = (bf16[272,1024]{1,0:T(8,128)(2,1)S(1)}, bf16[272,1024]{1,0:T(8,128)(2,1)S(1)}, u32[]{:S(2)}, u32[]{:S(2)}) collective-permute-start(bf16[272,1024]{1,0:T(8,128)(2,1)S(1)} %fusion.1.refs_0_), channel_id=1, source_target_pairs={{0,6},{2,0},{4,2},{6,4},{1,7},{3,1},{5,3},{7,5},{8,14},{10,8},{12,... | collective-permute-start | bytes 1671176 | tf_op jit(solution)/shard_map/ppermute | solution.py:358
  14.3 24.8 %collective-permute-start.6 = (bf16[272,1024]{1,0:T(8,128)(2,1)S(1)}, bf16[272,1024]{1,0:T(8,128)(2,1)S(1)}, u32[]{:S(2)}, u32[]{:S(2)}) collective-permute-start(bf16[272,1024]{1,0:T(8,128)(2,1)S(1)} %fusion.1.refs_0_), channel_id=1, source_target_pairs={{0,2},{2,4},{4,6},{6,0},{1,3},{3,5},{5,7},{7,1},{8,10},{10,12},{12... | collective-permute-start | bytes 1671176 | tf_op jit(solution)/shard_map/ppermute | solution.py:358
  14.3 28.2 %collective-permute-start.8 = (bf16[272,1024]{1,0:T(8,128)(2,1)S(1)}, bf16[272,1024]{1,0:T(8,128)(2,1)S(1)}, u32[]{:S(2)}, u32[]{:S(2)}) collective-permute-start(bf16[272,1024]{1,0:T(8,128)(2,1)S(1)} %fusion.1.refs_0_), channel_id=1, source_target_pairs={{0,4},{2,6},{4,0},{6,2},{1,5},{3,7},{5,1},{7,3},{8,12},{10,14},{12... | collective-permute-start | bytes 1671176 | tf_op jit(solution)/shard_map/ppermute | solution.py:358
  28.8 0.7 copy-start.1
  29.5 18.3 %copy-start.4 = (f32[1024]{0:T(1024)S(1)}, f32[1024]{0:T(1024)}, u32[]{:S(2)}) copy-start(f32[1024]{0:T(1024)} %param.10) | copy-start | bytes 12292
  29.5 18.3 %copy-start.5 = (f32[16]{0:T(128)S(1)}, f32[16]{0:T(128)}, u32[]{:S(2)}) copy-start(f32[16]{0:T(128)} %scales.1) | copy-start | bytes 196
  29.5 15.6 %all-to-all-start.1 = ((bf16[4,8,32,384]{3,2,1,0:T(8,128)(2,1)}), bf16[4,8,32,384]{3,2,1,0:T(8,128)(2,1)S(1)}, u32[]{:S(2)}, u32[]{:S(2)}) async-start(bf16[4,8,32,384]{3,2,1,0:T(8,128)(2,1)} %get-tuple-element.15), calls=%async_computation.1 | async-start | bytes 1572864 | tf_op jit(solution)/shard_map/all_to_all | solution.py:372
  33.7 11.8 %collective-permute-start.3 = (bf16[272,1024]{1,0:T(8,128)(2,1)S(1)}, bf16[272,1024]{1,0:T(8,128)(2,1)}, u32[]{:S(2)}, u32[]{:S(2)}) collective-permute-start(bf16[272,1024]{1,0:T(8,128)(2,1)S(1)} %fusion.1.refs_0_), channel_id=1, source_target_pairs={{0,1},{1,0},{2,3},{3,2},{4,5},{5,4},{6,7},{7,6},{8,9},{9,8},{10,11... | collective-permute-start | bytes 1671176 | tf_op jit(solution)/shard_map/ppermute | solution.py:361
  34.5 13.3 %collective-permute-start.5 = (bf16[272,1024]{1,0:T(8,128)(2,1)S(1)}, bf16[272,1024]{1,0:T(8,128)(2,1)}, u32[]{:S(2)}, u32[]{:S(2)}) collective-permute-start(bf16[272,1024]{1,0:T(8,128)(2,1)S(1)} %collective-permute-done.4.refs_2_), channel_id=1, source_target_pairs={{0,1},{1,0},{2,3},{3,2},{4,5},{5,4},{6,7},{7,6},{8,9},{9,8},{10,11... | collective-permute-start | bytes 1671176 | tf_op jit(solution)/shard_map/ppermute | solution.py:361
  39.1 8.8 %collective-permute-start.7 = (bf16[272,1024]{1,0:T(8,128)(2,1)S(1)}, bf16[272,1024]{1,0:T(8,128)(2,1)}, u32[]{:S(2)}, u32[]{:S(2)}) collective-permute-start(bf16[272,1024]{1,0:T(8,128)(2,1)S(1)} %collective-permute-done.6.refs_4_), channel_id=1, source_target_pairs={{0,1},{1,0},{2,3},{3,2},{4,5},{5,4},{6,7},{7,6},{8,9},{9,8},{10,11... | collective-permute-start | bytes 1671176 | tf_op jit(solution)/shard_map/ppermute | solution.py:361
  42.5 5.4 %collective-permute-start.9 = (bf16[272,1024]{1,0:T(8,128)(2,1)S(1)}, bf16[272,1024]{1,0:T(8,128)(2,1)}, u32[]{:S(2)}, u32[]{:S(2)}) collective-permute-start(bf16[272,1024]{1,0:T(8,128)(2,1)S(1)} %collective-permute-done.8.refs_6_), channel_id=1, source_target_pairs={{0,1},{1,0},{2,3},{3,2},{4,5},{5,4},{6,7},{7,6},{8,9},{9,8},{10,11... | collective-permute-start | bytes 1671176 | tf_op jit(solution)/shard_map/ppermute | solution.py:361
  45.1 17.7 %collective-permute-start = (bf16[8,32,512]{2,1,0:T(8,128)(2,1)}, bf16[8,32,512]{2,1,0:T(8,128)(2,1)}, u32[]{:S(2)}, u32[]{:S(2)}) collective-permute-start(bf16[8,32,512]{2,1,0:T(8,128)(2,1)} %copy-done.1), channel_id=1, source_target_pairs={{0,16},{8,24},{16,0},{24,8},{1,17},{9,25},{17,1},{25,9},{2,18},{10... | collective-permute-start | bytes 786440 | tf_op jit(solution)/shard_map/ppermute | solution.py:358
  45.5 17.4 %collective-permute-start.1 = (bf16[8,32,512]{2,1,0:T(8,128)(2,1)}, bf16[8,32,512]{2,1,0:T(8,128)(2,1)}, u32[]{:S(2)}, u32[]{:S(2)}) collective-permute-start(bf16[8,32,512]{2,1,0:T(8,128)(2,1)} %copy-done.1), channel_id=1, source_target_pairs={{0,24},{8,0},{16,8},{24,16},{1,25},{9,1},{17,9},{25,17},{2,26},{10... | collective-permute-start | bytes 786440 | tf_op jit(solution)/shard_map/ppermute | solution.py:358
  47.8 15.0 %collective-permute-start.2 = (bf16[8,32,512]{2,1,0:T(8,128)(2,1)}, bf16[8,32,512]{2,1,0:T(8,128)(2,1)}, u32[]{:S(2)}, u32[]{:S(2)}) collective-permute-start(bf16[8,32,512]{2,1,0:T(8,128)(2,1)} %copy-done.1), channel_id=1, source_target_pairs={{0,8},{8,16},{16,24},{24,0},{1,9},{9,17},{17,25},{25,1},{2,10},{10... | collective-permute-start | bytes 786440 | tf_op jit(solution)/shard_map/ppermute | solution.py:358
  62.8 24.0 %copy-start.2 = (bf16[8,32,512]{2,1,0:T(8,128)(2,1)S(1)}, bf16[8,32,512]{2,1,0:T(8,128)(2,1)}, u32[]{:S(2)}) copy-start(bf16[8,32,512]{2,1,0:T(8,128)(2,1)} %copy-done.1) | copy-start | bytes 786436
  62.8 25.0 %copy-start.7 = (f32[18]{0:T(128)S(1)}, f32[18]{0:T(128)}, u32[]{:S(2)}) copy-start(f32[18]{0:T(128)} %param.15) | copy-start | bytes 220
  62.8 33.5 %copy-start.3 = (bf16[1024,18]{0,1:T(8,128)(2,1)S(1)}, bf16[1024,18]{0,1:T(8,128)(2,1)}, u32[]{:S(2)}) copy-start(bf16[1024,18]{0,1:T(8,128)(2,1)} %param.14) | copy-start | bytes 110596
  62.9 33.4 %all-to-all-start.2 = ((bf16[8,256,128]{2,1,0:T(8,128)(2,1)}), bf16[8,256,128]{2,1,0:T(8,128)(2,1)S(1)}, u32[]{:S(2)}, u32[]{:S(2)}) async-start(bf16[8,256,128]{2,1,0:T(8,128)(2,1)} %layer.1), calls=%async_computation.2 | async-start | bytes 1048576 | tf_op jit(solution)/shard_map/all_to_all | solution.py:382
  86.8 1.5 %collective-permute-start.10 = (bf16[8,32,512]{2,1,0:T(8,128)(2,1)S(1)}, bf16[8,32,512]{2,1,0:T(8,128)(2,1)S(1)}, u32[]{:S(2)}, u32[]{:S(2)}) collective-permute-start(bf16[8,32,512]{2,1,0:T(8,128)(2,1)S(1)} %copy-done.2), channel_id=1, source_target_pairs={{0,1},{1,0},{2,3},{3,2},{4,5},{5,4},{6,7},{7,6},{8,9},{9,8},{10,11... | collective-permute-start | bytes 786440 | tf_op jit(solution)/shard_map/ppermute | solution.py:361
  86.9 2.0 %collective-permute-start.11 = (bf16[8,32,512]{2,1,0:T(8,128)(2,1)}, bf16[8,32,512]{2,1,0:T(8,128)(2,1)S(1)}, u32[]{:S(2)}, u32[]{:S(2)}) collective-permute-start(bf16[8,32,512]{2,1,0:T(8,128)(2,1)} %collective-permute-done.refs_1_), channel_id=1, source_target_pairs={{0,1},{1,0},{2,3},{3,2},{4,5},{5,4},{6,7},{7,6},{8,9},{9,8},{10,11... | collective-permute-start | bytes 786440 | tf_op jit(solution)/shard_map/ppermute | solution.py:361
  87.3 2.0 %collective-permute-start.12 = (bf16[8,32,512]{2,1,0:T(8,128)(2,1)}, bf16[8,32,512]{2,1,0:T(8,128)(2,1)S(1)}, u32[]{:S(2)}, u32[]{:S(2)}) collective-permute-start(bf16[8,32,512]{2,1,0:T(8,128)(2,1)} %collective-permute-done.1.refs_2_), channel_id=1, source_target_pairs={{0,1},{1,0},{2,3},{3,2},{4,5},{5,4},{6,7},{7,6},{8,9},{9,8},{10,11... | collective-permute-start | bytes 786440 | tf_op jit(solution)/shard_map/ppermute | solution.py:361
  87.4 2.3 %collective-permute-start.13 = (bf16[8,32,512]{2,1,0:T(8,128)(2,1)}, bf16[8,32,512]{2,1,0:T(8,128)(2,1)S(1)}, u32[]{:S(2)}, u32[]{:S(2)}) collective-permute-start(bf16[8,32,512]{2,1,0:T(8,128)(2,1)} %collective-permute-done.2.refs_3_), channel_id=1, source_target_pairs={{0,1},{1,0},{2,3},{3,2},{4,5},{5,4},{6,7},{7,6},{8,9},{9,8},{10,11... | collective-permute-start | bytes 786440 | tf_op jit(solution)/shard_map/ppermute | solution.py:361
  116.7 3.2 %collective-permute-start.14 = (f32[18]{0:T(128)S(1)}, f32[18]{0:T(128)S(1)}, u32[]{:S(2)}, u32[]{:S(2)}) collective-permute-start(f32[18]{0:T(128)S(1)} %reduce_sum.9), channel_id=1, source_target_pairs={{0,1},{1,0},{2,3},{3,2},{4,5},{5,4},{6,7},{7,6},{8,9},{9,8},{10,11... | collective-permute-start | bytes 224 | tf_op jit(solution)/shard_map/ppermute | solution.py:361

commit v7 on v6

--- a/solution.py
+++ b/solution.py
@@ -119,7 +119,7 @@
     lane = lax.broadcasted_iota(jnp.int32, (rows, 128), 1)
     spot = lax.broadcasted_iota(jnp.int32, (head, rows), 0)
     for pair in range(4):
-        step = (0, 1, 3, 2)[pair]
+        step = (0, 2, 1, 3)[pair]
         for side in range(2):
             wide = pieces[2 * pair + side][0:rows].astype(F32)
             inv = lax.rsqrt(jnp.mean(wide * wide, axis=-1, keepdims=True) + EPS)
@@ -362,7 +362,7 @@
 
     marked = jnp.pad(picture_label_tile.astype(BF16), ((0, 15), (0, width - count)))
     load = jnp.concatenate([rows, marked], axis=0)
-    near = [load] + [from_step(load, k) for k in (1, 3, 2)]
+    near = [load] + [from_step(load, k) for k in (2, 1, 3)]
 
     in_hbm = lambda x: pltpu.with_memory_space_constraint(x, pltpu.HBM)
     owned = pack(in_hbm(triple_projector), in_hbm(final_projector), lax.axis_size("dp_0"))

time: 121 us -> 122 us (level); the launches traced: 121 us -> 120 us
  starting transfers between devices: 56.4 us -> 33.2 us
  Pallas kernels: 20.1 us -> 37.2 us
  waiting for transfers between devices: 23.8 us -> 30.1 us
    pallas_call x1, Pallas kernels: 15 us -> 32 us  [layer(): pl.pallas_call(layer_kernel, in_specs=[smem()] + [vmem()] * 10, out_specs...]
    all_to_all x1, starting transfers between devices: 23.9 us -> 6.94 us  [on_device(): attended = lax.all_to_all(attended, SEQ, 0, 0, tiled=True)]
    ppermute x9, starting transfers between devices: 12.2 us -> 5.93 us  [from_other_core(): return lax.ppermute(x, 'seq_1', [(0, 1), (1, 0)])]
    ppermute x6, waiting for transfers between devices: 0.02 us -> 4.25 us  [from_step(): return lax.ppermute(x, axis, [(i, (i - k) % length) for i in range(length)])]
    all_to_all x1, waiting for transfers between devices: 2.67 us -> 4.71 us  [on_device(): shard = lax.all_to_all(shard, 'dp_1', 0, 0, tiled=True)]
  transfers between devices with their start and end apart: 18 -> 18, of which waited for: 8 -> 9; matrix products, arithmetic and copies ran while one was open for 0% -> 0% of each run, Pallas kernels for 13% -> 27%
where the time goes in v7:
time: 122 us; the launch traced here: 120 us
  Pallas kernels  37.2 us (30%)
  starting transfers between devices  33.2 us (27%)
  waiting for transfers between devices  30.1 us (25%)
  blocking collectives  16.9 us (14%)
  local copies, waits for them, and re-layouts  1.47 us (1%)
    pallas_call x1, Pallas kernels, layer(): pl.pallas_call(layer_kernel, in_specs=[smem()] + [vmem()] * 10, out_specs...  32 us
    all_to_all x1, blocking collectives, copy_for_each(): lax.all_to_all(jnp.broadcast_to(x[None], (length, *x.shape)), axis, 0, 0,...  16.9 us
    all_to_all x1, waiting for transfers between devices, on_device(): owned = lax.all_to_all(owned, 'dp_0', 0, 0, tiled=True)  11.9 us
    all_to_all x1, starting transfers between devices, on_device(): owned = lax.all_to_all(owned, 'dp_0', 0, 0, tiled=True)  9.03 us
    ppermute x6, starting transfers between devices, from_step(): return lax.ppermute(x, axis, [(i, (i - k) % length) for i in range(length)])  7.15 us
    all_to_all x1, starting transfers between devices, on_device(): attended = lax.all_to_all(attended, SEQ, 0, 0, tiled=True)  6.94 us
    all_to_all x1, waiting for transfers between devices, on_device(): attended = lax.all_to_all(attended, SEQ, 0, 0, tiled=True)  6.61 us
    ppermute x9, starting transfers between devices, from_other_core(): return lax.ppermute(x, 'seq_1', [(0, 1), (1, 0)])  5.93 us
  transfers between devices with their start and end apart: 18, of which 9 were waited for; matrix products, arithmetic and copies ran while one was open for 0% of the time, Pallas kernels for 27%

profile of v7, /device:TPU:1, one launch (start us, length us, event | category | flops | bytes accessed | tf_op | source)
XLA Modules:
  0.0 120.4 jit_solution(6545573885493877383)
XLA Ops:
  0.6 0.0 copy-start.6
  0.6 0.0 copy-start
  0.7 1.7 %pack.1 = bf16[8,32,896]{2,1,0:T(8,128)(2,1)} custom-call(bf16[32,3072]{1,0:T(8,128)(2,1)} %triple.1, bf16[32,1024]{1,0:T(8,128)(2,1)} %final.1), custom_call_target="tpu_custom_call" | custom-call | tf_op jit(solution)/shard_map/pack/pallas_call | solution.py:76
  2.4 9.0 %all-to-all-start = ((bf16[8,32,896]{2,1,0:T(8,128)(2,1)}), bf16[8,32,896]{2,1,0:T(8,128)(2,1)S(1)}, u32[]{:S(2)}, u32[]{:S(2)}) async-start(bf16[8,32,896]{2,1,0:T(8,128)(2,1)} %pack.1), calls=%async_computation | async-start | bytes 917504 | tf_op jit(solution)/shard_map/all_to_all | solution.py:369
  11.4 0.0 copy-done.6
  11.4 0.0 copy-done
  11.5 3.0 %collective-permute-start.4 = (bf16[272,1024]{1,0:T(8,128)(2,1)S(1)}, bf16[272,1024]{1,0:T(8,128)(2,1)S(1)}, u32[]{:S(2)}, u32[]{:S(2)}) collective-permute-start(bf16[272,1024]{1,0:T(8,128)(2,1)S(1)} %fusion.1.refs_0_), channel_id=1, source_target_pairs={{0,4},{2,6},{4,0},{6,2},{1,5},{3,7},{5,1},{7,3},{8,12},{10,14},{12... | collective-permute-start | bytes 1671176 | tf_op jit(solution)/shard_map/ppermute | solution.py:358
  14.5 0.8 collective-permute-start.6
  15.2 0.7 collective-permute-start.8
  15.9 11.9 %all-to-all-done.both = bf16[8,32,896]{2,1,0:T(8,128)(2,1)S(1)} async-done(((bf16[8,32,896]{2,1,0:T(8,128)(2,1)}), bf16[8,32,896]{2,1,0:T(8,128)(2,1)S(1)}, u32[]{:S(2)}, u32[]{:S(2)}) %all-to-all-start) | async-done | bytes 458784 | tf_op jit(solution)/shard_map/all_to_all | solution.py:369
  27.9 1.0 spread.1
  28.8 0.0 copy-start.1
  28.8 0.7 copy-done.1
  29.5 0.0 copy-start.4
  29.5 0.0 copy-start.5
  29.5 4.1 %all-to-all-start.1 = ((bf16[4,8,32,384]{3,2,1,0:T(8,128)(2,1)}), bf16[4,8,32,384]{3,2,1,0:T(8,128)(2,1)S(1)}, u32[]{:S(2)}, u32[]{:S(2)}) async-start(bf16[4,8,32,384]{3,2,1,0:T(8,128)(2,1)} %get-tuple-element.15), calls=%async_computation.1 | async-start | bytes 1572864 | tf_op jit(solution)/shard_map/all_to_all | solution.py:372
  33.7 0.9 collective-permute-start.3
  34.5 0.0 collective-permute-done.4.refs_2_
  34.5 0.1 collective-permute-start.5
  34.6 4.2 %collective-permute-done.6.refs_4_ = bf16[272,1024]{1,0:T(8,128)(2,1)S(1)} collective-permute-done((bf16[272,1024]{1,0:T(8,128)(2,1)S(1)}, bf16[272,1024]{1,0:T(8,128)(2,1)S(1)}, u32[]{:S(2)}, u32[]{:S(2)}) %collective-permute-start.6) | collective-permute-done | bytes 557088 | tf_op jit(solution)/shard_map/ppermute | solution.py:358
  38.9 1.6 %collective-permute-start.7 = (bf16[272,1024]{1,0:T(8,128)(2,1)S(1)}, bf16[272,1024]{1,0:T(8,128)(2,1)}, u32[]{:S(2)}, u32[]{:S(2)}) collective-permute-start(bf16[272,1024]{1,0:T(8,128)(2,1)S(1)} %collective-permute-done.6.refs_4_), channel_id=1, source_target_pairs={{0,1},{1,0},{2,3},{3,2},{4,5},{5,4},{6,7},{7,6},{8,9},{9,8},{10,11... | collective-permute-start | bytes 1671176 | tf_op jit(solution)/shard_map/ppermute | solution.py:361
  40.4 0.0 collective-permute-done.8.refs_6_
  40.4 0.0 collective-permute-start.9
  40.4 4.7 %all-to-all-done.1.refs_8_ = bf16[4,8,32,384]{3,2,1,0:T(8,128)(2,1)S(1)} async-done(((bf16[4,8,32,384]{3,2,1,0:T(8,128)(2,1)}), bf16[4,8,32,384]{3,2,1,0:T(8,128)(2,1)S(1)}, u32[]{:S(2)}, u32[]{:S(2)}) %all-to-all-start.1) | async-done | bytes 786464 | tf_op jit(solution)/shard_map/all_to_all | solution.py:372
  45.1 0.4 collective-permute-start
  45.5 0.0 collective-permute-done.3.refs_1_
  45.5 2.3 %collective-permute-start.1 = (bf16[8,32,512]{2,1,0:T(8,128)(2,1)}, bf16[8,32,512]{2,1,0:T(8,128)(2,1)}, u32[]{:S(2)}, u32[]{:S(2)}) collective-permute-start(bf16[8,32,512]{2,1,0:T(8,128)(2,1)} %copy-done.1), channel_id=1, source_target_pairs={{0,24},{8,0},{16,8},{24,16},{1,25},{9,1},{17,9},{25,17},{2,26},{10... | collective-permute-start | bytes 786440 | tf_op jit(solution)/shard_map/ppermute | solution.py:358
  47.8 0.0 collective-permute-done.5.refs_3_
  47.8 0.0 collective-permute-start.2
  47.8 0.0 collective-permute-done.7.refs_5_
  47.8 0.0 collective-permute-done.9.refs_7_
  47.8 0.0 copy-done.4
  47.9 0.0 copy-done.5
  47.9 32.0 %layer.1 = bf16[8,256,128]{2,1,0:T(8,128)(2,1)} custom-call(f32[16]{0:T(128)S(1)} %copy-done.5, f32[1,1024]{1,0:T(1,128)S(1)} %bitcast.11, bf16[272,1024]{1,0:T(8,128)(2,1)S(1)} %fusion.1.refs_0_, bf16[272,1024]{1,0:T(8,128)(2,1)} %collective-permute-done.3.refs_1_, bf16[272,1024]{1,0:T(8,128)(2,1)S(1)} %collective-permute-done.4.refs_2_, ...), custom_call_target="tpu_custom_call" | custom-call | tf_op jit(solution)/shard_map/layer/pallas_call | solution.py:260
  79.9 0.0 copy-start.2
  79.9 0.0 copy-start.7
  79.9 0.0 copy-start.3
  79.9 0.0 collective-permute-done.refs_1_
  79.9 0.0 collective-permute-done.1.refs_2_
  79.9 0.0 collective-permute-done.2.refs_3_
  79.9 6.9 %all-to-all-start.2 = ((bf16[8,256,128]{2,1,0:T(8,128)(2,1)}), bf16[8,256,128]{2,1,0:T(8,128)(2,1)S(1)}, u32[]{:S(2)}, u32[]{:S(2)}) async-start(bf16[8,256,128]{2,1,0:T(8,128)(2,1)} %layer.1), calls=%async_computation.2 | async-start | bytes 1048576 | tf_op jit(solution)/shard_map/all_to_all | solution.py:382
  86.9 0.0 copy-done.2
  86.9 0.1 collective-permute-start.10
  87.0 0.4 collective-permute-start.11
  87.4 0.1 collective-permute-start.12
  87.5 0.4 collective-permute-start.13
  87.9 0.0 copy-done.7
  87.9 0.1 copy.18.refs_10_
  88.0 0.4 collective-permute-done.10.refs_4_
  88.4 0.6 collective-permute-done.11.refs_5_
  89.0 0.4 collective-permute-done.12.refs_6_
  89.4 0.4 collective-permute-done.13.refs_7_
  89.8 6.6 %all-to-all-done.2.pieces = bf16[8,256,128]{2,1,0:T(8,128)(2,1)S(1)} async-done(((bf16[8,256,128]{2,1,0:T(8,128)(2,1)}), bf16[8,256,128]{2,1,0:T(8,128)(2,1)S(1)}, u32[]{:S(2)}, u32[]{:S(2)}) %all-to-all-start.2) | async-done | bytes 524320 | tf_op jit(solution)/shard_map/all_to_all | solution.py:382
  96.4 0.0 copy-done.3
  96.4 2.5 %finish.1 = (bf16[256,1024]{1,0:T(8,128)(2,1)}, f32[18,256]{1,0:T(8,128)S(1)}, f32[1,18]{1,0:T(1,128)S(1)}) custom-call(bf16[8,256,128]{2,1,0:T(8,128)(2,1)S(1)} %all-to-all-done.2.pieces, bf16[8,32,512]{2,1,0:T(8,128)(2,1)} %copy-done.1, bf16[8,32,512]{2,1,0:T(8,128)(2,1)} %collective-permute-done.refs_1_, ...), custom_call_target="tpu_custom_call" | custom-call | tf_op jit(solution)/shard_map/finish/pallas_call | solution.py:323
  98.9 16.9 %all_to_all.20 = f32[128,1,18]{2,1,0:T(1,128)S(1)} all-to-all(f32[128,1,18]{2,1,0:T(1,128)S(1)} %broadcast_in_dim.25), channel_id=1, replica_groups=mesh['dp_0'=8,'dp_1'=4,'seq_0'=4,'seq_1'=2] {'dp_0','dp_1','seq_0'}, dimensions={0} | all-to-all | bytes 18432 | tf_op jit(solution)/shard_map/all_to_all | solution.py:44
  115.8 0.2 reduce_sum.9
  116.0 2.4 %collective-permute-start.14 = (f32[18]{0:T(128)S(1)}, f32[18]{0:T(128)S(1)}, u32[]{:S(2)}, u32[]{:S(2)}) collective-permute-start(f32[18]{0:T(128)S(1)} %reduce_sum.9), channel_id=1, source_target_pairs={{0,1},{1,0},{2,3},{3,2},{4,5},{5,4},{6,7},{7,6},{8,9},{9,8},{10,11... | collective-permute-start | bytes 224 | tf_op jit(solution)/shard_map/ppermute | solution.py:361
  118.4 0.8 collective-permute-done.14
  119.2 0.5 fusion.3
  119.7 0.1 subtract_bitcast_fusion
  119.8 0.6 copy.20
  (3 shorter events, 0.1 us)
Async XLA Ops:
  0.6 10.8 %copy-start.6 = (s32[1,256]{1,0:T(1,128)S(1)}, s32[1,256]{1,0:T(1,128)}, u32[]{:S(2)}) copy-start(s32[1,256]{1,0:T(1,128)} %param.9) | copy-start | bytes 3076
  0.6 10.8 %copy-start = (bf16[1,256,1024]{2,1,0:T(8,128)(2,1)S(1)}, bf16[1,256,1024]{2,1,0:T(8,128)(2,1)}, u32[]{:S(2)}) copy-start(bf16[1,256,1024]{2,1,0:T(8,128)(2,1)} %param.8) | copy-start | bytes 1572868
  2.4 25.5 %all-to-all-start = ((bf16[8,32,896]{2,1,0:T(8,128)(2,1)}), bf16[8,32,896]{2,1,0:T(8,128)(2,1)S(1)}, u32[]{:S(2)}, u32[]{:S(2)}) async-start(bf16[8,32,896]{2,1,0:T(8,128)(2,1)} %pack.1), calls=%async_computation | async-start | bytes 917504 | tf_op jit(solution)/shard_map/all_to_all | solution.py:369
  11.5 23.1 %collective-permute-start.4 = (bf16[272,1024]{1,0:T(8,128)(2,1)S(1)}, bf16[272,1024]{1,0:T(8,128)(2,1)S(1)}, u32[]{:S(2)}, u32[]{:S(2)}) collective-permute-start(bf16[272,1024]{1,0:T(8,128)(2,1)S(1)} %fusion.1.refs_0_), channel_id=1, source_target_pairs={{0,4},{2,6},{4,0},{6,2},{1,5},{3,7},{5,1},{7,3},{8,12},{10,14},{12... | collective-permute-start | bytes 1671176 | tf_op jit(solution)/shard_map/ppermute | solution.py:358
  14.5 24.4 %collective-permute-start.6 = (bf16[272,1024]{1,0:T(8,128)(2,1)S(1)}, bf16[272,1024]{1,0:T(8,128)(2,1)S(1)}, u32[]{:S(2)}, u32[]{:S(2)}) collective-permute-start(bf16[272,1024]{1,0:T(8,128)(2,1)S(1)} %fusion.1.refs_0_), channel_id=1, source_target_pairs={{0,6},{2,0},{4,2},{6,4},{1,7},{3,1},{5,3},{7,5},{8,14},{10,8},{12,... | collective-permute-start | bytes 1671176 | tf_op jit(solution)/shard_map/ppermute | solution.py:358
  15.2 25.2 %collective-permute-start.8 = (bf16[272,1024]{1,0:T(8,128)(2,1)S(1)}, bf16[272,1024]{1,0:T(8,128)(2,1)S(1)}, u32[]{:S(2)}, u32[]{:S(2)}) collective-permute-start(bf16[272,1024]{1,0:T(8,128)(2,1)S(1)} %fusion.1.refs_0_), channel_id=1, source_target_pairs={{0,2},{2,4},{4,6},{6,0},{1,3},{3,5},{5,7},{7,1},{8,10},{10,12},{12... | collective-permute-start | bytes 1671176 | tf_op jit(solution)/shard_map/ppermute | solution.py:358
  28.8 0.7 copy-start.1
  29.5 18.3 %copy-start.4 = (f32[1024]{0:T(1024)S(1)}, f32[1024]{0:T(1024)}, u32[]{:S(2)}) copy-start(f32[1024]{0:T(1024)} %param.10) | copy-start | bytes 12292
  29.5 18.3 %copy-start.5 = (f32[16]{0:T(128)S(1)}, f32[16]{0:T(128)}, u32[]{:S(2)}) copy-start(f32[16]{0:T(128)} %scales.1) | copy-start | bytes 196
  29.5 15.6 %all-to-all-start.1 = ((bf16[4,8,32,384]{3,2,1,0:T(8,128)(2,1)}), bf16[4,8,32,384]{3,2,1,0:T(8,128)(2,1)S(1)}, u32[]{:S(2)}, u32[]{:S(2)}) async-start(bf16[4,8,32,384]{3,2,1,0:T(8,128)(2,1)} %get-tuple-element.15), calls=%async_computation.1 | async-start | bytes 1572864 | tf_op jit(solution)/shard_map/all_to_all | solution.py:372
  33.7 11.8 %collective-permute-start.3 = (bf16[272,1024]{1,0:T(8,128)(2,1)S(1)}, bf16[272,1024]{1,0:T(8,128)(2,1)}, u32[]{:S(2)}, u32[]{:S(2)}) collective-permute-start(bf16[272,1024]{1,0:T(8,128)(2,1)S(1)} %fusion.1.refs_0_), channel_id=1, source_target_pairs={{0,1},{1,0},{2,3},{3,2},{4,5},{5,4},{6,7},{7,6},{8,9},{9,8},{10,11... | collective-permute-start | bytes 1671176 | tf_op jit(solution)/shard_map/ppermute | solution.py:361
  34.5 13.3 %collective-permute-start.5 = (bf16[272,1024]{1,0:T(8,128)(2,1)S(1)}, bf16[272,1024]{1,0:T(8,128)(2,1)}, u32[]{:S(2)}, u32[]{:S(2)}) collective-permute-start(bf16[272,1024]{1,0:T(8,128)(2,1)S(1)} %collective-permute-done.4.refs_2_), channel_id=1, source_target_pairs={{0,1},{1,0},{2,3},{3,2},{4,5},{5,4},{6,7},{7,6},{8,9},{9,8},{10,11... | collective-permute-start | bytes 1671176 | tf_op jit(solution)/shard_map/ppermute | solution.py:361
  38.9 9.0 %collective-permute-start.7 = (bf16[272,1024]{1,0:T(8,128)(2,1)S(1)}, bf16[272,1024]{1,0:T(8,128)(2,1)}, u32[]{:S(2)}, u32[]{:S(2)}) collective-permute-start(bf16[272,1024]{1,0:T(8,128)(2,1)S(1)} %collective-permute-done.6.refs_4_), channel_id=1, source_target_pairs={{0,1},{1,0},{2,3},{3,2},{4,5},{5,4},{6,7},{7,6},{8,9},{9,8},{10,11... | collective-permute-start | bytes 1671176 | tf_op jit(solution)/shard_map/ppermute | solution.py:361
  40.4 7.4 %collective-permute-start.9 = (bf16[272,1024]{1,0:T(8,128)(2,1)S(1)}, bf16[272,1024]{1,0:T(8,128)(2,1)}, u32[]{:S(2)}, u32[]{:S(2)}) collective-permute-start(bf16[272,1024]{1,0:T(8,128)(2,1)S(1)} %collective-permute-done.8.refs_6_), channel_id=1, source_target_pairs={{0,1},{1,0},{2,3},{3,2},{4,5},{5,4},{6,7},{7,6},{8,9},{9,8},{10,11... | collective-permute-start | bytes 1671176 | tf_op jit(solution)/shard_map/ppermute | solution.py:361
  45.1 34.8 %collective-permute-start = (bf16[8,32,512]{2,1,0:T(8,128)(2,1)}, bf16[8,32,512]{2,1,0:T(8,128)(2,1)}, u32[]{:S(2)}, u32[]{:S(2)}) collective-permute-start(bf16[8,32,512]{2,1,0:T(8,128)(2,1)} %copy-done.1), channel_id=1, source_target_pairs={{0,16},{8,24},{16,0},{24,8},{1,17},{9,25},{17,1},{25,9},{2,18},{10... | collective-permute-start | bytes 786440 | tf_op jit(solution)/shard_map/ppermute | solution.py:358
  45.5 34.4 %collective-permute-start.1 = (bf16[8,32,512]{2,1,0:T(8,128)(2,1)}, bf16[8,32,512]{2,1,0:T(8,128)(2,1)}, u32[]{:S(2)}, u32[]{:S(2)}) collective-permute-start(bf16[8,32,512]{2,1,0:T(8,128)(2,1)} %copy-done.1), channel_id=1, source_target_pairs={{0,24},{8,0},{16,8},{24,16},{1,25},{9,1},{17,9},{25,17},{2,26},{10... | collective-permute-start | bytes 786440 | tf_op jit(solution)/shard_map/ppermute | solution.py:358
  47.8 32.1 %collective-permute-start.2 = (bf16[8,32,512]{2,1,0:T(8,128)(2,1)}, bf16[8,32,512]{2,1,0:T(8,128)(2,1)}, u32[]{:S(2)}, u32[]{:S(2)}) collective-permute-start(bf16[8,32,512]{2,1,0:T(8,128)(2,1)} %copy-done.1), channel_id=1, source_target_pairs={{0,8},{8,16},{16,24},{24,0},{1,9},{9,17},{17,25},{25,1},{2,10},{10... | collective-permute-start | bytes 786440 | tf_op jit(solution)/shard_map/ppermute | solution.py:358
  79.9 7.0 %copy-start.2 = (bf16[8,32,512]{2,1,0:T(8,128)(2,1)S(1)}, bf16[8,32,512]{2,1,0:T(8,128)(2,1)}, u32[]{:S(2)}) copy-start(bf16[8,32,512]{2,1,0:T(8,128)(2,1)} %copy-done.1) | copy-start | bytes 786436
  79.9 8.0 %copy-start.7 = (f32[18]{0:T(128)S(1)}, f32[18]{0:T(128)}, u32[]{:S(2)}) copy-start(f32[18]{0:T(128)} %param.15) | copy-start | bytes 220
  79.9 16.5 %copy-start.3 = (bf16[1024,18]{0,1:T(8,128)(2,1)S(1)}, bf16[1024,18]{0,1:T(8,128)(2,1)}, u32[]{:S(2)}) copy-start(bf16[1024,18]{0,1:T(8,128)(2,1)} %param.14) | copy-start | bytes 110596
  79.9 16.4 %all-to-all-start.2 = ((bf16[8,256,128]{2,1,0:T(8,128)(2,1)}), bf16[8,256,128]{2,1,0:T(8,128)(2,1)S(1)}, u32[]{:S(2)}, u32[]{:S(2)}) async-start(bf16[8,256,128]{2,1,0:T(8,128)(2,1)} %layer.1), calls=%async_computation.2 | async-start | bytes 1048576 | tf_op jit(solution)/shard_map/all_to_all | solution.py:382
  86.9 1.5 %collective-permute-start.10 = (bf16[8,32,512]{2,1,0:T(8,128)(2,1)S(1)}, bf16[8,32,512]{2,1,0:T(8,128)(2,1)S(1)}, u32[]{:S(2)}, u32[]{:S(2)}) collective-permute-start(bf16[8,32,512]{2,1,0:T(8,128)(2,1)S(1)} %copy-done.2), channel_id=1, source_target_pairs={{0,1},{1,0},{2,3},{3,2},{4,5},{5,4},{6,7},{7,6},{8,9},{9,8},{10,11... | collective-permute-start | bytes 786440 | tf_op jit(solution)/shard_map/ppermute | solution.py:361
  87.0 2.0 %collective-permute-start.11 = (bf16[8,32,512]{2,1,0:T(8,128)(2,1)}, bf16[8,32,512]{2,1,0:T(8,128)(2,1)S(1)}, u32[]{:S(2)}, u32[]{:S(2)}) collective-permute-start(bf16[8,32,512]{2,1,0:T(8,128)(2,1)} %collective-permute-done.refs_1_), channel_id=1, source_target_pairs={{0,1},{1,0},{2,3},{3,2},{4,5},{5,4},{6,7},{7,6},{8,9},{9,8},{10,11... | collective-permute-start | bytes 786440 | tf_op jit(solution)/shard_map/ppermute | solution.py:361
  87.4 2.0 %collective-permute-start.12 = (bf16[8,32,512]{2,1,0:T(8,128)(2,1)}, bf16[8,32,512]{2,1,0:T(8,128)(2,1)S(1)}, u32[]{:S(2)}, u32[]{:S(2)}) collective-permute-start(bf16[8,32,512]{2,1,0:T(8,128)(2,1)} %collective-permute-done.1.refs_2_), channel_id=1, source_target_pairs={{0,1},{1,0},{2,3},{3,2},{4,5},{5,4},{6,7},{7,6},{8,9},{9,8},{10,11... | collective-permute-start | bytes 786440 | tf_op jit(solution)/shard_map/ppermute | solution.py:361
  87.5 2.3 %collective-permute-start.13 = (bf16[8,32,512]{2,1,0:T(8,128)(2,1)}, bf16[8,32,512]{2,1,0:T(8,128)(2,1)S(1)}, u32[]{:S(2)}, u32[]{:S(2)}) collective-permute-start(bf16[8,32,512]{2,1,0:T(8,128)(2,1)} %collective-permute-done.2.refs_3_), channel_id=1, source_target_pairs={{0,1},{1,0},{2,3},{3,2},{4,5},{5,4},{6,7},{7,6},{8,9},{9,8},{10,11... | collective-permute-start | bytes 786440 | tf_op jit(solution)/shard_map/ppermute | solution.py:361
  116.0 3.2 %collective-permute-start.14 = (f32[18]{0:T(128)S(1)}, f32[18]{0:T(128)S(1)}, u32[]{:S(2)}, u32[]{:S(2)}) collective-permute-start(f32[18]{0:T(128)S(1)} %reduce_sum.9), channel_id=1, source_target_pairs={{0,1},{1,0},{2,3},{3,2},{4,5},{5,4},{6,7},{7,6},{8,9},{9,8},{10,11... | collective-permute-start | bytes 224 | tf_op jit(solution)/shard_map/ppermute | solution.py:361
